TPU v7x, 256 devices: a whole 4x4x8 slice. The times are simulated.
256 devices in a mesh: xy: 64 (over z, y_hi, x), gz: 4 (over y_lo, core).
Axes of the slice: x: 4, y: 4 (y_hi: 2, y_lo: 2; y = y_hi * 2 + y_lo), z: 8, core: 2. Of those that a mesh axis runs over, the one named last changes fastest.
Arguments:
- gauge_links: float32 [4, 2, 3, 3, 6, 128, 1024], P(None, None, None, None, None, 'xy', 'gz'), may hold values from -2.4 to 2.4
- pattern: int32 [4, 4], replicated, may hold values from 0 to 1
- link_parity: int32 [4], replicated, may hold values from 0 to 1
- conv_weight: bfloat16 [81, 48, 64], replicated, may hold values from -0.09375 to 0.09375
- conv_bias: float32 [64], replicated, may hold values from -3 to 3
- head_weight: float32 [64, 4], replicated, may hold values from -0.75 to 0.75
- cotangent: float32 [4, 2, 128, 1024], P(None, None, 'xy', 'gz'), may hold values from -6 to 6
Outputs:
- coefficients: float32 [4, 2, 128, 1024], P(None, None, 'xy', 'gz')
- grad_conv_weight: float32 [81, 48, 64], replicated
- grad_conv_bias: float32 [64], replicated
- grad_head_weight: float32 [64, 4], replicated
All inputs are finite; a program needn't handle non-finite values.
Results may differ from a plain program's by a relative error of at most 0.0059.
Values may be sent and summed in bfloat16 or wider, within the bound.
No kernel may reach another device: no remote copies, remote signals or barrier semaphores. Data moves between devices by JAX's collectives and lax.ppermute only.
A program may use at most 128 MiB of HBM per device.

v0:
```python
import math

import jax
import jax.numpy as jnp
from jax import lax
from jax.sharding import PartitionSpec as P

LY = 64
ROWS = 1024


plane_pairs = ((0, 1), (0, 2), (0, 3), (1, 2), (1, 3), (2, 3))


def shifted(x, axis, by):
    count = lax.axis_size(axis)
    return lax.ppermute(x, axis, [(i, (i + by) % count) for i in range(count)])


def padded(x, sides, width):
    for axis, dim in sides:
        count, length = (lax.axis_size(axis), x.shape[dim])
        up = [(i, (i + 1) % count) for i in range(count)]
        down = [(j, i) for i, j in up]
        last = lax.slice_in_dim(x, length - width, length, axis=dim)
        leading = lax.slice_in_dim(x, 0, width, axis=dim)
        before = lax.ppermute(last, axis, up)
        after = lax.ppermute(leading, axis, down)
        x = jnp.concatenate([before, x, after], axis=dim)
    return x


def complex_product(left_side, right_side):
    real_part = jnp.sum(left_side[0][:, :, None] * right_side[0][None], axis=1) - jnp.sum(
        left_side[1][:, :, None] * right_side[1][None], axis=1
    )
    imag_part = jnp.sum(left_side[0][:, :, None] * right_side[1][None], axis=1) + jnp.sum(
        left_side[1][:, :, None] * right_side[0][None], axis=1
    )
    return jnp.stack([real_part, imag_part])


def plaquettes(extended):
    time_span = extended.shape[4] - 1
    width_x = extended.shape[5] - 1
    width_z = extended.shape[6] - 1

    def at_site(direction):
        return extended[direction, :, :, :, :time_span, :width_x, :width_z, :]

    def one_ahead(direction, step_dir):
        if step_dir == 0:
            return extended[direction, :, :, :, :time_span, 1:, :width_z, :]
        if step_dir == 1:
            return jnp.roll(at_site(direction), -1, axis=6)
        if step_dir == 2:
            return extended[direction, :, :, :, :time_span, :width_x, 1:, :]
        return extended[direction, :, :, :, 1:, :width_x, :width_z, :]

    wilson_loops = []
    for dir_one, dir_two in plane_pairs:
        first_pair = complex_product(at_site(dir_one), one_ahead(dir_two, dir_one))
        second = complex_product(at_site(dir_two), one_ahead(dir_one, dir_two))
        real_part = jnp.sum(first_pair[0] * second[0] + first_pair[1] * second[1], axis=(0, 1))
        imag_part = jnp.sum(first_pair[1] * second[0] - first_pair[0] * second[1], axis=(0, 1))
        wilson_loops.append(real_part)
        wilson_loops.append(imag_part)
    return jnp.stack(wilson_loops)


def clover(wilson_loops, start_x, start_z, count_x, count_z, time_slab):
    leaves = []
    for plane_num, pair in enumerate(plane_pairs):
        for leaf_set in ((), (pair[0],), (pair[1],), pair):
            shift_x = -1 if 0 in leaf_set else 0
            shift_z = -1 if 2 in leaf_set else 0
            shift_t = -1 if 3 in leaf_set else 0
            leaf_piece = wilson_loops[
                2 * plane_num : 2 * plane_num + 2,
                1 + shift_t : 1 + shift_t + time_slab + 2,
                start_x + shift_x : start_x + shift_x + count_x,
                start_z + shift_z : start_z + shift_z + count_z,
                :,
            ]
            if 1 in leaf_set:
                leaf_piece = jnp.roll(leaf_piece, 1, axis=4)
            leaves.append(leaf_piece)
    return jnp.concatenate(leaves).astype(jnp.bfloat16)


def stacked(feat_ext):
    return jnp.concatenate(
        [jnp.roll(feat_ext, 1, axis=4), feat_ext, jnp.roll(feat_ext, -1, axis=4)]
    )


def window(stacked_feats, offset, time_slab, count_x, count_z):
    step_x = offset // 9
    step_z = offset // 3 % 3
    step_t = offset % 3
    part_view = stacked_feats[
        :, step_t : step_t + time_slab, step_x : step_x + count_x, step_z : step_z + count_z, :
    ]
    return part_view.reshape(stacked_feats.shape[0], -1)


def convolve(stacked_feats, kernel, conv_bias, time_slab, count_x, count_z):
    running = None
    for offset in range(27):
        term = lax.dot_general(
            kernel[offset],
            window(stacked_feats, offset, time_slab, count_x, count_z),
            (((0,), (0,)), ((), ())),
            preferred_element_type=jnp.float32,
        )
        running = term if running is None else running + term
    return running + conv_bias[:, None]


def kernel_grad(stacked_feats, hidden_low, time_slab, count_x, count_z):
    parts_list = []
    for offset in range(27):
        parts_list.append(
            lax.dot_general(
                window(stacked_feats, offset, time_slab, count_x, count_z),
                hidden_low,
                (((1,), (1,)), ((), ())),
                preferred_element_type=jnp.float32,
            )
        )
    return jnp.stack(parts_list).reshape(81, 48, -1)


def link_mask(pattern, link_parity, time_pos, x_pos, z_pos, y_pos):
    summed = (
        pattern[:, 0][:, None, None, None, None] * x_pos[None, None, :, None, None]
        + pattern[:, 1][:, None, None, None, None] * y_pos[None, None, None, None, :]
        + pattern[:, 2][:, None, None, None, None] * z_pos[None, None, None, :, None]
        + pattern[:, 3][:, None, None, None, None] * time_pos[None, :, None, None, None]
        + link_parity[:, None, None, None, None]
    )
    return (summed % 2 == 0).astype(jnp.float32).reshape(4, -1)


def head_and_grads(hidden, active, head_weight, cotangent_rows):
    activation = jnp.tanh(hidden)
    coefficients = active * lax.dot_general(
        head_weight,
        activation,
        (((0,), (0,)), ((), ())),
        precision=lax.Precision.HIGHEST,
        preferred_element_type=jnp.float32,
    )
    grad_scale = 1.0 / math.sqrt(ROWS)
    coef_grad = active * cotangent_rows * grad_scale
    act_grad = jnp.dot(
        head_weight, coef_grad, precision=lax.Precision.HIGHEST, preferred_element_type=jnp.float32
    )
    hidden_grad = act_grad * (1.0 - activation * activation)
    grad_bias = jnp.sum(hidden_grad, axis=1)
    grad_head = lax.dot_general(
        activation,
        coef_grad,
        (((1,), (1,)), ((), ())),
        precision=lax.Precision.HIGHEST,
        preferred_element_type=jnp.float32,
    )
    return (coefficients, hidden_grad.astype(jnp.bfloat16), grad_bias, grad_head)


def per_device(gauge_links, pattern, link_parity, conv_weight, conv_bias, head_weight, cotangent):
    time_len = gauge_links.shape[4]
    count_x = gauge_links.shape[5]
    count_z = gauge_links.shape[6] // LY
    time_slab = time_len - 4
    lattice = gauge_links.reshape(4, 2, 3, 3, time_len, count_x, count_z, LY)
    next_x = shifted(lattice[:, :, :, :, :, 0:1], "xy", -1)
    wider_x = jnp.concatenate([lattice, next_x], axis=5)
    next_z = shifted(wider_x[:, :, :, :, :, :, 0:1], "gz", -1)
    extended = jnp.concatenate([wider_x, next_z], axis=6)
    wilson_loops = plaquettes(extended)
    loops_ext = padded(wilson_loops.astype(jnp.bfloat16), (("xy", 2), ("gz", 3)), 2).astype(
        wilson_loops.dtype
    )
    feat_ext = clover(loops_ext, 1, 1, count_x + 2, count_z + 2, time_slab)
    stacked_feats = stacked(feat_ext)
    kernel = conv_weight.reshape(27, 144, -1)
    hidden = convolve(stacked_feats, kernel, conv_bias, time_slab, count_x, count_z)
    x_pos = lax.axis_index("xy") * count_x + jnp.arange(count_x, dtype=jnp.int32)
    z_pos = lax.axis_index("gz") * count_z + jnp.arange(count_z, dtype=jnp.int32)
    active = link_mask(
        pattern,
        link_parity,
        jnp.arange(time_slab, dtype=jnp.int32),
        x_pos,
        z_pos,
        jnp.arange(LY, dtype=jnp.int32),
    )
    coefficients, hidden_low, grad_bias, grad_head = head_and_grads(
        hidden, active, head_weight, cotangent.reshape(4, -1)
    )
    grad_kernel = kernel_grad(stacked_feats, hidden_low, time_slab, count_x, count_z)
    grad_kernel, grad_bias, grad_head = lax.psum((grad_kernel, grad_bias, grad_head), ("xy", "gz"))
    return (
        coefficients.reshape(4, time_slab, count_x, count_z * LY),
        grad_kernel,
        grad_bias,
        grad_head,
    )


def solution(mesh):
    return jax.shard_map(
        per_device,
        mesh=mesh,
        in_specs=(
            P(None, None, None, None, None, "xy", "gz"),
            P(),
            P(),
            P(),
            P(),
            P(),
            P(None, None, "xy", "gz"),
        ),
        out_specs=(P(None, None, "xy", "gz"), P(), P(), P()),
        check_vma=False,
    )
```

profile of v0, /device:TPU:1, one launch (start us, length us, event | category | flops | bytes accessed | tf_op | source)
XLA Modules:
  0.0 493.0 jit_solution(4760283650788397721)
XLA Ops:
  7.2 2.5 reshape.387
  10.8 11.2 %collective-permute-start = (f32[4,2,3,3,6,1,4,64]{7,6,5,4,3,2,1,0:T(4,128)}, f32[4,2,3,3,6,1,4,64]{7,6,5,4,3,2,1,0:T(4,128)}, u32[]{:S(2)}, u32[]{:S(2)}) collective-permute-start(f32[4,2,3,3,6,1,4,64]{7,6,5,4,3,2,1,0:T(4,128)} %slice.806), channel_id=1, source_target_pairs={{0,252},{4,0},{8,4},{12,8},{16,12},{20,16},{24,20},{28,24},{32,28}... | collective-permute-start | bytes 1327112 | tf_op jit(solution)/shard_map/ppermute | solution.py:17
  26.4 7.4 %fusion.71 = (bf16[3,48,64]{0,2,1:T(8,128)(2,1)}, bf16[3,48,64]{0,2,1:T(8,128)(2,1)}, bf16[3,48,64]{0,2,1:T(8,128)(2,1)}, bf16[3,48,64]{0,2,1:T(8,128)(2,1)}, bf...) fusion(bf16[81,48,64]{0,2,1:T(8,128)(2,1)S(1)} %copy-done.1), kind=kLoop, calls=%fused_computation.322 | loop fusion | bytes 700416 | tf_op jit(solution)/shard_map/slice | solution.py:111
  34.8 4.3 fusion.72
  45.0 8.0 %collective-permute-done.1 = f32[4,2,3,3,6,3,1,64]{7,6,5,4,3,2,1,0:T(1,128)S(1)} collective-permute-done((f32[4,2,3,3,6,3,1,64]{7,6,5,4,3,2,1,0:T(1,128)S(1)}, f32[4,2,3,3,6,3,1,64]{7,6,5,4,3,2,1,0:T(1,128)S(1)}, u32[]{:S(2)}, u32[]{:S(2)}) %collective-permute-start.1) | collective-permute-done | bytes 331808 | tf_op jit(solution)/shard_map/ppermute | solution.py:17
  53.8 6.2 %multiply_reduce_fusion.14 = (f32[3,3,5,2,4,64]{5,4,3,2,1,0:T(4,128)S(1)}, f32[3,3,5,2,4,64]{5,4,3,2,1,0:T(4,128)S(1)}, f32[3,3,5,2,4,64]{5,4,3,2,1,0:T(4,128)S(...) fusion(f32[3,3,5,2,4,64]{5,4,3,2,1,0:T(4,128)S(1)} %get-tuple-e, ...), kind=kLoop, calls=%fused_computation.114 | loop fusion | flops 2764800 | bytes 3686400 | tf_op jit(solution)/shard_map/reduce_sum | solution.py:34
  60.3 6.2 %multiply_reduce_fusion.4 = (f32[3,3,5,2,4,64]{5,4,3,2,1,0:T(4,128)S(1)}, f32[3,3,5,2,4,64]{5,4,3,2,1,0:T(4,128)S(1)}, f32[3,3,5,2,4,64]{5,4,3,2,1,0:T(4,128)S(1...) fusion(f32[3,3,5,2,4,64]{5,4,3,2,1,0:T(4,128)S(1)} %get-tuple-e, ...), kind=kLoop, calls=%fused_computation.104 | loop fusion | flops 2764800 | bytes 3686400 | tf_op jit(solution)/shard_map/reduce_sum | solution.py:34
  68.0 8.6 %collective-permute-start.3 = (bf16[12,5,2,4,64]{4,3,2,1,0:T(4,128)(2,1)S(1)}, bf16[12,5,2,4,64]{4,3,2,1,0:T(4,128)(2,1)S(1)}, u32[]{:S(2)}, u32[]{:S(2)}) collective-permute-start(bf16[12,5,2,4,64]{4,3,2,1,0:T(4,128)(2,1)S(1)} %constant_dynamic-update-slice_fusion.2), channel_id=1, source_target_pairs={{4,0},{8,4},{12,8},{16,12},{20,16},{24,20},{28,24},{32,28},{36,32}... | collective-permute-start | bytes 184328 | tf_op jit(solution)/shard_map/ppermute | solution.py:28
  76.7 2.5 collective-permute-done.3
  79.2 8.0 %collective-permute-done.2 = bf16[12,5,2,4,64]{4,3,2,1,0:T(4,128)(2,1)S(1)} collective-permute-done((bf16[12,5,2,4,64]{4,3,2,1,0:T(4,128)(2,1)S(1)}, bf16[12,5,2,4,64]{4,3,2,1,0:T(4,128)(2,1)S(1)}, u32[]{:S(2)}, u32[]{:S(2)}) %collective-permute-start.2) | collective-permute-done | bytes 61472 | tf_op jit(solution)/shard_map/ppermute | solution.py:27
  114.5 2.2 copy.56
  137.6 3.0 fusion.68
  140.6 6.9 %fusion.67 = (bf16[144,2,2,4,64]{4,3,2,1,0:T(4,128)(2,1)}, bf16[144,2,2,4,64]{4,3,2,1,0:T(4,128)(2,1)S(1)}, bf16[144,2,2,4,64]{4,3,2,1,0:T(4,128)(2,1)}, bf16[14...) fusion(bf16[144,4,4,6,64]{4,3,2,1,0:T(8,128)(2,1)S(1)} %maximum, ...), kind=kLoop, calls=%fused_computation.318 | loop fusion | bytes 11206656 | tf_op jit(solution)/shard_map/slice | solution.py:101
  149.8 2.2 reshape.392
  152.0 2.2 reshape.391
  154.2 2.2 reshape.390
  156.4 2.2 reshape.389
  158.6 2.2 reshape.388
  160.8 2.2 reshape.414
  173.2 2.2 reshape.404
  175.5 2.2 reshape.403
  177.7 2.2 reshape.402
  179.9 2.2 reshape.401
  182.1 2.2 reshape.400
  184.3 2.2 reshape.399
  186.5 2.2 reshape.398
  188.8 2.2 reshape.397
  191.0 2.2 reshape.396
  226.5 3.0 copy.67
  231.7 72.7 %all-reduce = (f32[64]{0:T(128)}, f32[64,4]{0,1:T(4,128)}) all-reduce(f32[64]{0:T(128)S(1)} %get-tuple-element.195, f32[64,4]{0,1:T(4,128)S(1)} %fusion.55), channel_id=1, replica_groups=mesh['xy'=64,'gz'=4] {'xy','gz'}, use_global_device_ids=true, to_apply=%region_62.63 | all-reduce | flops 320 | bytes 2560 | tf_op jit(solution)/shard_map/psum | solution.py:203
  304.4 178.7 %all-reduce.3.cloned.1.call-done = f32[81,48,64]{2,1,0:T(8,128)} async-done(((f32[81,48,64]{2,1,0:T(8,128)}), f32[81,48,64]{2,1,0:T(8,128)}) %all-reduce.3.cloned.1.call-update) | async-done | bytes 995344 | tf_op jit(solution)/shard_map/psum | solution.py:203
  483.1 2.8 copy.68
  (344 shorter events, 109.7 us)
Async XLA Ops:
  7.2 196.1 %copy-start = (f32[64,4]{0,1:T(4,128)S(1)}, f32[64,4]{0,1:T(4,128)}, u32[]{:S(2)}) copy-start(f32[64,4]{0,1:T(4,128)} %param.12) | copy-start | bytes 3076
  7.2 475.9 %all-reduce.3.cloned.1.call-start = ((), (), s32[]{:S(2)}) async-start(), calls=%async_computation | async-start | bytes 3981312 | tf_op jit(solution)/shard_map/psum | solution.py:203
  10.8 29.9 %collective-permute-start = (f32[4,2,3,3,6,1,4,64]{7,6,5,4,3,2,1,0:T(4,128)}, f32[4,2,3,3,6,1,4,64]{7,6,5,4,3,2,1,0:T(4,128)}, u32[]{:S(2)}, u32[]{:S(2)}) collective-permute-start(f32[4,2,3,3,6,1,4,64]{7,6,5,4,3,2,1,0:T(4,128)} %slice.806), channel_id=1, source_target_pairs={{0,252},{4,0},{8,4},{12,8},{16,12},{20,16},{24,20},{28,24},{32,28}... | collective-permute-start | bytes 1327112 | tf_op jit(solution)/shard_map/ppermute | solution.py:17
  26.4 7.6 %copy-start.3 = (f32[2,3,3,5,2,4,64]{6,5,4,3,2,1,0:T(4,128)S(1)}, f32[2,3,3,5,2,4,64]{6,5,4,3,2,1,0:T(4,128)}, u32[]{:S(2)}) copy-start(f32[2,3,3,5,2,4,64]{6,5,4,3,2,1,0:T(4,128)} %get-tuple-element.143) | copy-start | bytes 552964
  34.8 5.9 %copy-start.2 = (f32[4,2,3,3,6,3,4,64]{7,6,5,4,3,2,1,0:T(4,128)S(1)}, f32[4,2,3,3,6,3,4,64]{7,6,5,4,3,2,1,0:T(4,128)}, u32[]{:S(2)}) copy-start(f32[4,2,3,3,6,3,4,64]{7,6,5,4,3,2,1,0:T(4,128)} %constant_dynamic-update-slice_fusion.1) | copy-start | bytes 3981316
  42.5 10.4 %collective-permute-start.1 = (f32[4,2,3,3,6,3,1,64]{7,6,5,4,3,2,1,0:T(1,128)S(1)}, f32[4,2,3,3,6,3,1,64]{7,6,5,4,3,2,1,0:T(1,128)S(1)}, u32[]{:S(2)}, u32[]{:S(2)}) collective-permute-start(f32[4,2,3,3,6,3,1,64]{7,6,5,4,3,2,1,0:T(1,128)S(1)} %slice.820), channel_id=1, source_target_pairs={{0,3},{1,0},{2,1},{3,2},{4,7},{5,4},{6,5},{7,6},{8,11},{9,8},{10,9... | collective-permute-start | bytes 995336 | tf_op jit(solution)/shard_map/ppermute | solution.py:17
  67.7 22.1 %copy-start.67 = (f32[4,2,2,256]{3,2,1,0:T(2,128)S(1)}, f32[4,2,2,256]{3,2,1,0:T(2,128)}, u32[]{:S(2)}) copy-start(f32[4,2,2,256]{3,2,1,0:T(2,128)} %param.13) | copy-start | bytes 49156
  67.7 22.7 %copy-start.9 = (bf16[3,48,64]{0,2,1:T(8,128)(2,1)S(1)}, bf16[3,48,64]{0,2,1:T(8,128)(2,1)}, u32[]{:S(2)}) copy-start(bf16[3,48,64]{0,2,1:T(8,128)(2,1)} %get-tuple-element.169) | copy-start | bytes 55300
  67.7 23.7 %copy-start.8 = (bf16[3,48,64]{0,2,1:T(8,128)(2,1)S(1)}, bf16[3,48,64]{0,2,1:T(8,128)(2,1)}, u32[]{:S(2)}) copy-start(bf16[3,48,64]{0,2,1:T(8,128)(2,1)} %get-tuple-element.170) | copy-start | bytes 55300
  68.0 24.4 %copy-start.7 = (bf16[3,48,64]{0,2,1:T(8,128)(2,1)S(1)}, bf16[3,48,64]{0,2,1:T(8,128)(2,1)}, u32[]{:S(2)}) copy-start(bf16[3,48,64]{0,2,1:T(8,128)(2,1)} %get-tuple-element.171) | copy-start | bytes 55300
  68.0 11.2 %collective-permute-start.3 = (bf16[12,5,2,4,64]{4,3,2,1,0:T(4,128)(2,1)S(1)}, bf16[12,5,2,4,64]{4,3,2,1,0:T(4,128)(2,1)S(1)}, u32[]{:S(2)}, u32[]{:S(2)}) collective-permute-start(bf16[12,5,2,4,64]{4,3,2,1,0:T(4,128)(2,1)S(1)} %constant_dynamic-update-slice_fusion.2), channel_id=1, source_target_pairs={{4,0},{8,4},{12,8},{16,12},{20,16},{24,20},{28,24},{32,28},{36,32}... | collective-permute-start | bytes 184328 | tf_op jit(solution)/shard_map/ppermute | solution.py:28
  76.6 10.6 %collective-permute-start.2 = (bf16[12,5,2,4,64]{4,3,2,1,0:T(4,128)(2,1)S(1)}, bf16[12,5,2,4,64]{4,3,2,1,0:T(4,128)(2,1)S(1)}, u32[]{:S(2)}, u32[]{:S(2)}) collective-permute-start(bf16[12,5,2,4,64]{4,3,2,1,0:T(4,128)(2,1)S(1)} %constant_dynamic-update-slice_fusion.2), channel_id=1, source_target_pairs={{0,4},{4,8},{8,12},{12,16},{16,20},{20,24},{24,28},{28,32},{32,36}... | collective-permute-start | bytes 184328 | tf_op jit(solution)/shard_map/ppermute | solution.py:27
  87.8 41.4 %collective-permute-start.4 = (bf16[12,5,6,2,64]{4,3,2,1,0:T(2,128)(2,1)S(1)}, bf16[12,5,6,2,64]{4,3,2,1,0:T(2,128)(2,1)S(1)}, u32[]{:S(2)}, u32[]{:S(2)}) collective-permute-start(bf16[12,5,6,2,64]{4,3,2,1,0:T(2,128)(2,1)S(1)} %get-tuple-element.193), channel_id=1, source_target_pairs={{0,1},{1,2},{2,3},{3,0},{4,5},{5,6},{6,7},{7,4},{8,9},{9,10},{10,1... | collective-permute-start | bytes 276488 | tf_op jit(solution)/shard_map/ppermute | solution.py:27
  88.6 40.6 %collective-permute-start.5 = (bf16[12,5,6,2,64]{4,3,2,1,0:T(2,128)(2,1)S(1)}, bf16[12,5,6,2,64]{4,3,2,1,0:T(2,128)(2,1)S(1)}, u32[]{:S(2)}, u32[]{:S(2)}) collective-permute-start(bf16[12,5,6,2,64]{4,3,2,1,0:T(2,128)(2,1)S(1)} %get-tuple-element.194), channel_id=1, source_target_pairs={{1,0},{2,1},{3,2},{0,3},{5,4},{6,5},{7,6},{4,7},{9,8},{10,9},{11,1... | collective-permute-start | bytes 276488 | tf_op jit(solution)/shard_map/ppermute | solution.py:28
  91.4 6.4 %copy-start.6 = (bf16[3,48,64]{0,2,1:T(8,128)(2,1)S(1)}, bf16[3,48,64]{0,2,1:T(8,128)(2,1)}, u32[]{:S(2)}) copy-start(bf16[3,48,64]{0,2,1:T(8,128)(2,1)} %get-tuple-element.174) | copy-start | bytes 55300
  92.4 6.4 %copy-start.5 = (bf16[3,48,64]{0,2,1:T(8,128)(2,1)S(1)}, bf16[3,48,64]{0,2,1:T(8,128)(2,1)}, u32[]{:S(2)}) copy-start(bf16[3,48,64]{0,2,1:T(8,128)(2,1)} %get-tuple-element.175) | copy-start | bytes 55300
  93.4 6.4 %copy-start.4 = (bf16[3,48,64]{0,2,1:T(8,128)(2,1)S(1)}, bf16[3,48,64]{0,2,1:T(8,128)(2,1)}, u32[]{:S(2)}) copy-start(bf16[3,48,64]{0,2,1:T(8,128)(2,1)} %get-tuple-element.176) | copy-start | bytes 55300
  98.8 4.1 copy-start.20
  99.8 4.1 copy-start.19
  103.9 7.5 %copy-start.18 = (bf16[3,48,64]{0,2,1:T(8,128)(2,1)S(1)}, bf16[3,48,64]{0,2,1:T(8,128)(2,1)}, u32[]{:S(2)}) copy-start(bf16[3,48,64]{0,2,1:T(8,128)(2,1)} %get-tuple-element.156) | copy-start | bytes 55300
  104.9 7.5 %copy-start.17 = (bf16[3,48,64]{0,2,1:T(8,128)(2,1)S(1)}, bf16[3,48,64]{0,2,1:T(8,128)(2,1)}, u32[]{:S(2)}) copy-start(bf16[3,48,64]{0,2,1:T(8,128)(2,1)} %get-tuple-element.157) | copy-start | bytes 55300
  107.1 6.3 %copy-start.16 = (bf16[3,48,64]{0,2,1:T(8,128)(2,1)S(1)}, bf16[3,48,64]{0,2,1:T(8,128)(2,1)}, u32[]{:S(2)}) copy-start(bf16[3,48,64]{0,2,1:T(8,128)(2,1)} %get-tuple-element.158) | copy-start | bytes 55300
  112.5 6.4 %copy-start.15 = (bf16[3,48,64]{0,2,1:T(8,128)(2,1)S(1)}, bf16[3,48,64]{0,2,1:T(8,128)(2,1)}, u32[]{:S(2)}) copy-start(bf16[3,48,64]{0,2,1:T(8,128)(2,1)} %get-tuple-element.161) | copy-start | bytes 55300
  113.5 6.4 %copy-start.14 = (bf16[3,48,64]{0,2,1:T(8,128)(2,1)S(1)}, bf16[3,48,64]{0,2,1:T(8,128)(2,1)}, u32[]{:S(2)}) copy-start(bf16[3,48,64]{0,2,1:T(8,128)(2,1)} %get-tuple-element.162) | copy-start | bytes 55300
  114.5 6.4 %copy-start.13 = (bf16[3,48,64]{0,2,1:T(8,128)(2,1)S(1)}, bf16[3,48,64]{0,2,1:T(8,128)(2,1)}, u32[]{:S(2)}) copy-start(bf16[3,48,64]{0,2,1:T(8,128)(2,1)} %get-tuple-element.163) | copy-start | bytes 55300
  119.8 6.3 %copy-start.12 = (bf16[3,48,64]{0,2,1:T(8,128)(2,1)S(1)}, bf16[3,48,64]{0,2,1:T(8,128)(2,1)}, u32[]{:S(2)}) copy-start(bf16[3,48,64]{0,2,1:T(8,128)(2,1)} %get-tuple-element.166) | copy-start | bytes 55300
  120.8 6.3 %copy-start.11 = (bf16[3,48,64]{0,2,1:T(8,128)(2,1)S(1)}, bf16[3,48,64]{0,2,1:T(8,128)(2,1)}, u32[]{:S(2)}) copy-start(bf16[3,48,64]{0,2,1:T(8,128)(2,1)} %get-tuple-element.167) | copy-start | bytes 55300
  121.8 6.3 %copy-start.10 = (bf16[3,48,64]{0,2,1:T(8,128)(2,1)S(1)}, bf16[3,48,64]{0,2,1:T(8,128)(2,1)}, u32[]{:S(2)}) copy-start(bf16[3,48,64]{0,2,1:T(8,128)(2,1)} %get-tuple-element.168) | copy-start | bytes 55300
  193.2 3.6 copy-start.56
  193.2 3.9 copy-start.23
  193.2 3.9 copy-start.54
  203.3 6.4 %copy-start.36 = (f32[64,1024]{1,0:T(8,128)}, f32[64,1024]{1,0:T(8,128)S(1)}, u32[]{:S(2)}) copy-start(f32[64,1024]{1,0:T(8,128)S(1)} %fusion.6) | copy-start | bytes 786436
  (45 other events, 65.2 us)
Sparse Core Ops, SparseCore 0:
  229.6 253.4 all-reduce.2
where the time goes:
time: 503 us; the launch traced here: 493 us
  waiting for transfers between devices  199 us (40%)
  local copies, waits for them, and re-layouts  129 us (26%)
  blocking collectives  72.7 us (14%)
  matrix products  32.8 us (7%)
  starting transfers between devices  22.9 us (5%)
  other arithmetic  21.3 us (4%)
  between operations  15.8 us (3%)
    psum x1, waiting for transfers between devices, per_device(): lax.psum((grad_kernel, grad_bias, grad_head), ('xy', 'gz'))  179 us
    psum x1, blocking collectives, per_device(): lax.psum((grad_kernel, grad_bias, grad_head), ('xy', 'gz'))  72.7 us
    slice x29, local copies, waits for them, and re-layouts, convolve(): kernel[offset]  50.3 us
    reshape x27, local copies, waits for them, and re-layouts, window(): return part_view.reshape(stacked_feats.shape[0], -1)  45.7 us
    dot_general x27, matrix products, kernel_grad(): lax.dot_general(window(stacked_feats, offset, time_slab, count_x, count_z...  22.7 us
    ppermute x2, starting transfers between devices, shifted(): return lax.ppermute(x, axis, [(i, (i + by) % count) for i in range(count)])  13 us
    reduce_sum x2, other arithmetic, complex_product(): jnp.sum(left_side[1][:, :, None] * right_side[1][None], axis=1)  12.4 us
  transfers between devices with their start and end apart: 7, of which 5 were waited for; matrix products, arithmetic and copies ran while one was open for 12% of the time, Pallas kernels for 0%

commit v1 on v0

v1 whole, which is shorter than its diff:
```python
import math

import jax
import jax.numpy as jnp
from jax import lax
from jax.experimental import pallas as pl
from jax.experimental.pallas import tpu as pltpu
from jax.sharding import PartitionSpec as P

LY = 64
ROWS = 1024
F32 = jnp.float32
BF16 = jnp.bfloat16

plane_pairs = ((0, 1), (0, 2), (0, 3), (1, 2), (1, 3), (2, 3))
INTERPRET = False
PARAMS = pltpu.CompilerParams(vmem_limit_bytes=56 * 2**20)


def lanes(shape):
    return lax.broadcasted_iota(jnp.int32, shape, len(shape) - 1)


def shift_y(x, by):
    if by == 0:
        return x
    axis = x.ndim - 1
    inner = pltpu.roll(x, (-by) % 128, axis)
    wrapped = pltpu.roll(x, (64 - by) % 128, axis)
    y = lanes(x.shape) % LY
    crossed = (y >= LY - by) if by > 0 else (y < -by)
    return jnp.where(crossed, wrapped, inner)


def leaf_starts(pair, leaf):
    back = ((), (pair[0],), (pair[1],), pair)[leaf]
    return tuple(0 if d in back else 1 for d in range(4))


LEAVES = [
    (p, leaf) + leaf_starts(pair, leaf) for p, pair in enumerate(plane_pairs) for leaf in range(4)
]


def weights_body(w_ref, out_ref, sum_ref):
    sum_ref[...] = jnp.zeros_like(sum_ref)

    def step(k, carry):
        dx = lax.div(k, 9)
        dz = lax.rem(lax.div(k, 3), 3)
        dt = lax.rem(k, 3)
        for dy in range(3):
            block = w_ref[k * 3 + dy].astype(F32)
            for p, leaf, sx, sy, sz, st in LEAVES:
                at = (((dt + st) * 4 + dz + sz) * 4 + dx + sx) * 4 + dy + sy
                c = 8 * p + 2 * leaf
                sum_ref[at, 2 * p : 2 * p + 2, :] += block[c : c + 2]
        return carry

    lax.fori_loop(0, 27, step, 0)
    for g in range(16):
        full = sum_ref[g * 16 : (g + 1) * 16].reshape(256, 64)
        high = full.astype(BF16).astype(F32)
        both = jnp.concatenate([high, full - high], axis=1)
        out_ref[g] = both.T.astype(BF16)


def loops_body(l_ref, xh_ref, zh_ref, o0_ref, o1_ref, xs_ref, zs_ref, pq_ref):
    pq_ref[...] = jnp.zeros_like(pq_ref)

    def stage(c, carry):
        for tau in range(5):
            xs_ref[c, pl.ds(4 * tau + 1, 2, stride=2), :] = xh_ref[c, tau]
            zs_ref[c, 4 * tau + 2 : 4 * tau + 4, :] = zh_ref[c, tau]
        return carry

    lax.fori_loop(0, 54, stage, 0)
    row = lax.broadcasted_iota(jnp.int32, (8, 128), 0)
    odd_x = row % 2 == 1
    high_z = row % 4 >= 2
    upper = lanes((8, 128)) >= LY

    def comp(d, ri, i, j):
        return ((d * 2 + ri) * 3 + i) * 3 + j

    def at_site(d, k):
        return [
            [[l_ref[comp(d, ri, i, j), 8 * k : 8 * k + 8, :] for j in range(3)] for i in range(3)]
            for ri in range(2)
        ]

    def ahead(d, step, k):
        def one(ri, i, j):
            c = comp(d, ri, i, j)
            if step == 3:
                if k < 2:
                    return l_ref[c, 8 * k + 4 : 8 * k + 12, :]
                return pltpu.roll(l_ref[c, 16:24, :], 4, 0)
            own = l_ref[c, 8 * k : 8 * k + 8, :]
            if step == 0:
                return jnp.where(odd_x, xs_ref[c - 18, 8 * k : 8 * k + 8, :], pltpu.roll(own, 7, 0))
            if step == 1:
                return shift_y(own, 1)
            h = c if d < 2 else c - 18
            beyond = jnp.where(high_z, zs_ref[h, 8 * k : 8 * k + 8, :], pltpu.roll(own, 6, 0))
            return pltpu.roll(jnp.where(upper, own, beyond), LY, 1)

        return [[[one(ri, i, j) for j in range(3)] for i in range(3)] for ri in range(2)]

    def product(a, b, i, j):
        re = a[0][i][0] * b[0][0][j] - a[1][i][0] * b[1][0][j]
        im = a[0][i][0] * b[1][0][j] + a[1][i][0] * b[0][0][j]
        for m in (1, 2):
            re = re + a[0][i][m] * b[0][m][j] - a[1][i][m] * b[1][m][j]
            im = im + a[0][i][m] * b[1][m][j] + a[1][i][m] * b[0][m][j]
        return re, im

    for k in range(3):
        for p, (mu, nu) in enumerate(plane_pairs):
            u_mu = at_site(mu, k)
            u_nu = at_site(nu, k)
            nu_ahead = ahead(nu, mu, k)
            mu_ahead = ahead(mu, nu, k)
            re = im = None
            for i in range(3):
                for j in range(3):
                    r1, i1 = product(u_mu, nu_ahead, i, j)
                    r2, i2 = product(u_nu, mu_ahead, i, j)
                    re_term = r1 * r2 + i1 * i2
                    im_term = i1 * r2 - r1 * i2
                    re = re_term if re is None else re + re_term
                    im = im_term if im is None else im + im_term
            pq_ref[pl.ds(128 * k + 2 * p, 8, stride=16), :] = re
            pq_ref[pl.ds(128 * k + 2 * p + 1, 8, stride=16), :] = im
    for tau in range(5):
        for x in range(2):
            r = tau * 4 + x
            o0_ref[x, tau] = pq_ref[r * 16 : r * 16 + 16, :].astype(BF16)
            r = tau * 4 + 2 + x
            o1_ref[x, tau] = pq_ref[r * 16 : r * 16 + 16, :].astype(BF16)


def layer_body(
    pos_ref, pat_ref, par_ref, el_ref, e_ref, er_ref, w_ref, bias_ref, head_ref, cot_ref,
    coef_ref, g_ref, q_ref, first_ref,
):
    upper = lanes((16, 128)) >= LY

    def build(tau, carry):
        for xi in range(5):
            src, x = ((el_ref, 0), (el_ref, 1), (e_ref, 0), (e_ref, 1), (er_ref, 0))[xi]
            tiles = [src[i, x, tau].astype(F32) for i in range(4)]
            for zs in range(6):
                if zs % 2 == 0:
                    tile = tiles[zs // 2]
                else:
                    mixed = jnp.where(upper, tiles[zs // 2], tiles[zs // 2 + 1])
                    tile = pltpu.roll(mixed, LY, 1)
                for dy in range(4):
                    lo = xi * 64 + dy * 16
                    q_ref[tau * 6 + zs, lo : lo + 16, :] = shift_y(tile, dy - 2).astype(BF16)
        return carry

    lax.fori_loop(0, 5, build, 0)

    def columns(t, x, g):
        at = (t + g // 4) * 6 + g % 4
        rows = slice(x * 64, x * 64 + 256)
        return jnp.concatenate([q_ref[at, rows, :], q_ref[at + 2, rows, :]], axis=1)

    lane = lanes((1, 256))
    y_pos = lane % LY
    z_pos = pos_ref[1] + lane // LY
    bias_sum = jnp.zeros((64, 256), F32)
    head_sums = [jnp.zeros((64, 256), F32) for _ in range(4)]
    lows = {}
    for t in range(2):
        for x in range(2):
            acc = jnp.zeros((128, 256), F32)
            for g in range(16):
                acc = acc + jnp.dot(w_ref[g], columns(t, x, g), preferred_element_type=F32)
            hidden = acc[:64] + acc[64:] + bias_ref[...]
            act = jnp.tanh(hidden)
            act_grad = jnp.zeros((64, 256), F32)
            for mu in range(4):
                fixed = pat_ref[mu, 0] * (pos_ref[0] + x) + pat_ref[mu, 3] * t + par_ref[mu]
                summed = pat_ref[mu, 1] * y_pos + pat_ref[mu, 2] * z_pos + fixed
                active = ((summed & 1) == 0).astype(F32)
                weight = head_ref[:, mu : mu + 1]
                coef = active * jnp.sum(weight * act, axis=0, keepdims=True)
                coef_ref[mu, t, x : x + 1, :] = coef
                coef_grad = active * cot_ref[mu, t, x : x + 1, :] * (1.0 / math.sqrt(ROWS))
                act_grad = act_grad + weight * coef_grad
                head_sums[mu] = head_sums[mu] + act * coef_grad
            hidden_grad = act_grad * (1.0 - act * act)
            bias_sum = bias_sum + hidden_grad
            lows[t, x] = hidden_grad.astype(BF16)

    small = jnp.zeros((64, 128), F32)
    spot = lanes((64, 128))
    for i, total in enumerate(head_sums + [bias_sum]):
        small = jnp.where(spot == i, jnp.sum(total, axis=1, keepdims=True), small)
    small = small.T

    def grad(g):
        acc = jnp.zeros((256, 64), F32)
        for t in range(2):
            for x in range(2):
                acc = acc + lax.dot_general(
                    columns(t, x, g), lows[t, x], (((1,), (1,)), ((), ())),
                    preferred_element_type=F32,
                )
        return acc

    for j in range(8):
        pair = jnp.concatenate([grad(j), grad(j + 8)], axis=1)
        if j == 0:
            first_ref[...] = pair[:16]
            rounded = small.astype(BF16).astype(F32)
            for row, part in ((12, rounded), (8, small - rounded)):
                first_ref[row : row + 4, 0:64] = part[0:4]
                first_ref[row : row + 1, 64:128] = part[4:5]
            pair = jnp.concatenate([first_ref[...], pair[16:]], axis=0)
        g_ref[j * 16 : (j + 1) * 16] = pair.reshape(16, 16, 128).astype(BF16)


def total_body(me_ref, in_ref, out_ref, sum_ref):
    sum_ref[...] = jnp.sum(in_ref[...].astype(F32), axis=0)
    count = sum_ref.shape[0]

    @pl.when(me_ref[0] == 8 // count)
    def _():
        at = 8 % count
        small = sum_ref[at : at + 4] + sum_ref[at + 4 : at + 8]
        rounded = small.astype(BF16).astype(F32)
        sum_ref[at : at + 4] = small - rounded
        sum_ref[at + 4 : at + 8] = rounded

    out_ref[...] = jnp.broadcast_to(sum_ref[...].astype(BF16)[None], out_ref.shape)


def expand_body(g_ref, k_ref, b_ref, h_ref, full_ref):
    for j in range(8):
        both = g_ref[j * 16 : (j + 1) * 16].astype(F32)
        full_ref[j * 16 : (j + 1) * 16] = both[:, :, :64]
        full_ref[(j + 8) * 16 : (j + 9) * 16] = both[:, :, 64:]

    def step(k, carry):
        dx = lax.div(k, 9)
        dz = lax.rem(lax.div(k, 3), 3)
        dt = lax.rem(k, 3)
        for dy in range(3):
            for p, leaf, sx, sy, sz, st in LEAVES:
                at = (((dt + st) * 4 + dz + sz) * 4 + dx + sx) * 4 + dy + sy
                c = 8 * p + 2 * leaf
                k_ref[k * 3 + dy, c : c + 2, :] = full_ref[at, 2 * p : 2 * p + 2, :]
        return carry

    lax.fori_loop(0, 27, step, 0)
    small = g_ref[0].astype(F32)
    small = small[12:16] + small[8:12]
    b_ref[...] = small[0:1, 64:128]
    h_ref[...] = jnp.concatenate([small, small], axis=0).T[0:64, 0:4]


def call(body, outs, scratch, *args, smem=0, name):
    vmem = pl.BlockSpec(memory_space=pltpu.VMEM)
    specs = [pl.BlockSpec(memory_space=pltpu.SMEM)] * smem + [vmem] * (len(args) - smem)
    return pl.pallas_call(
        body,
        out_shape=outs,
        in_specs=specs,
        out_specs=jax.tree.map(lambda _: vmem, outs),
        scratch_shapes=scratch,
        compiler_params=PARAMS,
        interpret=INTERPRET,
        name=name,
    )(*args)


def shifted(x, axis, by):
    count = lax.axis_size(axis)
    return lax.ppermute(x, axis, [(i, (i + by) % count) for i in range(count)])


def per_device(gauge_links, pattern, link_parity, conv_weight, conv_bias, head_weight, cotangent):
    rows = gauge_links.reshape(72, 6, 2, 2, 128).transpose(0, 1, 3, 2, 4)
    next_x = shifted(rows[18:, :5, :, 0, :], "xy", -1)
    edge_z = jnp.concatenate([rows[:36, :5, 0], rows[54:, :5, 0]])
    next_z = shifted(edge_z, "gz", -1)
    shape = jax.ShapeDtypeStruct
    weights = call(
        weights_body, shape((16, 128, 256), BF16), [pltpu.VMEM((256, 16, 64), F32)], conv_weight,
        name="weights",
    )
    half = shape((2, 5, 16, 128), BF16)
    low_z, high_z = call(
        loops_body, (half, half),
        [pltpu.VMEM((54, 24, 128), F32), pltpu.VMEM((54, 24, 128), F32), pltpu.VMEM((384, 128), F32)],
        rows.reshape(72, 24, 128), next_x, next_z, name="loops",
    )
    before_z = shifted(high_z, "gz", 1)
    after_z = shifted(low_z, "gz", -1)
    block = jnp.stack([before_z, low_z, high_z, after_z])
    before_x = shifted(block, "xy", 1)
    after_x = shifted(block, "xy", -1)
    pos = jnp.stack([lax.axis_index("xy") * 2, lax.axis_index("gz") * 4]).astype(jnp.int32)
    coefficients, grads = call(
        layer_body, (shape((4, 2, 2, 256), F32), shape((128, 16, 128), BF16)),
        [pltpu.VMEM((30, 320, 128), BF16), pltpu.VMEM((16, 128), F32)],
        pos, pattern, link_parity, before_x, block, after_x, weights, conv_bias[:, None],
        head_weight, cotangent, smem=3, name="layer",
    )
    both = ("xy", "gz")
    count = lax.axis_size(both)
    chunks = grads.reshape(count, 2048 // count, 128)
    chunks = lax.all_to_all(chunks, both, 0, 0, tiled=True)
    me = lax.axis_index(both).reshape(1)
    chunks = call(
        total_body, shape(chunks.shape, BF16), [pltpu.VMEM(chunks.shape[1:], F32)], me, chunks,
        smem=1, name="total",
    )
    chunks = lax.all_to_all(chunks, both, 0, 0, tiled=True)
    grad_kernel, grad_bias, grad_head = call(
        expand_body, (shape((81, 48, 64), F32), shape((1, 64), F32), shape((64, 4), F32)),
        [pltpu.VMEM((256, 16, 64), F32)], chunks.reshape(128, 16, 128), name="expand",
    )
    return coefficients, grad_kernel, grad_bias.reshape(64), grad_head


def solution(mesh):
    return jax.shard_map(
        per_device,
        mesh=mesh,
        in_specs=(
            P(None, None, None, None, None, "xy", "gz"),
            P(),
            P(),
            P(),
            P(),
            P(),
            P(None, None, "xy", "gz"),
        ),
        out_specs=(P(None, None, "xy", "gz"), P(), P(), P()),
        check_vma=False,
    )
```

time: 503 us -> 126 us (0.25); the launches traced: 493 us -> 125 us
  waiting for transfers between devices: 199 us -> 31.5 us
  local copies, waits for them, and re-layouts: 129 us -> 12.9 us
  blocking collectives: 72.7 us -> 26.5 us
  matrix products: 32.8 us -> 0 us
  Pallas kernels: 0 us -> 23.7 us
  other arithmetic: 21.3 us -> 1.54 us
  between operations: 15.8 us -> 0.76 us
  starting transfers between devices: 22.9 us -> 28.6 us
    psum x1 -> x0, waiting for transfers between devices: 179 us -> none  [per_device(): lax.psum((grad_kernel, grad_bias, grad_head), ('xy', 'gz'))]
    psum x1 -> x0, blocking collectives: 72.7 us -> none  [per_device(): lax.psum((grad_kernel, grad_bias, grad_head), ('xy', 'gz'))]
    slice x42 -> x2, local copies, waits for them, and re-layouts: 66.2 us -> 0.21 us  [per_device(): next_x = shifted(rows[18:, :5, :, 0, :], 'xy', -1)]
    reshape x30 -> x3, local copies, waits for them, and re-layouts: 49.5 us -> 3.71 us  [the longest x2 2.64 us: per_device(): rows = gauge_links.reshape(72, 6, 2, 2, 128).transpose(0, 1, 3, 2, 4)]
    dot_general x57 -> x0, matrix products: 32.8 us -> none  [the longest x27 22.7 us: kernel_grad(): lax.dot_general(window(stacked_feats, offset, time_slab, count_x, count_z...]
    all_to_all x0 -> x1, blocking collectives: none -> 26.5 us  [per_device(): chunks = lax.all_to_all(chunks, both, 0, 0, tiled=True)]
    pallas_call x0 -> x5, Pallas kernels: none -> 23.7 us  [call(): pl.pallas_call(body, out_shape=outs, in_specs=specs, out_specs=jax.tree.m...]
    all_to_all x0 -> x1, waiting for transfers between devices: none -> 20.2 us  [per_device(): chunks = lax.all_to_all(chunks, both, 0, 0, tiled=True)]
  transfers between devices with their start and end apart: 7 -> 7, of which waited for: 5 -> 6; matrix products, arithmetic and copies ran while one was open for 12% -> 4% of each run, Pallas kernels for 0% -> 3%
where the time goes in v1:
time: 126 us; the launch traced here: 125 us
  waiting for transfers between devices  31.5 us (25%)
  starting transfers between devices  28.6 us (23%)
  blocking collectives  26.5 us (21%)
  Pallas kernels  23.7 us (19%)
  local copies, waits for them, and re-layouts  12.9 us (10%)
  other arithmetic  1.54 us (1%)
    all_to_all x1, blocking collectives, per_device(): chunks = lax.all_to_all(chunks, both, 0, 0, tiled=True)  26.5 us
    pallas_call x5, Pallas kernels, call(): pl.pallas_call(body, out_shape=outs, in_specs=specs, out_specs=jax.tree.m...  23.7 us
    ppermute x6, starting transfers between devices, shifted(): return lax.ppermute(x, axis, [(i, (i + by) % count) for i in range(count)])  22.6 us
    all_to_all x1, waiting for transfers between devices, per_device(): chunks = lax.all_to_all(chunks, both, 0, 0, tiled=True)  20.2 us
    ppermute x6, waiting for transfers between devices, shifted(): return lax.ppermute(x, axis, [(i, (i + by) % count) for i in range(count)])  11.4 us
    unnamed x24, local copies, waits for them, and re-layouts  7.95 us
    all_to_all x1, starting transfers between devices, per_device(): chunks = lax.all_to_all(chunks, both, 0, 0, tiled=True)  6.07 us
    reshape x2, local copies, waits for them, and re-layouts, per_device(): rows = gauge_links.reshape(72, 6, 2, 2, 128).transpose(0, 1, 3, 2, 4)  2.64 us
  transfers between devices with their start and end apart: 7, of which 6 were waited for; matrix products, arithmetic and copies ran while one was open for 4% of the time, Pallas kernels for 3%

profile of v1, /device:TPU:1, one launch (start us, length us, event | category | flops | bytes accessed | tf_op | source)
XLA Modules:
  0.0 125.5 jit_solution(6955162816035736100)
XLA Ops:
  0.6 2.2 %reshape.26 = f32[72,6,2,2,128]{4,3,2,1,0:T(2,128)S(1)} reshape(f32[4,2,3,3,6,2,256]{6,5,4,3,2,1,0:T(2,128)} %param.7) | data formatting | bytes 1769472 | tf_op jit(solution)/shard_map/reshape | solution.py:287
  2.8 0.5 copy.30
  3.3 0.2 slice.12
  3.7 11.3 %collective-permute-start = (f32[54,5,2,128]{3,2,1,0:T(2,128)S(1)}, f32[54,5,2,128]{3,2,1,0:T(2,128)S(1)}, u32[]{:S(2)}, u32[]{:S(2)}) collective-permute-start(f32[54,5,2,128]{3,2,1,0:T(2,128)S(1)} %copy.20), channel_id=1, source_target_pairs={{0,252},{4,0},{8,4},{12,8},{16,12},{20,16},{24,20},{28,24},{32,28}... | collective-permute-start | bytes 829448 | tf_op jit(solution)/shard_map/ppermute | solution.py:283
  15.1 1.0 collective-permute-start.1
  16.2 0.2 copy.18
  16.4 1.1 copy.21.l_ref
  17.5 2.8 %collective-permute-done.xh_ref = f32[54,5,2,128]{3,2,1,0:T(2,128)S(1)} collective-permute-done((f32[54,5,2,128]{3,2,1,0:T(2,128)S(1)}, f32[54,5,2,128]{3,2,1,0:T(2,128)S(1)}, u32[]{:S(2)}, u32[]{:S(2)}) %collective-permute-start) | collective-permute-done | bytes 276512 | tf_op jit(solution)/shard_map/ppermute | solution.py:283
  20.2 0.9 collective-permute-done.1.zh_ref
  21.2 0.7 copy-done.4
  21.9 3.7 %loops.1 = (bf16[2,5,16,128]{3,2,1,0:T(8,128)(2,1)}, bf16[2,5,16,128]{3,2,1,0:T(8,128)(2,1)}) custom-call(f32[72,24,128]{2,1,0:T(8,128)} %copy.21.l_ref, f32[54,5,2,128]{3,2,1,0:T(2,128)} %copy-done.3, f32[54,5,2,128]{3,2,1,0:T(2,128)} %copy-done.4), custom_call_target="tpu_custom_call" | custom-call | tf_op jit(solution)/shard_map/loops/pallas_call | solution.py:269
  25.5 1.6 %collective-permute-start.2 = (bf16[2,5,16,128]{3,2,1,0:T(8,128)(2,1)}, bf16[2,5,16,128]{3,2,1,0:T(8,128)(2,1)S(1)}, u32[]{:S(2)}, u32[]{:S(2)}) collective-permute-start(bf16[2,5,16,128]{3,2,1,0:T(8,128)(2,1)} %get-tuple-element.11), channel_id=1, source_target_pairs={{0,1},{1,2},{2,3},{3,0},{4,5},{5,6},{6,7},{7,4},{8,9},{9,10},{10,1... | collective-permute-start | bytes 122888 | tf_op jit(solution)/shard_map/ppermute | solution.py:283
  27.1 1.4 %collective-permute-done.2 = bf16[2,5,16,128]{3,2,1,0:T(8,128)(2,1)S(1)} collective-permute-done((bf16[2,5,16,128]{3,2,1,0:T(8,128)(2,1)}, bf16[2,5,16,128]{3,2,1,0:T(8,128)(2,1)S(1)}, u32[]{:S(2)}, u32[]{:S(2)}) %collective-permute-start.2) | collective-permute-done | bytes 40992 | tf_op jit(solution)/shard_map/ppermute | solution.py:283
  28.6 2.2 %collective-permute-done.3 = bf16[2,5,16,128]{3,2,1,0:T(8,128)(2,1)S(1)} collective-permute-done((bf16[2,5,16,128]{3,2,1,0:T(8,128)(2,1)}, bf16[2,5,16,128]{3,2,1,0:T(8,128)(2,1)S(1)}, u32[]{:S(2)}, u32[]{:S(2)}) %collective-permute-start.3) | collective-permute-done | bytes 40992 | tf_op jit(solution)/shard_map/ppermute | solution.py:283
  30.8 0.8 pad_maximum_fusion.1.e_ref
  31.6 8.6 %collective-permute-start.5 = (bf16[4,2,5,16,128]{4,3,2,1,0:T(8,128)(2,1)S(1)}, bf16[4,2,5,16,128]{4,3,2,1,0:T(8,128)(2,1)S(1)}, u32[]{:S(2)}, u32[]{:S(2)}) collective-permute-start(bf16[4,2,5,16,128]{4,3,2,1,0:T(8,128)(2,1)S(1)} %pad_maximum_fusion.1.e_ref), channel_id=1, source_target_pairs={{0,252},{4,0},{8,4},{12,8},{16,12},{20,16},{24,20},{28,24},{32,28}... | collective-permute-start | bytes 491528 | tf_op jit(solution)/shard_map/ppermute | solution.py:283
  40.2 0.7 copy.23.bias_ref
  40.9 0.7 copy.24.head_ref
  41.6 1.5 %copy.22.w_ref = bf16[81,48,64]{2,1,0:T(8,128)(2,1)} copy(bf16[81,48,64]{0,2,1:T(8,128)(2,1)S(1)} %copy-done.1) | data formatting | bytes 995328 | tf_op args[3]
  43.2 4.2 %weights.1.w_ref = bf16[16,128,256]{2,1,0:T(8,128)(2,1)} custom-call(bf16[81,48,64]{2,1,0:T(8,128)(2,1)} %copy.22.w_ref), custom_call_target="tpu_custom_call" | custom-call | tf_op jit(solution)/shard_map/weights/pallas_call | solution.py:269
  47.4 0.6 pad_add_fusion.pos_ref
  48.0 4.0 %collective-permute-done.4.el_ref = bf16[4,2,5,16,128]{4,3,2,1,0:T(8,128)(2,1)S(1)} collective-permute-done((bf16[4,2,5,16,128]{4,3,2,1,0:T(8,128)(2,1)S(1)}, bf16[4,2,5,16,128]{4,3,2,1,0:T(8,128)(2,1)S(1)}, u32[]{:S(2)}, u32[]{:S(2)}) %collective-permute-start.4) | collective-permute-done | bytes 163872 | tf_op jit(solution)/shard_map/ppermute | solution.py:283
  52.1 0.7 copy-done.6
  52.7 10.0 %layer.1 = (f32[4,2,2,256]{3,2,1,0:T(2,128)}, bf16[128,16,128]{2,1,0:T(8,128)(2,1)}) custom-call(s32[2]{0:T(128)} %pad_add_fusion.pos_ref, s32[4,4]{1,0:T(4,128)} %pat_ref.1, s32[4]{0:T(128)} %par_ref.1, bf16[4,2,5,16,128]{4,3,2,1,0:T(8,128)(2,1)} %copy-done.6, bf16[4,2,5,16,128]{4,3,2,1,0:T(8,128)(2,1)} %copy-done.2, bf16[4,2,5,16,128]{4,3,2,1,0:T(8,128)(2,1)} %copy-done.5, ...), custom_call_target="tpu_custom_call" | custom-call | tf_op jit(solution)/shard_map/layer/pallas_call | solution.py:269
  62.7 6.1 %all-to-all-start = ((bf16[256,8,128]{2,1,0:T(8,128)(2,1)}), bf16[256,8,128]{2,1,0:T(8,128)(2,1)S(1)}, u32[]{:S(2)}, u32[]{:S(2)}) async-start(bf16[256,8,128]{2,1,0:T(8,128)(2,1)} %bitcast.30), calls=%async_computation | async-start | bytes 1048576 | tf_op jit(solution)/shard_map/all_to_all | solution.py:317
  68.8 20.2 %all-to-all-done.in_ref = bf16[256,8,128]{2,1,0:T(8,128)(2,1)S(1)} async-done(((bf16[256,8,128]{2,1,0:T(8,128)(2,1)}), bf16[256,8,128]{2,1,0:T(8,128)(2,1)S(1)}, u32[]{:S(2)}, u32[]{:S(2)}) %all-to-all-start) | async-done | bytes 524320 | tf_op jit(solution)/shard_map/all_to_all | solution.py:317
  88.9 0.8 copy-done
  89.7 2.2 %total.1 = bf16[256,8,128]{2,1,0:T(8,128)(2,1)} custom-call(s32[1]{0:T(128)} %bitcast.13.me_ref, bf16[256,8,128]{2,1,0:T(8,128)(2,1)} %copy-done), custom_call_target="tpu_custom_call" | custom-call | tf_op jit(solution)/shard_map/total/pallas_call | solution.py:269
  91.9 26.5 %all_to_all.10 = bf16[256,8,128]{2,1,0:T(8,128)(2,1)} all-to-all(bf16[256,8,128]{2,1,0:T(8,128)(2,1)} %total.1), channel_id=1, replica_groups=mesh['xy'=64,'gz'=4] {'xy','gz'}, dimensions={0} | all-to-all | bytes 1048576 | tf_op jit(solution)/shard_map/all_to_all | solution.py:323
  118.3 3.7 %expand.1 = (f32[81,48,64]{2,1,0:T(8,128)}, f32[1,64]{1,0:T(1,128)}, f32[64,4]{1,0:T(8,128)}) custom-call(bf16[128,16,128]{2,1,0:T(8,128)(2,1)} %bitcast.28), custom_call_target="tpu_custom_call" | custom-call | tf_op jit(solution)/shard_map/expand/pallas_call | solution.py:269
  122.0 2.8 %copy.25 = f32[81,48,64]{0,2,1:T(8,128)} copy(f32[81,48,64]{2,1,0:T(8,128)} %get-tuple-element.23) | data formatting | bytes 1990656
  124.8 0.7 copy.26
  (25 shorter events, 0.4 us)
Async XLA Ops:
  3.7 16.6 %collective-permute-start = (f32[54,5,2,128]{3,2,1,0:T(2,128)S(1)}, f32[54,5,2,128]{3,2,1,0:T(2,128)S(1)}, u32[]{:S(2)}, u32[]{:S(2)}) collective-permute-start(f32[54,5,2,128]{3,2,1,0:T(2,128)S(1)} %copy.20), channel_id=1, source_target_pairs={{0,252},{4,0},{8,4},{12,8},{16,12},{20,16},{24,20},{28,24},{32,28}... | collective-permute-start | bytes 829448 | tf_op jit(solution)/shard_map/ppermute | solution.py:283
  15.1 6.0 %collective-permute-start.1 = (f32[54,5,2,128]{3,2,1,0:T(2,128)S(1)}, f32[54,5,2,128]{3,2,1,0:T(2,128)S(1)}, u32[]{:S(2)}, u32[]{:S(2)}) collective-permute-start(f32[54,5,2,128]{3,2,1,0:T(2,128)S(1)} %pad_maximum_fusion), channel_id=1, source_target_pairs={{0,3},{1,0},{2,1},{3,2},{4,7},{5,4},{6,5},{7,6},{8,11},{9,8},{10,9... | collective-permute-start | bytes 829448 | tf_op jit(solution)/shard_map/ppermute | solution.py:283
  16.4 23.9 %copy-start.9 = (f32[64]{0:T(128)S(1)}, f32[64]{0:T(128)}, u32[]{:S(2)}) copy-start(f32[64]{0:T(128)} %param.11) | copy-start | bytes 772
  16.4 24.6 %copy-start.8 = (f32[64,4]{0,1:T(4,128)S(1)}, f32[64,4]{0,1:T(4,128)}, u32[]{:S(2)}) copy-start(f32[64,4]{0,1:T(4,128)} %param.12) | copy-start | bytes 3076
  16.4 25.3 %copy-start.1 = (bf16[81,48,64]{0,2,1:T(8,128)(2,1)S(1)}, bf16[81,48,64]{0,2,1:T(8,128)(2,1)}, u32[]{:S(2)}) copy-start(bf16[81,48,64]{0,2,1:T(8,128)(2,1)} %param.10) | copy-start | bytes 1492996
  20.2 0.9 copy-start.3
  21.2 0.7 copy-start.4
  25.5 3.0 %collective-permute-start.2 = (bf16[2,5,16,128]{3,2,1,0:T(8,128)(2,1)}, bf16[2,5,16,128]{3,2,1,0:T(8,128)(2,1)S(1)}, u32[]{:S(2)}, u32[]{:S(2)}) collective-permute-start(bf16[2,5,16,128]{3,2,1,0:T(8,128)(2,1)} %get-tuple-element.11), channel_id=1, source_target_pairs={{0,1},{1,2},{2,3},{3,0},{4,5},{5,6},{6,7},{7,4},{8,9},{9,10},{10,1... | collective-permute-start | bytes 122888 | tf_op jit(solution)/shard_map/ppermute | solution.py:283
  27.1 3.6 %collective-permute-start.3 = (bf16[2,5,16,128]{3,2,1,0:T(8,128)(2,1)}, bf16[2,5,16,128]{3,2,1,0:T(8,128)(2,1)S(1)}, u32[]{:S(2)}, u32[]{:S(2)}) collective-permute-start(bf16[2,5,16,128]{3,2,1,0:T(8,128)(2,1)} %get-tuple-element.12), channel_id=1, source_target_pairs={{0,3},{1,0},{2,1},{3,2},{4,7},{5,4},{6,5},{7,6},{8,11},{9,8},{10,9... | collective-permute-start | bytes 122888 | tf_op jit(solution)/shard_map/ppermute | solution.py:283
  31.6 20.5 %copy-start.2 = (bf16[4,2,5,16,128]{4,3,2,1,0:T(8,128)(2,1)}, bf16[4,2,5,16,128]{4,3,2,1,0:T(8,128)(2,1)S(1)}, u32[]{:S(2)}) copy-start(bf16[4,2,5,16,128]{4,3,2,1,0:T(8,128)(2,1)S(1)} %pad_maximum_fusion.1.e_ref) | copy-start | bytes 491524
  31.6 16.4 %collective-permute-start.5 = (bf16[4,2,5,16,128]{4,3,2,1,0:T(8,128)(2,1)S(1)}, bf16[4,2,5,16,128]{4,3,2,1,0:T(8,128)(2,1)S(1)}, u32[]{:S(2)}, u32[]{:S(2)}) collective-permute-start(bf16[4,2,5,16,128]{4,3,2,1,0:T(8,128)(2,1)S(1)} %pad_maximum_fusion.1.e_ref), channel_id=1, source_target_pairs={{0,252},{4,0},{8,4},{12,8},{16,12},{20,16},{24,20},{28,24},{32,28}... | collective-permute-start | bytes 491528 | tf_op jit(solution)/shard_map/ppermute | solution.py:283
  40.2 11.8 %collective-permute-start.4 = (bf16[4,2,5,16,128]{4,3,2,1,0:T(8,128)(2,1)S(1)}, bf16[4,2,5,16,128]{4,3,2,1,0:T(8,128)(2,1)S(1)}, u32[]{:S(2)}, u32[]{:S(2)}) collective-permute-start(bf16[4,2,5,16,128]{4,3,2,1,0:T(8,128)(2,1)S(1)} %pad_maximum_fusion.1.e_ref), channel_id=1, source_target_pairs={{0,4},{4,8},{8,12},{12,16},{16,20},{20,24},{24,28},{28,32},{32,36}... | collective-permute-start | bytes 491528 | tf_op jit(solution)/shard_map/ppermute | solution.py:283
  48.0 4.0 %copy-start.5 = (bf16[4,2,5,16,128]{4,3,2,1,0:T(8,128)(2,1)}, bf16[4,2,5,16,128]{4,3,2,1,0:T(8,128)(2,1)S(1)}, u32[]{:S(2)}) copy-start(bf16[4,2,5,16,128]{4,3,2,1,0:T(8,128)(2,1)S(1)} %collective-permute-done.5.er_ref) | copy-start | bytes 491524
  52.1 0.7 copy-start.6
  62.7 26.2 %all-to-all-start = ((bf16[256,8,128]{2,1,0:T(8,128)(2,1)}), bf16[256,8,128]{2,1,0:T(8,128)(2,1)S(1)}, u32[]{:S(2)}, u32[]{:S(2)}) async-start(bf16[256,8,128]{2,1,0:T(8,128)(2,1)} %bitcast.30), calls=%async_computation | async-start | bytes 1048576 | tf_op jit(solution)/shard_map/all_to_all | solution.py:317
  88.9 0.8 copy-start
  122.0 2.9 %copy-start.7 = (f32[64,4]{1,0:T(8,128)S(1)}, f32[64,4]{1,0:T(8,128)}, u32[]{:S(2)}) copy-start(f32[64,4]{1,0:T(8,128)} %get-tuple-element.25) | copy-start | bytes 3076

commit v2 on v1

v2 whole, which is shorter than its diff:
```python
import math

import jax
import jax.numpy as jnp
import numpy as np
from jax import lax
from jax.experimental import pallas as pl
from jax.experimental.pallas import tpu as pltpu
from jax.sharding import PartitionSpec as P

LY = 64
ROWS = 1024
F32 = jnp.float32
BF16 = jnp.bfloat16

plane_pairs = ((0, 1), (0, 2), (0, 3), (1, 2), (1, 3), (2, 3))
INTERPRET = False
PARAMS = pltpu.CompilerParams(vmem_limit_bytes=56 * 2**20)


def lanes(shape):
    return lax.broadcasted_iota(jnp.int32, shape, len(shape) - 1)


def shift_y(x, by):
    if by == 0:
        return x
    axis = x.ndim - 1
    inner = pltpu.roll(x, (-by) % 128, axis)
    wrapped = pltpu.roll(x, (64 - by) % 128, axis)
    y = lanes(x.shape) % LY
    crossed = (y >= LY - by) if by > 0 else (y < -by)
    return jnp.where(crossed, wrapped, inner)


def plane_tables():
    tiles, keep, spread = [], [], np.zeros((6, 144, 512), np.float32)
    for p, pair in enumerate(plane_pairs):
        spans = [range(0 if d in pair else 1, 4) for d in range(4)]
        tiles.append([(z, y) for z in spans[2] for y in spans[1]])
        kept = {}
        table = np.zeros((16 * len(tiles[p]), 256), np.float32)
        for i, (z, y) in enumerate(tiles[p]):
            for x in spans[0]:
                for t in spans[3]:
                    table[16 * i + 4 * x + t, len(kept)] = 1
                    kept[x, y, z, t] = len(kept)
        keep.append(table)
        for leaf, back in enumerate(((), (pair[0],), (pair[1],), pair)):
            sx, sy, sz, st = (0 if d in back else 1 for d in range(4))
            for k in range(81):
                dx, dz, dt, dy = k // 27, k // 9 % 3, k // 3 % 3, k % 3
                spread[p, kept[dx + sx, dy + sy, dz + sz, dt + st], leaf * 128 + k] = 1
    return tiles, keep, spread


TILES, KEEP, SPREAD = plane_tables()
SIZES = [16 * len(t) for t in TILES]
STARTS = [sum(SIZES[:p]) for p in range(6)]
NT = (((1,), (1,)), ((), ()))


def weights_body(w_ref, spread_ref, keep_ref, head_ref, bias_ref, out_ref, small_ref):
    for p in range(6):
        table = keep_ref[STARTS[p] : STARTS[p] + SIZES[p], :]
        for r in range(2):
            full = jnp.zeros((64, 144), F32)
            for leaf in range(4):
                full = full + lax.dot_general(
                    w_ref[8 * p + 2 * leaf + r], spread_ref[p, :, leaf * 128 : leaf * 128 + 81], NT,
                    preferred_element_type=F32,
                )
            high = full.astype(BF16)
            low = (full - high.astype(F32)).astype(BF16)
            both = jnp.concatenate([high, low], axis=0)
            out_ref[2 * p + r, :, 0 : SIZES[p]] = lax.dot_general(
                both, table[:, :144], NT, preferred_element_type=F32
            ).astype(BF16)
    small_ref[...] = jnp.concatenate([head_ref[...], bias_ref[...], jnp.zeros((3, 64), F32)], axis=0).T


def loops_body(l_ref, xh_ref, zh_ref, o0_ref, o1_ref, xs_ref, zs_ref, pq_ref, tile_ref):
    def stage(c, carry):
        for tau in range(5):
            xs_ref[c, pl.ds(4 * tau + 1, 2, stride=2), :] = xh_ref[c, tau]
            zs_ref[c, 4 * tau + 2 : 4 * tau + 4, :] = zh_ref[c, tau]
        return carry

    lax.fori_loop(0, 54, stage, 0)
    row = lax.broadcasted_iota(jnp.int32, (8, 128), 0)
    odd_x = row % 2 == 1
    high_z = row % 4 >= 2
    upper = lanes((8, 128)) >= LY

    def comp(d, ri, i, j):
        return ((d * 2 + ri) * 3 + i) * 3 + j

    def at_site(d, k):
        return [
            [[l_ref[comp(d, ri, i, j), 8 * k : 8 * k + 8, :] for j in range(3)] for i in range(3)]
            for ri in range(2)
        ]

    def ahead(d, step, k):
        def one(ri, i, j):
            c = comp(d, ri, i, j)
            if step == 3:
                if k < 2:
                    return l_ref[c, 8 * k + 4 : 8 * k + 12, :]
                return pltpu.roll(l_ref[c, 16:24, :], 4, 0)
            own = l_ref[c, 8 * k : 8 * k + 8, :]
            if step == 0:
                return jnp.where(odd_x, xs_ref[c - 18, 8 * k : 8 * k + 8, :], pltpu.roll(own, 7, 0))
            if step == 1:
                return shift_y(own, 1)
            h = c if d < 2 else c - 18
            beyond = jnp.where(high_z, zs_ref[h, 8 * k : 8 * k + 8, :], pltpu.roll(own, 6, 0))
            return pltpu.roll(jnp.where(upper, own, beyond), LY, 1)

        return [[[one(ri, i, j) for j in range(3)] for i in range(3)] for ri in range(2)]

    def product(a, b, i, j):
        re = a[0][i][0] * b[0][0][j] - a[1][i][0] * b[1][0][j]
        im = a[0][i][0] * b[1][0][j] + a[1][i][0] * b[0][0][j]
        for m in (1, 2):
            re = re + a[0][i][m] * b[0][m][j] - a[1][i][m] * b[1][m][j]
            im = im + a[0][i][m] * b[1][m][j] + a[1][i][m] * b[0][m][j]
        return re, im

    for k in range(3):
        for p, (mu, nu) in enumerate(plane_pairs):
            u_mu = at_site(mu, k)
            u_nu = at_site(nu, k)
            nu_ahead = ahead(nu, mu, k)
            mu_ahead = ahead(mu, nu, k)
            re = im = None
            for i in range(3):
                for j in range(3):
                    r1, i1 = product(u_mu, nu_ahead, i, j)
                    r2, i2 = product(u_nu, mu_ahead, i, j)
                    re_term = r1 * r2 + i1 * i2
                    im_term = i1 * r2 - r1 * i2
                    re = re_term if re is None else re + re_term
                    im = im_term if im is None else im + im_term
            pq_ref[2 * p, 8 * k : 8 * k + 8, :] = re
            pq_ref[2 * p + 1, 8 * k : 8 * k + 8, :] = im
    for c in range(12):
        for lb, o_ref in enumerate((o0_ref, o1_ref)):
            for t in range(2):
                for x in range(2):
                    tile_ref[c, lb, t * 8 + x * 4 : t * 8 + x * 4 + 4, :] = pq_ref[
                        c, pl.ds(4 * t + 2 * lb + x, 4, stride=4), :
                    ]
            o_ref[c] = tile_ref[c, lb].astype(BF16)


def layer_body(
    x0_ref, z0_ref, pat_ref, par_ref, el_ref, e_ref, er_ref, w_ref, small_ref, keep_ref, cot_ref,
    coef_ref, g_ref, a_ref, low_ref, rows_ref,
):
    first = lax.broadcasted_iota(jnp.int32, (8, 128), 0) < 4
    lane = lanes((8, 128))
    upper = lane >= LY

    def crossed(by):
        y = lane % LY
        return (y >= LY - by) if by > 0 else (y < -by)

    for p in range(6):
        offsets = sorted({y for _, y in TILES[p]})
        for r in range(2):
            c = 2 * p + r
            for t in range(2):
                part = slice(8 * t, 8 * t + 8)
                cols = []
                for i in range(4):
                    left, own, right = (ref[i, c].astype(F32)[part] for ref in (el_ref, e_ref, er_ref))
                    cols.append((
                        (left, own),
                        (
                            pltpu.roll(jnp.where(first, own, left), 4, 0),
                            pltpu.roll(jnp.where(first, right, own), 4, 0),
                        ),
                    ))
                for x in range(2):
                    for y in offsets:
                        by = y - 2
                        made = []
                        for h in range(2):
                            plain, other = [], []
                            for i in range(4):
                                v = cols[i][x][h]
                                near = v if by == 0 else pltpu.roll(v, (-by) % 128, 1)
                                far = pltpu.roll(v, (LY - by) % 128, 1)
                                if by == 0:
                                    plain.append(near)
                                    other.append(far)
                                else:
                                    plain.append(jnp.where(crossed(by), far, near))
                                    other.append(jnp.where(crossed(by), near, far))
                            made.append([
                                plain[z // 2] if z % 2 == 0 else jnp.where(upper, other[z // 2 + 1], other[z // 2])
                                for z in range(6)
                            ])
                        both = [jnp.concatenate([u, v], axis=0).astype(BF16) for u, v in zip(*made)]
                        for n, (z, y_at) in enumerate(TILES[p]):
                            if y_at == y:
                                for lb in range(2):
                                    col = (t * 4 + x * 2 + lb) * 128
                                    a_ref[c, 16 * n : 16 * n + 16, col : col + 128] = both[z + 2 * lb]

    lane = lanes((1, 256))
    y_pos = lane % LY
    z_pos = z0_ref[0] + lane // LY
    bias_sum = jnp.zeros((64, 256), F32)
    head_sums = [jnp.zeros((64, 256), F32) for _ in range(4)]
    for t in range(2):
        for x in range(2):
            cols = slice((t * 2 + x) * 256, (t * 2 + x) * 256 + 256)
            acc = jnp.zeros((128, 256), F32)
            for c in range(12):
                size = SIZES[c // 2]
                acc = acc + jnp.dot(
                    w_ref[c, :, 0:size], a_ref[c, 0:size, cols], preferred_element_type=F32
                )
            hidden = acc[:64] + acc[64:] + small_ref[:, 4:5]
            act = jnp.tanh(hidden)
            act_grad = jnp.zeros((64, 256), F32)
            for mu in range(4):
                fixed = pat_ref[mu, 0] * (x0_ref[0] + x) + pat_ref[mu, 3] * t + par_ref[mu]
                summed = pat_ref[mu, 1] * y_pos + pat_ref[mu, 2] * z_pos + fixed
                active = ((summed & 1) == 0).astype(F32)
                weight = small_ref[:, mu : mu + 1]
                coef = active * jnp.sum(weight * act, axis=0, keepdims=True)
                coef_ref[mu, t, x : x + 1, :] = coef
                coef_grad = active * cot_ref[mu, t, x : x + 1, :] * (1.0 / math.sqrt(ROWS))
                act_grad = act_grad + weight * coef_grad
                head_sums[mu] = head_sums[mu] + act * coef_grad
            hidden_grad = act_grad * (1.0 - act * act)
            bias_sum = bias_sum + hidden_grad
            low_ref[:, cols] = hidden_grad.astype(BF16)

    spot = lanes((64, 128))
    small = jnp.zeros((64, 128), F32)
    for i, total in enumerate(head_sums + [bias_sum]):
        value = jnp.sum(total, axis=1, keepdims=True)
        rounded = value.astype(BF16).astype(F32)
        small = jnp.where(spot == i, rounded, jnp.where(spot == i + 8, value - rounded, small))

    def put(j, value):
        rows_ref[pl.ds(j, 64, stride=16), :] = value

    ends = [jnp.zeros((64, 128), F32), jnp.zeros((64, 128), F32)]
    for c in range(12):
        start, size = STARTS[c // 2], SIZES[c // 2]
        grad = lax.dot_general(low_ref[...], a_ref[c, 0:size, :], NT, preferred_element_type=F32)
        kept = jnp.dot(grad.astype(BF16), keep_ref[start : start + size, :], preferred_element_type=F32)
        put(c, kept[:, :128])
        end = kept[:, 128:]
        ends[c // 8] = ends[c // 8] + (pltpu.roll(end, 16 * (c % 8), 1) if c % 8 else end)
    put(12, ends[0])
    put(13, ends[1])
    put(14, small)
    put(15, jnp.zeros((64, 128), F32))
    g_ref[...] = rows_ref[...].reshape(64, 16, 128).astype(BF16)


def total_body(me_ref, in_ref, out_ref):
    total = jnp.sum(in_ref[...].astype(F32), axis=0)
    row = me_ref[0] * total.shape[0] + lax.broadcasted_iota(jnp.int32, total.shape, 0)
    lane = lanes(total.shape)
    whole = jnp.where(lane < 8, total + pltpu.roll(total, 120, 1), 0.0)
    rounded = whole.astype(BF16).astype(F32)
    rest = pltpu.roll(whole - rounded, 8, 1)
    total = jnp.where(row % 16 == 14, jnp.where(lane < 8, rounded, rest), total)
    out_ref[...] = jnp.broadcast_to(total.astype(BF16)[None], out_ref.shape)


def expand_body(g_ref, spread_ref, k_ref, b_ref, h_ref, rows_ref):
    rows_ref[...] = g_ref[...].astype(F32).reshape(1024, 128)

    def get(j):
        return rows_ref[pl.ds(j, 64, stride=16), :]

    ends = [get(12), get(13)]
    for c in range(12):
        p, r = c // 2, c % 2
        end = ends[c // 8]
        end = pltpu.roll(end, 128 - 16 * (c % 8), 1) if c % 8 else end
        kept = jnp.concatenate([get(c), end[:, :16]], axis=1).astype(BF16)
        full = jnp.dot(kept, spread_ref[p], preferred_element_type=F32)
        for leaf in range(4):
            k_ref[8 * p + 2 * leaf + r] = full[:, leaf * 128 : leaf * 128 + 81]
    small = get(14)
    small = (small + pltpu.roll(small, 120, 1)).T
    h_ref[...] = small[0:4]
    b_ref[...] = small[4:5]


def call(body, outs, scratch, *args, smem=0, name):
    vmem = pl.BlockSpec(memory_space=pltpu.VMEM)
    specs = [pl.BlockSpec(memory_space=pltpu.SMEM)] * smem + [vmem] * (len(args) - smem)
    return pl.pallas_call(
        body,
        out_shape=outs,
        in_specs=specs,
        out_specs=jax.tree.map(lambda _: vmem, outs),
        scratch_shapes=scratch,
        compiler_params=PARAMS,
        interpret=INTERPRET,
        name=name,
    )(*args)


def shifted(x, axis, by):
    count = lax.axis_size(axis)
    return lax.ppermute(x, axis, [(i, (i + by) % count) for i in range(count)])


def per_device(gauge_links, pattern, link_parity, conv_weight, conv_bias, head_weight, cotangent):
    rows = gauge_links.reshape(72, 6, 2, 2, 128).transpose(0, 1, 3, 2, 4)
    next_x = shifted(rows[18:, :5, :, 0, :], "xy", -1)
    edge_z = jnp.concatenate([rows[:36, :5, 0], rows[54:, :5, 0]])
    next_z = shifted(edge_z, "gz", -1)
    shape = jax.ShapeDtypeStruct
    keep = jnp.asarray(np.concatenate(KEEP), BF16)
    spread = jnp.asarray(SPREAD, BF16)
    weights, small = call(
        weights_body, (shape((12, 128, 256), BF16), shape((64, 8), F32)), [],
        conv_weight.transpose(1, 2, 0), spread, keep, head_weight.T, conv_bias[None], name="weights",
    )
    half = shape((12, 16, 128), BF16)
    halo = pltpu.VMEM((54, 24, 128), F32)
    low_z, high_z = call(
        loops_body, (half, half),
        [halo, halo, pltpu.VMEM((12, 24, 128), F32), pltpu.VMEM((12, 2, 16, 128), F32)],
        rows.reshape(72, 24, 128), next_x, next_z, name="loops",
    )
    before_z = shifted(high_z, "gz", 1)
    after_z = shifted(low_z, "gz", -1)
    block = jnp.stack([before_z, low_z, high_z, after_z])
    before_x = shifted(block, "xy", 1)
    after_x = shifted(block, "xy", -1)
    x_first = (lax.axis_index("xy") * 2).reshape(1)
    z_first = (lax.axis_index("gz") * 4).reshape(1)
    coefficients, grads = call(
        layer_body, (shape((4, 2, 2, 256), F32), shape((64, 16, 128), BF16)),
        [pltpu.VMEM((12, 256, 1024), BF16), pltpu.VMEM((64, 1024), BF16), pltpu.VMEM((1024, 128), F32)],
        x_first, z_first, pattern, link_parity, before_x, block, after_x, weights, small, keep,
        cotangent, smem=4, name="layer",
    )
    both = ("xy", "gz")
    count = lax.axis_size(both)
    chunks = grads.reshape(count, 1024 // count, 128)
    chunks = lax.all_to_all(chunks, both, 0, 0, tiled=True)
    me = lax.axis_index(both).reshape(1)
    chunks = call(total_body, shape(chunks.shape, BF16), [], me, chunks, smem=1, name="total")
    chunks = lax.all_to_all(chunks, both, 0, 0, tiled=True)
    grad_kernel, grad_bias, grad_head = call(
        expand_body, (shape((48, 64, 81), F32), shape((1, 64), F32), shape((4, 64), F32)),
        [pltpu.VMEM((1024, 128), F32)], chunks.reshape(64, 16, 128), spread, name="expand",
    )
    return coefficients, grad_kernel.transpose(2, 0, 1), grad_bias.reshape(64), grad_head.T


def solution(mesh):
    return jax.shard_map(
        per_device,
        mesh=mesh,
        in_specs=(
            P(None, None, None, None, None, "xy", "gz"),
            P(),
            P(),
            P(),
            P(),
            P(),
            P(None, None, "xy", "gz"),
        ),
        out_specs=(P(None, None, "xy", "gz"), P(), P(), P()),
        check_vma=False,
    )
```

time: 126 us -> 107 us (0.85)
  waiting for transfers between devices: 31.5 us -> 21.2 us
  local copies, waits for them, and re-layouts: 12.9 us -> 6.41 us
  blocking collectives: 26.5 us -> 22.7 us
  starting transfers between devices: 28.6 us -> 32.2 us
    unnamed x24 -> x12, local copies, waits for them, and re-layouts: 7.95 us -> 2.13 us
    ppermute x6, waiting for transfers between devices: 11.4 us -> 5.96 us  [shifted(): return lax.ppermute(x, axis, [(i, (i + by) % count) for i in range(count)])]
    all_to_all x1, waiting for transfers between devices: 20.2 us -> 15.3 us  [per_device(): chunks = lax.all_to_all(chunks, both, 0, 0, tiled=True)]
    all_to_all x1, blocking collectives: 26.5 us -> 22.7 us  [per_device(): chunks = lax.all_to_all(chunks, both, 0, 0, tiled=True)]
    all_to_all x1, starting transfers between devices: 6.07 us -> 9.4 us  [per_device(): chunks = lax.all_to_all(chunks, both, 0, 0, tiled=True)]
  transfers between devices with their start and end apart: 7 -> 7, of which waited for: 6 -> 3; matrix products, arithmetic and copies ran while one was open for 4% -> 1% of each run, Pallas kernels for 3% -> 6%
where the time goes in v2:
time: 107 us
  starting transfers between devices  32.2 us (30%)
  blocking collectives  22.7 us (21%)
  Pallas kernels  22.5 us (21%)
  waiting for transfers between devices  21.2 us (20%)
  local copies, waits for them, and re-layouts  6.41 us (6%)
    ppermute x6, starting transfers between devices, shifted(): return lax.ppermute(x, axis, [(i, (i + by) % count) for i in range(count)])  22.8 us
    all_to_all x1, blocking collectives, per_device(): chunks = lax.all_to_all(chunks, both, 0, 0, tiled=True)  22.7 us
    pallas_call x5, Pallas kernels, call(): pl.pallas_call(body, out_shape=outs, in_specs=specs, out_specs=jax.tree.m...  22.5 us
    all_to_all x1, waiting for transfers between devices, per_device(): chunks = lax.all_to_all(chunks, both, 0, 0, tiled=True)  15.3 us
    all_to_all x1, starting transfers between devices, per_device(): chunks = lax.all_to_all(chunks, both, 0, 0, tiled=True)  9.4 us
    ppermute x6, waiting for transfers between devices, shifted(): return lax.ppermute(x, axis, [(i, (i + by) % count) for i in range(count)])  5.96 us
    reshape x2, local copies, waits for them, and re-layouts, per_device(): rows = gauge_links.reshape(72, 6, 2, 2, 128).transpose(0, 1, 3, 2, 4)  2.64 us
  transfers between devices with their start and end apart: 7, of which 3 were waited for; matrix products, arithmetic and copies ran while one was open for 1% of the time, Pallas kernels for 6%

profile of v2, /device:TPU:1, one launch (start us, length us, event | category | flops | bytes accessed | tf_op | source)
XLA Modules:
  0.0 106.8 jit_solution(8836388824259091333)
XLA Ops:
  0.6 2.2 %reshape.34 = f32[72,6,2,2,128]{4,3,2,1,0:T(2,128)S(1)} reshape(f32[4,2,3,3,6,2,256]{6,5,4,3,2,1,0:T(2,128)} %param.9) | data formatting | bytes 1769472 | tf_op jit(solution)/shard_map/reshape | solution.py:321
  2.8 0.5 copy.22
  3.3 0.1 pad_maximum_fusion
  3.5 3.3 %collective-permute-start.1 = (f32[54,5,2,128]{3,2,1,0:T(2,128)S(1)}, f32[54,5,2,128]{3,2,1,0:T(2,128)S(1)}, u32[]{:S(2)}, u32[]{:S(2)}) collective-permute-start(f32[54,5,2,128]{3,2,1,0:T(2,128)S(1)} %pad_maximum_fusion), channel_id=1, source_target_pairs={{0,3},{1,0},{2,1},{3,2},{4,7},{5,4},{6,5},{7,6},{8,11},{9,8},{10,9... | collective-permute-start | bytes 829448 | tf_op jit(solution)/shard_map/ppermute | solution.py:317
  6.8 0.2 slice.12
  7.0 0.1 copy.17
  7.2 8.7 %collective-permute-start = (f32[54,5,2,128]{3,2,1,0:T(2,128)S(1)}, f32[54,5,2,128]{3,2,1,0:T(2,128)S(1)}, u32[]{:S(2)}, u32[]{:S(2)}) collective-permute-start(f32[54,5,2,128]{3,2,1,0:T(2,128)S(1)} %copy.17), channel_id=1, source_target_pairs={{0,252},{4,0},{8,4},{12,8},{16,12},{20,16},{24,20},{28,24},{32,28}... | collective-permute-start | bytes 829448 | tf_op jit(solution)/shard_map/ppermute | solution.py:317
  15.9 0.2 copy.15
  16.1 1.1 %copy.18.l_ref = f32[72,24,128]{2,1,0:T(8,128)} copy(f32[72,24,128]{2,0,1:T(8,128)S(1)} %bitcast.28) | data formatting | bytes 1769472 | tf_op jit(solution)/shard_map/reshape | solution.py:337
  17.1 0.0 collective-permute-done.1.zh_ref
  17.1 4.0 %collective-permute-done.xh_ref = f32[54,5,2,128]{3,2,1,0:T(2,128)S(1)} collective-permute-done((f32[54,5,2,128]{3,2,1,0:T(2,128)S(1)}, f32[54,5,2,128]{3,2,1,0:T(2,128)S(1)}, u32[]{:S(2)}, u32[]{:S(2)}) %collective-permute-start) | collective-permute-done | bytes 276512 | tf_op jit(solution)/shard_map/ppermute | solution.py:317
  21.1 0.7 copy-done.3
  21.8 3.7 %loops.1 = (bf16[12,16,128]{2,1,0:T(8,128)(2,1)}, bf16[12,16,128]{2,1,0:T(8,128)(2,1)}) custom-call(f32[72,24,128]{2,1,0:T(8,128)} %copy.18.l_ref, f32[54,5,2,128]{3,2,1,0:T(2,128)} %copy-done.3, f32[54,5,2,128]{3,2,1,0:T(2,128)} %copy-done.2), custom_call_target="tpu_custom_call" | custom-call | tf_op jit(solution)/shard_map/loops/pallas_call | solution.py:303
  25.5 1.6 %collective-permute-start.3 = (bf16[12,16,128]{2,1,0:T(8,128)(2,1)}, bf16[12,16,128]{2,1,0:T(8,128)(2,1)S(1)}, u32[]{:S(2)}, u32[]{:S(2)}) collective-permute-start(bf16[12,16,128]{2,1,0:T(8,128)(2,1)} %get-tuple-element.14), channel_id=1, source_target_pairs={{0,3},{1,0},{2,1},{3,2},{4,7},{5,4},{6,5},{7,6},{8,11},{9,8},{10,9... | collective-permute-start | bytes 147464 | tf_op jit(solution)/shard_map/ppermute | solution.py:317
  27.1 0.3 collective-permute-start.2
  27.4 2.0 %collective-permute-done.3 = bf16[12,16,128]{2,1,0:T(8,128)(2,1)S(1)} collective-permute-done((bf16[12,16,128]{2,1,0:T(8,128)(2,1)}, bf16[12,16,128]{2,1,0:T(8,128)(2,1)S(1)}, u32[]{:S(2)}, u32[]{:S(2)}) %collective-permute-start.3) | collective-permute-done | bytes 49184 | tf_op jit(solution)/shard_map/ppermute | solution.py:317
  29.4 0.0 collective-permute-done.2
  29.4 0.8 pad_maximum_fusion.1.e_ref
  30.3 0.1 collective-permute-start.4
  30.4 8.8 %collective-permute-start.5 = (bf16[4,12,16,128]{3,2,1,0:T(8,128)(2,1)S(1)}, bf16[4,12,16,128]{3,2,1,0:T(8,128)(2,1)S(1)}, u32[]{:S(2)}, u32[]{:S(2)}) collective-permute-start(bf16[4,12,16,128]{3,2,1,0:T(8,128)(2,1)S(1)} %pad_maximum_fusion.1.e_ref), channel_id=1, source_target_pairs={{0,252},{4,0},{8,4},{12,8},{16,12},{20,16},{24,20},{28,24},{32,28}... | collective-permute-start | bytes 589832 | tf_op jit(solution)/shard_map/ppermute | solution.py:317
  39.1 5.9 %weights.1 = (bf16[12,128,256]{2,1,0:T(8,128)(2,1)}, f32[64,8]{1,0:T(8,128)}) custom-call(bf16[48,64,81]{2,1,0:T(8,128)(2,1)} %bitcast.34, bf16[6,144,512]{2,1,0:T(8,128)(2,1)} %constant.18.clone.spread_ref, bf16[1168,256]{1,0:T(8,128)(2,1)} %constant.17.clone.keep_ref, f32[4,64]{1,0:T(4,128)} %bitcast.40, f32[1,64]{1,0:T(1,128)} %bitcast.41), custom_call_target="tpu_custom_call" | custom-call | tf_op jit(solution)/shard_map/weights/pallas_call | solution.py:303
  45.1 0.0 collective-permute-done.4.el_ref
  45.1 0.0 collective-permute-done.5.er_ref
  45.1 0.6 copy-done.4
  45.7 0.1 copy-done.5
  45.8 8.0 %layer.1 = (f32[4,2,2,256]{3,2,1,0:T(2,128)}, bf16[64,16,128]{2,1,0:T(8,128)(2,1)}) custom-call(s32[1]{0:T(128)} %bitcast.x0_ref, s32[1]{0:T(128)} %bitcast.1.z0_ref, s32[4,4]{1,0:T(4,128)} %pat_ref.1, s32[4]{0:T(128)} %par_ref.1, bf16[4,12,16,128]{3,2,1,0:T(8,128)(2,1)} %copy-done.4, bf16[4,12,16,128]{3,2,1,0:T(8,128)(2,1)} %copy-done.1, ...), custom_call_target="tpu_custom_call" | custom-call | tf_op jit(solution)/shard_map/layer/pallas_call | solution.py:303
  53.8 9.4 %all-to-all-start = ((bf16[256,4,128]{2,1,0:T(4,128)(2,1)}), bf16[256,4,128]{2,1,0:T(4,128)(2,1)S(1)}, u32[]{:S(2)}, u32[]{:S(2)}) async-start(bf16[256,4,128]{2,1,0:T(4,128)(2,1)} %bitcast.35), calls=%async_computation | async-start | bytes 524288 | tf_op jit(solution)/shard_map/all_to_all | solution.py:355
  63.2 15.3 %all-to-all-done.in_ref = bf16[256,4,128]{2,1,0:T(4,128)(2,1)S(1)} async-done(((bf16[256,4,128]{2,1,0:T(4,128)(2,1)}), bf16[256,4,128]{2,1,0:T(4,128)(2,1)S(1)}, u32[]{:S(2)}, u32[]{:S(2)}) %all-to-all-start) | async-done | bytes 262176 | tf_op jit(solution)/shard_map/all_to_all | solution.py:355
  78.5 0.7 copy-done
  79.2 2.1 %total.1 = bf16[256,4,128]{2,1,0:T(4,128)(2,1)} custom-call(s32[1]{0:T(128)} %bitcast.15.me_ref, bf16[256,4,128]{2,1,0:T(4,128)(2,1)} %copy-done), custom_call_target="tpu_custom_call" | custom-call | tf_op jit(solution)/shard_map/total/pallas_call | solution.py:303
  81.3 22.7 %all_to_all.10 = bf16[256,4,128]{2,1,0:T(4,128)(2,1)} all-to-all(bf16[256,4,128]{2,1,0:T(4,128)(2,1)} %total.1), channel_id=1, replica_groups=mesh['xy'=64,'gz'=4] {'xy','gz'}, dimensions={0} | all-to-all | bytes 524288 | tf_op jit(solution)/shard_map/all_to_all | solution.py:358
  104.0 2.8 %expand.1 = (f32[48,64,81]{2,1,0:T(8,128)}, f32[1,64]{1,0:T(1,128)}, f32[4,64]{1,0:T(4,128)}) custom-call(bf16[64,16,128]{2,1,0:T(8,128)(2,1)} %bitcast.33, bf16[6,144,512]{2,1,0:T(8,128)(2,1)} %constant.18.clone.spread_ref), custom_call_target="tpu_custom_call" | custom-call | tf_op jit(solution)/shard_map/expand/pallas_call | solution.py:303
  (11 shorter events, 0.1 us)
Async XLA Ops:
  3.5 13.7 %collective-permute-start.1 = (f32[54,5,2,128]{3,2,1,0:T(2,128)S(1)}, f32[54,5,2,128]{3,2,1,0:T(2,128)S(1)}, u32[]{:S(2)}, u32[]{:S(2)}) collective-permute-start(f32[54,5,2,128]{3,2,1,0:T(2,128)S(1)} %pad_maximum_fusion), channel_id=1, source_target_pairs={{0,3},{1,0},{2,1},{3,2},{4,7},{5,4},{6,5},{7,6},{8,11},{9,8},{10,9... | collective-permute-start | bytes 829448 | tf_op jit(solution)/shard_map/ppermute | solution.py:317
  7.2 14.0 %collective-permute-start = (f32[54,5,2,128]{3,2,1,0:T(2,128)S(1)}, f32[54,5,2,128]{3,2,1,0:T(2,128)S(1)}, u32[]{:S(2)}, u32[]{:S(2)}) collective-permute-start(f32[54,5,2,128]{3,2,1,0:T(2,128)S(1)} %copy.17), channel_id=1, source_target_pairs={{0,252},{4,0},{8,4},{12,8},{16,12},{20,16},{24,20},{28,24},{32,28}... | collective-permute-start | bytes 829448 | tf_op jit(solution)/shard_map/ppermute | solution.py:317
  17.1 4.0 %copy-start.2 = (f32[54,5,2,128]{3,2,1,0:T(2,128)}, f32[54,5,2,128]{3,2,1,0:T(2,128)S(1)}, u32[]{:S(2)}) copy-start(f32[54,5,2,128]{3,2,1,0:T(2,128)S(1)} %collective-permute-done.1.zh_ref) | copy-start | bytes 829444
  21.1 0.7 copy-start.3
  25.5 3.9 %collective-permute-start.3 = (bf16[12,16,128]{2,1,0:T(8,128)(2,1)}, bf16[12,16,128]{2,1,0:T(8,128)(2,1)S(1)}, u32[]{:S(2)}, u32[]{:S(2)}) collective-permute-start(bf16[12,16,128]{2,1,0:T(8,128)(2,1)} %get-tuple-element.14), channel_id=1, source_target_pairs={{0,3},{1,0},{2,1},{3,2},{4,7},{5,4},{6,5},{7,6},{8,11},{9,8},{10,9... | collective-permute-start | bytes 147464 | tf_op jit(solution)/shard_map/ppermute | solution.py:317
  27.1 2.3 %collective-permute-start.2 = (bf16[12,16,128]{2,1,0:T(8,128)(2,1)}, bf16[12,16,128]{2,1,0:T(8,128)(2,1)S(1)}, u32[]{:S(2)}, u32[]{:S(2)}) collective-permute-start(bf16[12,16,128]{2,1,0:T(8,128)(2,1)} %get-tuple-element.13), channel_id=1, source_target_pairs={{0,1},{1,2},{2,3},{3,0},{4,5},{5,6},{6,7},{7,4},{8,9},{9,10},{10,1... | collective-permute-start | bytes 147464 | tf_op jit(solution)/shard_map/ppermute | solution.py:317
  30.3 14.8 %copy-start.1 = (bf16[4,12,16,128]{3,2,1,0:T(8,128)(2,1)}, bf16[4,12,16,128]{3,2,1,0:T(8,128)(2,1)S(1)}, u32[]{:S(2)}) copy-start(bf16[4,12,16,128]{3,2,1,0:T(8,128)(2,1)S(1)} %pad_maximum_fusion.1.e_ref) | copy-start | bytes 589828
  30.3 14.8 %collective-permute-start.4 = (bf16[4,12,16,128]{3,2,1,0:T(8,128)(2,1)S(1)}, bf16[4,12,16,128]{3,2,1,0:T(8,128)(2,1)S(1)}, u32[]{:S(2)}, u32[]{:S(2)}) collective-permute-start(bf16[4,12,16,128]{3,2,1,0:T(8,128)(2,1)S(1)} %pad_maximum_fusion.1.e_ref), channel_id=1, source_target_pairs={{0,4},{4,8},{8,12},{12,16},{16,20},{20,24},{24,28},{28,32},{32,36}... | collective-permute-start | bytes 589832 | tf_op jit(solution)/shard_map/ppermute | solution.py:317
  30.4 14.7 %collective-permute-start.5 = (bf16[4,12,16,128]{3,2,1,0:T(8,128)(2,1)S(1)}, bf16[4,12,16,128]{3,2,1,0:T(8,128)(2,1)S(1)}, u32[]{:S(2)}, u32[]{:S(2)}) collective-permute-start(bf16[4,12,16,128]{3,2,1,0:T(8,128)(2,1)S(1)} %pad_maximum_fusion.1.e_ref), channel_id=1, source_target_pairs={{0,252},{4,0},{8,4},{12,8},{16,12},{20,16},{24,20},{28,24},{32,28}... | collective-permute-start | bytes 589832 | tf_op jit(solution)/shard_map/ppermute | solution.py:317
  45.1 0.7 copy-start.4
  45.1 0.7 copy-start.5
  53.8 24.7 %all-to-all-start = ((bf16[256,4,128]{2,1,0:T(4,128)(2,1)}), bf16[256,4,128]{2,1,0:T(4,128)(2,1)S(1)}, u32[]{:S(2)}, u32[]{:S(2)}) async-start(bf16[256,4,128]{2,1,0:T(4,128)(2,1)} %bitcast.35), calls=%async_computation | async-start | bytes 524288 | tf_op jit(solution)/shard_map/all_to_all | solution.py:355
  78.5 0.7 copy-start

commit v3 on v2

--- a/solution.py
+++ b/solution.py
@@ -1,3 +1,4 @@
+import functools
 import math
 
 import jax
@@ -60,8 +61,8 @@
 NT = (((1,), (1,)), ((), ()))
 
 
-def weights_body(w_ref, spread_ref, keep_ref, head_ref, bias_ref, out_ref, small_ref):
-    for p in range(6):
+def weights_body(planes, w_ref, spread_ref, keep_ref, head_ref, bias_ref, out_ref, small_ref):
+    for p in planes:
         table = keep_ref[STARTS[p] : STARTS[p] + SIZES[p], :]
         for r in range(2):
             full = jnp.zeros((64, 144), F32)
@@ -73,48 +74,87 @@
             high = full.astype(BF16)
             low = (full - high.astype(F32)).astype(BF16)
             both = jnp.concatenate([high, low], axis=0)
-            out_ref[2 * p + r, :, 0 : SIZES[p]] = lax.dot_general(
+            out_ref[2 * (p - planes[0]) + r, :, 0 : SIZES[p]] = lax.dot_general(
                 both, table[:, :144], NT, preferred_element_type=F32
             ).astype(BF16)
     small_ref[...] = jnp.concatenate([head_ref[...], bias_ref[...], jnp.zeros((3, 64), F32)], axis=0).T
 
 
-def loops_body(l_ref, xh_ref, zh_ref, o0_ref, o1_ref, xs_ref, zs_ref, pq_ref, tile_ref):
+def run(copies):
+    for copy in copies:
+        copy.start()
+    for copy in copies:
+        copy.wait()
+
+
+def send_body(l_ref, x_ref, z_ref, sems):
+    z_part = l_ref.at[:, :, :, :, 0:5, :, 0:128]
+    run([
+        pltpu.make_async_copy(l_ref.at[1:4, :, :, :, 0:5, 0:1, :], x_ref, sems.at[0]),
+        pltpu.make_async_copy(z_part.at[0:2], z_ref.at[0:2], sems.at[1]),
+        pltpu.make_async_copy(z_part.at[3:4], z_ref.at[2:3], sems.at[2]),
+    ])
+
+
+def loops_body(
+    links_ref, x_any, z_any, o0_ref, o1_ref, l_ref, xh_ref, zh_ref, xs_ref, zs_ref, pq_ref, tile_ref, sems
+):
+    copies = [
+        pltpu.make_async_copy(x_any, xh_ref, sems.at[12]),
+        pltpu.make_async_copy(z_any, zh_ref, sems.at[13]),
+    ]
+    for tau in range(6):
+        for lb in range(2):
+            at = tau * 4 + lb * 2
+            copies.append(
+                pltpu.make_async_copy(
+                    links_ref.at[:, :, :, :, tau, :, lb * 128 : lb * 128 + 128],
+                    l_ref.at[:, :, :, :, at : at + 2, :],
+                    sems.at[tau * 2 + lb],
+                )
+            )
+    run(copies)
+
     def stage(c, carry):
-        for tau in range(5):
-            xs_ref[c, pl.ds(4 * tau + 1, 2, stride=2), :] = xh_ref[c, tau]
-            zs_ref[c, 4 * tau + 2 : 4 * tau + 4, :] = zh_ref[c, tau]
+        d, ri = lax.div(c, 6), lax.rem(c, 6)
+        ri, i = lax.div(ri, 3), lax.rem(ri, 3)
+        for j in range(3):
+            for tau in range(5):
+                for lb in range(2):
+                    row = 4 * tau + 2 * lb + 1
+                    xs_ref[d, ri, i, j, row : row + 1, :] = xh_ref[
+                        d, ri, i, j, tau, :, lb * 128 : lb * 128 + 128
+                    ]
+                zs_ref[d, ri, i, j, 4 * tau + 2 : 4 * tau + 4, :] = zh_ref[d, ri, i, j, tau]
         return carry
 
-    lax.fori_loop(0, 54, stage, 0)
+    lax.fori_loop(0, 18, stage, 0)
     row = lax.broadcasted_iota(jnp.int32, (8, 128), 0)
     odd_x = row % 2 == 1
     high_z = row % 4 >= 2
     upper = lanes((8, 128)) >= LY
 
-    def comp(d, ri, i, j):
-        return ((d * 2 + ri) * 3 + i) * 3 + j
-
     def at_site(d, k):
+        part = slice(8 * k, 8 * k + 8)
         return [
-            [[l_ref[comp(d, ri, i, j), 8 * k : 8 * k + 8, :] for j in range(3)] for i in range(3)]
-            for ri in range(2)
+            [[l_ref[d, ri, i, j, part, :] for j in range(3)] for i in range(3)] for ri in range(2)
         ]
 
     def ahead(d, step, k):
+        part = slice(8 * k, 8 * k + 8)
+
         def one(ri, i, j):
-            c = comp(d, ri, i, j)
             if step == 3:
                 if k < 2:
-                    return l_ref[c, 8 * k + 4 : 8 * k + 12, :]
-                return pltpu.roll(l_ref[c, 16:24, :], 4, 0)
-            own = l_ref[c, 8 * k : 8 * k + 8, :]
+                    return l_ref[d, ri, i, j, 8 * k + 4 : 8 * k + 12, :]
+                return pltpu.roll(l_ref[d, ri, i, j, 16:24, :], 4, 0)
+            own = l_ref[d, ri, i, j, part, :]
             if step == 0:
-                return jnp.where(odd_x, xs_ref[c - 18, 8 * k : 8 * k + 8, :], pltpu.roll(own, 7, 0))
+                return jnp.where(odd_x, xs_ref[d - 1, ri, i, j, part, :], pltpu.roll(own, 7, 0))
             if step == 1:
                 return shift_y(own, 1)
-            h = c if d < 2 else c - 18
-            beyond = jnp.where(high_z, zs_ref[h, 8 * k : 8 * k + 8, :], pltpu.roll(own, 6, 0))
+            edge = zs_ref[min(d, 2), ri, i, j, part, :]
+            beyond = jnp.where(high_z, edge, pltpu.roll(own, 6, 0))
             return pltpu.roll(jnp.where(upper, own, beyond), LY, 1)
 
         return [[[one(ri, i, j) for j in range(3)] for i in range(3)] for ri in range(2)]
@@ -155,9 +195,22 @@
 
 
 def layer_body(
-    x0_ref, z0_ref, pat_ref, par_ref, el_ref, e_ref, er_ref, w_ref, small_ref, keep_ref, cot_ref,
-    coef_ref, g_ref, a_ref, low_ref, rows_ref,
+    x0_ref, z0_ref, pat_ref, par_ref, el_any, e_any, er_any, w0_any, w1_any, keep_any, small_ref, cot_ref,
+    coef_ref, g_ref, el_ref, e_ref, er_ref, w_ref, keep_ref, a_ref, low_ref, rows_ref, sems,
 ):
+    halo = [
+        pltpu.make_async_copy(src, dst, sems.at[i])
+        for i, (src, dst) in enumerate(((el_any, el_ref), (e_any, e_ref), (er_any, er_ref)))
+    ]
+    later = [
+        pltpu.make_async_copy(w0_any, w_ref.at[0:6], sems.at[3]),
+        pltpu.make_async_copy(w1_any, w_ref.at[6:12], sems.at[4]),
+        pltpu.make_async_copy(keep_any, keep_ref, sems.at[5]),
+    ]
+    for copy in halo + later:
+        copy.start()
+    for copy in halo:
+        copy.wait()
     first = lax.broadcasted_iota(jnp.int32, (8, 128), 0) < 4
     lane = lanes((8, 128))
     upper = lane >= LY
@@ -209,6 +262,8 @@
                                     col = (t * 4 + x * 2 + lb) * 128
                                     a_ref[c, 16 * n : 16 * n + 16, col : col + 128] = both[z + 2 * lb]
 
+    for copy in later:
+        copy.wait()
     lane = lanes((1, 256))
     y_pos = lane % LY
     z_pos = z0_ref[0] + lane // LY
@@ -276,35 +331,44 @@
     out_ref[...] = jnp.broadcast_to(total.astype(BF16)[None], out_ref.shape)
 
 
-def expand_body(g_ref, spread_ref, k_ref, b_ref, h_ref, rows_ref):
+def expand_body(g_ref, spread_ref, k_any, b_ref, h_ref, rows_ref, k_ref, sems):
     rows_ref[...] = g_ref[...].astype(F32).reshape(1024, 128)
 
     def get(j):
         return rows_ref[pl.ds(j, 64, stride=16), :]
 
     ends = [get(12), get(13)]
-    for c in range(12):
-        p, r = c // 2, c % 2
-        end = ends[c // 8]
-        end = pltpu.roll(end, 128 - 16 * (c % 8), 1) if c % 8 else end
-        kept = jnp.concatenate([get(c), end[:, :16]], axis=1).astype(BF16)
-        full = jnp.dot(kept, spread_ref[p], preferred_element_type=F32)
-        for leaf in range(4):
-            k_ref[8 * p + 2 * leaf + r] = full[:, leaf * 128 : leaf * 128 + 81]
+    copies = []
+    for p in range(6):
+        for r in range(2):
+            c = 2 * p + r
+            end = ends[c // 8]
+            end = pltpu.roll(end, 128 - 16 * (c % 8), 1) if c % 8 else end
+            kept = jnp.concatenate([get(c), end[:, :16]], axis=1).astype(BF16)
+            full = jnp.dot(kept, spread_ref[p], preferred_element_type=F32)
+            for leaf in range(4):
+                k_ref[8 * p + 2 * leaf + r] = full[:, leaf * 128 : leaf * 128 + 81]
+        part = slice(8 * p, 8 * p + 8)
+        copies.append(pltpu.make_async_copy(k_ref.at[part], k_any.at[part], sems.at[p]))
+        copies[-1].start()
     small = get(14)
     small = (small + pltpu.roll(small, 120, 1)).T
     h_ref[...] = small[0:4]
     b_ref[...] = small[4:5]
-
-
-def call(body, outs, scratch, *args, smem=0, name):
-    vmem = pl.BlockSpec(memory_space=pltpu.VMEM)
-    specs = [pl.BlockSpec(memory_space=pltpu.SMEM)] * smem + [vmem] * (len(args) - smem)
+    for copy in copies:
+        copy.wait()
+
+
+def call(body, outs, scratch, *args, smem=0, away=(), outs_away=(), name):
+    def spec(i, away):
+        return pl.BlockSpec(memory_space=pl.ANY if i in away else pltpu.VMEM)
+
+    specs = [pl.BlockSpec(memory_space=pltpu.SMEM)] * smem
     return pl.pallas_call(
         body,
         out_shape=outs,
-        in_specs=specs,
-        out_specs=jax.tree.map(lambda _: vmem, outs),
+        in_specs=specs + [spec(i, away) for i in range(smem, len(args))],
+        out_specs=tuple(spec(i, outs_away) for i in range(len(outs))),
         scratch_shapes=scratch,
         compiler_params=PARAMS,
         interpret=INTERPRET,
@@ -318,23 +382,32 @@
 
 
 def per_device(gauge_links, pattern, link_parity, conv_weight, conv_bias, head_weight, cotangent):
-    rows = gauge_links.reshape(72, 6, 2, 2, 128).transpose(0, 1, 3, 2, 4)
-    next_x = shifted(rows[18:, :5, :, 0, :], "xy", -1)
-    edge_z = jnp.concatenate([rows[:36, :5, 0], rows[54:, :5, 0]])
-    next_z = shifted(edge_z, "gz", -1)
     shape = jax.ShapeDtypeStruct
+    sems = pltpu.SemaphoreType.DMA
+    x_edge, z_edge = call(
+        send_body, (shape((3, 2, 3, 3, 5, 1, 256), F32), shape((3, 2, 3, 3, 5, 2, 128), F32)), [sems((3,))],
+        gauge_links, away=(0,), outs_away=(0, 1), name="send",
+    )
+    next_x = shifted(x_edge, "xy", -1)
+    next_z = shifted(z_edge, "gz", -1)
     keep = jnp.asarray(np.concatenate(KEEP), BF16)
     spread = jnp.asarray(SPREAD, BF16)
-    weights, small = call(
-        weights_body, (shape((12, 128, 256), BF16), shape((64, 8), F32)), [],
-        conv_weight.transpose(1, 2, 0), spread, keep, head_weight.T, conv_bias[None], name="weights",
-    )
+    weights = []
+    for planes in ((0, 1, 2), (3, 4, 5)):
+        weights.append(call(
+            functools.partial(weights_body, planes), (shape((6, 128, 256), BF16), shape((64, 8), F32)), [],
+            conv_weight.transpose(1, 2, 0), spread, keep, head_weight.T, conv_bias[None], name="weights",
+        ))
+    next_x, next_z, weights[0] = lax.optimization_barrier((next_x, next_z, weights[0]))
     half = shape((12, 16, 128), BF16)
-    halo = pltpu.VMEM((54, 24, 128), F32)
+    halo = pltpu.VMEM((3, 2, 3, 3, 24, 128), F32)
     low_z, high_z = call(
         loops_body, (half, half),
-        [halo, halo, pltpu.VMEM((12, 24, 128), F32), pltpu.VMEM((12, 2, 16, 128), F32)],
-        rows.reshape(72, 24, 128), next_x, next_z, name="loops",
+        [
+            pltpu.VMEM((4, 2, 3, 3, 24, 128), F32), pltpu.VMEM(next_x.shape, F32), pltpu.VMEM(next_z.shape, F32),
+            halo, halo, pltpu.VMEM((12, 24, 128), F32), pltpu.VMEM((12, 2, 16, 128), F32), sems((14,)),
+        ],
+        gauge_links, next_x, next_z, away=(0, 1, 2), name="loops",
     )
     before_z = shifted(high_z, "gz", 1)
     after_z = shifted(low_z, "gz", -1)
@@ -345,20 +418,25 @@
     z_first = (lax.axis_index("gz") * 4).reshape(1)
     coefficients, grads = call(
         layer_body, (shape((4, 2, 2, 256), F32), shape((64, 16, 128), BF16)),
-        [pltpu.VMEM((12, 256, 1024), BF16), pltpu.VMEM((64, 1024), BF16), pltpu.VMEM((1024, 128), F32)],
-        x_first, z_first, pattern, link_parity, before_x, block, after_x, weights, small, keep,
-        cotangent, smem=4, name="layer",
+        [pltpu.VMEM(block.shape, BF16)] * 3
+        + [
+            pltpu.VMEM((12, 128, 256), BF16), pltpu.VMEM(keep.shape, BF16), pltpu.VMEM((12, 256, 1024), BF16),
+            pltpu.VMEM((64, 1024), BF16), pltpu.VMEM((1024, 128), F32), sems((6,)),
+        ],
+        x_first, z_first, pattern, link_parity, before_x, block, after_x, weights[0][0], weights[1][0], keep,
+        weights[0][1], cotangent, smem=4, away=range(4, 10), name="layer",
     )
     both = ("xy", "gz")
     count = lax.axis_size(both)
     chunks = grads.reshape(count, 1024 // count, 128)
     chunks = lax.all_to_all(chunks, both, 0, 0, tiled=True)
     me = lax.axis_index(both).reshape(1)
-    chunks = call(total_body, shape(chunks.shape, BF16), [], me, chunks, smem=1, name="total")
+    chunks = call(total_body, (shape(chunks.shape, BF16),), [], me, chunks, smem=1, name="total")[0]
     chunks = lax.all_to_all(chunks, both, 0, 0, tiled=True)
     grad_kernel, grad_bias, grad_head = call(
         expand_body, (shape((48, 64, 81), F32), shape((1, 64), F32), shape((4, 64), F32)),
-        [pltpu.VMEM((1024, 128), F32)], chunks.reshape(64, 16, 128), spread, name="expand",
+        [pltpu.VMEM((1024, 128), F32), pltpu.VMEM((48, 64, 81), F32), sems((6,))],
+        chunks.reshape(64, 16, 128), spread, outs_away=(0,), name="expand",
     )
     return coefficients, grad_kernel.transpose(2, 0, 1), grad_bias.reshape(64), grad_head.T
 

time: 107 us -> 128 us (1.20)
  Pallas kernels: 22.5 us -> 44.7 us
  waiting for transfers between devices: 21.2 us -> 28.9 us
  starting transfers between devices: 32.2 us -> 27.8 us
  local copies, waits for them, and re-layouts: 6.41 us -> 2.09 us
    pallas_call x5 -> x7, Pallas kernels: 22.5 us -> 44.7 us  [call(): pl.pallas_call(body, out_shape=outs, in_specs=specs + [spec(i, away) for...]
    ppermute x6, waiting for transfers between devices: 5.96 us -> 13.2 us  [shifted(): return lax.ppermute(x, axis, [(i, (i + by) % count) for i in range(count)])]
    all_to_all x1, starting transfers between devices: 9.4 us -> 5.58 us  [per_device(): chunks = lax.all_to_all(chunks, both, 0, 0, tiled=True)]
    reshape x3 -> x0, local copies, waits for them, and re-layouts: 3.71 us -> none  [the longest x2 2.64 us: per_device(): rows = gauge_links.reshape(72, 6, 2, 2, 128).transpose(0, 1, 3, 2, 4)]
  transfers between devices with their start and end apart: 7 -> 7, of which waited for: 3 -> 7; matrix products, arithmetic and copies ran while one was open for 1% -> 0% of each run, Pallas kernels for 6% -> 6%
where the time goes in v3:
time: 128 us
  Pallas kernels  44.7 us (35%)
  waiting for transfers between devices  28.9 us (23%)
  starting transfers between devices  27.8 us (22%)
  blocking collectives  22.4 us (18%)
  local copies, waits for them, and re-layouts  2.09 us (2%)
    pallas_call x7, Pallas kernels, call(): pl.pallas_call(body, out_shape=outs, in_specs=specs + [spec(i, away) for...  44.7 us
    all_to_all x1, blocking collectives, per_device(): chunks = lax.all_to_all(chunks, both, 0, 0, tiled=True)  22.4 us
    ppermute x6, starting transfers between devices, shifted(): return lax.ppermute(x, axis, [(i, (i + by) % count) for i in range(count)])  22.2 us
    all_to_all x1, waiting for transfers between devices, per_device(): chunks = lax.all_to_all(chunks, both, 0, 0, tiled=True)  15.7 us
    ppermute x6, waiting for transfers between devices, shifted(): return lax.ppermute(x, axis, [(i, (i + by) % count) for i in range(count)])  13.2 us
    all_to_all x1, starting transfers between devices, per_device(): chunks = lax.all_to_all(chunks, both, 0, 0, tiled=True)  5.58 us
  transfers between devices with their start and end apart: 7, of which 7 were waited for; matrix products, arithmetic and copies ran while one was open for 0% of the time, Pallas kernels for 6%

profile of v3, /device:TPU:1, one launch (start us, length us, event | category | flops | bytes accessed | tf_op | source)
XLA Modules:
  0.0 127.6 jit_solution(2373157615334574903)
XLA Ops:
  0.6 17.9 %send.1 = (f32[3,2,3,3,5,1,256]{6,5,4,3,2,1,0:T(1,128)}, f32[3,2,3,3,5,2,128]{6,5,4,3,2,1,0:T(2,128)}) custom-call(f32[4,2,3,3,6,2,256]{6,5,4,3,2,1,0:T(2,128)} %links_ref.1), custom_call_target="tpu_custom_call" | custom-call | tf_op jit(solution)/shard_map/send/pallas_call | solution.py:367
  18.5 11.3 %collective-permute-start = (f32[3,2,3,3,5,1,256]{6,5,4,3,2,1,0:T(1,128)}, f32[3,2,3,3,5,1,256]{6,5,4,3,2,1,0:T(1,128)S(1)}, u32[]{:S(2)}, u32[]{:S(2)}) collective-permute-start(f32[3,2,3,3,5,1,256]{6,5,4,3,2,1,0:T(1,128)} %get-tuple-element.20), channel_id=1, source_target_pairs={{0,252},{4,0},{8,4},{12,8},{16,12},{20,16},{24,20},{28,24},{32,28}... | collective-permute-start | bytes 829448 | tf_op jit(solution)/shard_map/ppermute | solution.py:381
  29.8 1.0 collective-permute-start.1
  30.8 4.1 %weights.2 = (bf16[6,128,256]{2,1,0:T(8,128)(2,1)}, f32[64,8]{1,0:T(8,128)}) custom-call(bf16[48,64,81]{2,1,0:T(8,128)(2,1)} %bitcast.15, bf16[6,144,512]{2,1,0:T(8,128)(2,1)} %constant.18.clone.spread_ref, bf16[1168,256]{1,0:T(8,128)(2,1)} %constant.17.clone.keep_ref.keep_any, f32[4,64]{1,0:T(4,128)} %bitcast.23, f32[1,64]{1,0:T(1,128)} %bitcast.25), custom_call_target="tpu_custom_call" | custom-call | tf_op jit(solution)/shard_map/weights/pallas_call | solution.py:367
  34.9 0.5 collective-permute-done.x_any
  35.4 0.0 copy-start.2
  35.4 0.6 collective-permute-done.1.z_any
  36.0 0.0 copy-start.3
  36.0 0.1 copy-done.2
  36.1 0.6 copy-done.3
  36.7 4.2 %loops.1 = (bf16[12,16,128]{2,1,0:T(8,128)(2,1)}, bf16[12,16,128]{2,1,0:T(8,128)(2,1)}) custom-call(f32[4,2,3,3,6,2,256]{6,5,4,3,2,1,0:T(2,128)} %links_ref.1, f32[3,2,3,3,5,1,256]{6,5,4,3,2,1,0:T(1,128)} %copy-done.2, f32[3,2,3,3,5,2,128]{6,5,4,3,2,1,0:T(2,128)} %copy-done.3), custom_call_target="tpu_custom_call" | custom-call | tf_op jit(solution)/shard_map/loops/pallas_call | solution.py:367
  40.9 1.4 %collective-permute-start.2 = (bf16[12,16,128]{2,1,0:T(8,128)(2,1)}, bf16[12,16,128]{2,1,0:T(8,128)(2,1)S(1)}, u32[]{:S(2)}, u32[]{:S(2)}) collective-permute-start(bf16[12,16,128]{2,1,0:T(8,128)(2,1)} %get-tuple-element.26), channel_id=1, source_target_pairs={{0,1},{1,2},{2,3},{3,0},{4,5},{5,6},{6,7},{7,4},{8,9},{9,10},{10,1... | collective-permute-start | bytes 147464 | tf_op jit(solution)/shard_map/ppermute | solution.py:381
  42.3 0.0 collective-permute-start.3
  42.3 1.5 %collective-permute-done.2 = bf16[12,16,128]{2,1,0:T(8,128)(2,1)S(1)} collective-permute-done((bf16[12,16,128]{2,1,0:T(8,128)(2,1)}, bf16[12,16,128]{2,1,0:T(8,128)(2,1)S(1)}, u32[]{:S(2)}, u32[]{:S(2)}) %collective-permute-start.2) | collective-permute-done | bytes 49184 | tf_op jit(solution)/shard_map/ppermute | solution.py:381
  43.8 2.2 %collective-permute-done.3 = bf16[12,16,128]{2,1,0:T(8,128)(2,1)S(1)} collective-permute-done((bf16[12,16,128]{2,1,0:T(8,128)(2,1)}, bf16[12,16,128]{2,1,0:T(8,128)(2,1)S(1)}, u32[]{:S(2)}, u32[]{:S(2)}) %collective-permute-start.3) | collective-permute-done | bytes 49184 | tf_op jit(solution)/shard_map/ppermute | solution.py:381
  46.1 0.8 pad_maximum_fusion.e_any
  46.9 0.0 copy-start.1
  46.9 8.5 %collective-permute-start.5 = (bf16[4,12,16,128]{3,2,1,0:T(8,128)(2,1)S(1)}, bf16[4,12,16,128]{3,2,1,0:T(8,128)(2,1)S(1)}, u32[]{:S(2)}, u32[]{:S(2)}) collective-permute-start(bf16[4,12,16,128]{3,2,1,0:T(8,128)(2,1)S(1)} %pad_maximum_fusion.e_any), channel_id=1, source_target_pairs={{0,252},{4,0},{8,4},{12,8},{16,12},{20,16},{24,20},{28,24},{32,28}... | collective-permute-start | bytes 589832 | tf_op jit(solution)/shard_map/ppermute | solution.py:381
  55.4 0.0 collective-permute-start.4
  55.4 4.1 %weights.3 = (bf16[6,128,256]{2,1,0:T(8,128)(2,1)}, f32[64,8]{1,0:T(8,128)}) custom-call(bf16[48,64,81]{2,1,0:T(8,128)(2,1)} %bitcast.16, bf16[6,144,512]{2,1,0:T(8,128)(2,1)} %constant.18.clone.spread_ref, bf16[1168,256]{1,0:T(8,128)(2,1)} %constant.17.clone.keep_ref.keep_any, f32[4,64]{1,0:T(4,128)} %bitcast.24, f32[1,64]{1,0:T(1,128)} %bitcast.26), custom_call_target="tpu_custom_call" | custom-call | tf_op jit(solution)/shard_map/weights/pallas_call | solution.py:367
  59.6 0.2 collective-permute-done.5.er_any
  59.8 8.1 %collective-permute-done.4.el_any = bf16[4,12,16,128]{3,2,1,0:T(8,128)(2,1)S(1)} collective-permute-done((bf16[4,12,16,128]{3,2,1,0:T(8,128)(2,1)S(1)}, bf16[4,12,16,128]{3,2,1,0:T(8,128)(2,1)S(1)}, u32[]{:S(2)}, u32[]{:S(2)}) %collective-permute-start.4) | collective-permute-done | bytes 196640 | tf_op jit(solution)/shard_map/ppermute | solution.py:381
  67.9 0.0 copy-done.1
  68.0 0.0 copy-done.4
  68.0 0.7 copy-done.5
  68.6 9.0 %layer.1 = (f32[4,2,2,256]{3,2,1,0:T(2,128)}, bf16[64,16,128]{2,1,0:T(8,128)(2,1)}) custom-call(s32[1]{0:T(128)} %bitcast.x0_ref, s32[1]{0:T(128)} %bitcast.1.z0_ref, s32[4,4]{1,0:T(4,128)} %pat_ref.1, s32[4]{0:T(128)} %par_ref.1, bf16[4,12,16,128]{3,2,1,0:T(8,128)(2,1)} %copy-done.5, bf16[4,12,16,128]{3,2,1,0:T(8,128)(2,1)} %copy-done.1, ...), custom_call_target="tpu_custom_call" | custom-call | tf_op jit(solution)/shard_map/layer/pallas_call | solution.py:367
  77.6 5.6 %all-to-all-start = ((bf16[256,4,128]{2,1,0:T(4,128)(2,1)}), bf16[256,4,128]{2,1,0:T(4,128)(2,1)S(1)}, u32[]{:S(2)}, u32[]{:S(2)}) async-start(bf16[256,4,128]{2,1,0:T(4,128)(2,1)} %bitcast.18), calls=%async_computation | async-start | bytes 524288 | tf_op jit(solution)/shard_map/all_to_all | solution.py:432
  83.2 15.7 %all-to-all-done.in_ref = bf16[256,4,128]{2,1,0:T(4,128)(2,1)S(1)} async-done(((bf16[256,4,128]{2,1,0:T(4,128)(2,1)}), bf16[256,4,128]{2,1,0:T(4,128)(2,1)S(1)}, u32[]{:S(2)}, u32[]{:S(2)}) %all-to-all-start) | async-done | bytes 262176 | tf_op jit(solution)/shard_map/all_to_all | solution.py:432
  99.0 0.7 copy-done
  99.7 2.1 %total.1 = bf16[256,4,128]{2,1,0:T(4,128)(2,1)} custom-call(s32[1]{0:T(128)} %bitcast.9.me_ref, bf16[256,4,128]{2,1,0:T(4,128)(2,1)} %copy-done), custom_call_target="tpu_custom_call" | custom-call | tf_op jit(solution)/shard_map/total/pallas_call | solution.py:367
  101.8 22.4 %all_to_all.10 = bf16[256,4,128]{2,1,0:T(4,128)(2,1)} all-to-all(bf16[256,4,128]{2,1,0:T(4,128)(2,1)} %total.1), channel_id=1, replica_groups=mesh['xy'=64,'gz'=4] {'xy','gz'}, dimensions={0} | all-to-all | bytes 524288 | tf_op jit(solution)/shard_map/all_to_all | solution.py:435
  124.2 3.3 %expand.1 = (f32[48,64,81]{2,1,0:T(8,128)}, f32[1,64]{1,0:T(1,128)}, f32[4,64]{1,0:T(4,128)}) custom-call(bf16[64,16,128]{2,1,0:T(8,128)(2,1)} %bitcast.17, bf16[6,144,512]{2,1,0:T(8,128)(2,1)} %constant.18.clone.spread_ref), custom_call_target="tpu_custom_call" | custom-call | tf_op jit(solution)/shard_map/expand/pallas_call | solution.py:367
  (3 shorter events, 0.0 us)
Async XLA Ops:
  18.5 16.9 %collective-permute-start = (f32[3,2,3,3,5,1,256]{6,5,4,3,2,1,0:T(1,128)}, f32[3,2,3,3,5,1,256]{6,5,4,3,2,1,0:T(1,128)S(1)}, u32[]{:S(2)}, u32[]{:S(2)}) collective-permute-start(f32[3,2,3,3,5,1,256]{6,5,4,3,2,1,0:T(1,128)} %get-tuple-element.20), channel_id=1, source_target_pairs={{0,252},{4,0},{8,4},{12,8},{16,12},{20,16},{24,20},{28,24},{32,28}... | collective-permute-start | bytes 829448 | tf_op jit(solution)/shard_map/ppermute | solution.py:381
  29.8 6.2 %collective-permute-start.1 = (f32[3,2,3,3,5,2,128]{6,5,4,3,2,1,0:T(2,128)}, f32[3,2,3,3,5,2,128]{6,5,4,3,2,1,0:T(2,128)S(1)}, u32[]{:S(2)}, u32[]{:S(2)}) collective-permute-start(f32[3,2,3,3,5,2,128]{6,5,4,3,2,1,0:T(2,128)} %get-tuple-element.21), channel_id=1, source_target_pairs={{0,3},{1,0},{2,1},{3,2},{4,7},{5,4},{6,5},{7,6},{8,11},{9,8},{10,9... | collective-permute-start | bytes 829448 | tf_op jit(solution)/shard_map/ppermute | solution.py:381
  35.4 0.7 copy-start.2
  36.0 0.7 copy-start.3
  40.9 2.9 %collective-permute-start.2 = (bf16[12,16,128]{2,1,0:T(8,128)(2,1)}, bf16[12,16,128]{2,1,0:T(8,128)(2,1)S(1)}, u32[]{:S(2)}, u32[]{:S(2)}) collective-permute-start(bf16[12,16,128]{2,1,0:T(8,128)(2,1)} %get-tuple-element.26), channel_id=1, source_target_pairs={{0,1},{1,2},{2,3},{3,0},{4,5},{5,6},{6,7},{7,4},{8,9},{9,10},{10,1... | collective-permute-start | bytes 147464 | tf_op jit(solution)/shard_map/ppermute | solution.py:381
  42.3 3.7 %collective-permute-start.3 = (bf16[12,16,128]{2,1,0:T(8,128)(2,1)}, bf16[12,16,128]{2,1,0:T(8,128)(2,1)S(1)}, u32[]{:S(2)}, u32[]{:S(2)}) collective-permute-start(bf16[12,16,128]{2,1,0:T(8,128)(2,1)} %get-tuple-element.27), channel_id=1, source_target_pairs={{0,3},{1,0},{2,1},{3,2},{4,7},{5,4},{6,5},{7,6},{8,11},{9,8},{10,9... | collective-permute-start | bytes 147464 | tf_op jit(solution)/shard_map/ppermute | solution.py:381
  46.9 21.0 %copy-start.1 = (bf16[4,12,16,128]{3,2,1,0:T(8,128)(2,1)}, bf16[4,12,16,128]{3,2,1,0:T(8,128)(2,1)S(1)}, u32[]{:S(2)}) copy-start(bf16[4,12,16,128]{3,2,1,0:T(8,128)(2,1)S(1)} %pad_maximum_fusion.e_any) | copy-start | bytes 589828
  46.9 12.9 %collective-permute-start.5 = (bf16[4,12,16,128]{3,2,1,0:T(8,128)(2,1)S(1)}, bf16[4,12,16,128]{3,2,1,0:T(8,128)(2,1)S(1)}, u32[]{:S(2)}, u32[]{:S(2)}) collective-permute-start(bf16[4,12,16,128]{3,2,1,0:T(8,128)(2,1)S(1)} %pad_maximum_fusion.e_any), channel_id=1, source_target_pairs={{0,252},{4,0},{8,4},{12,8},{16,12},{20,16},{24,20},{28,24},{32,28}... | collective-permute-start | bytes 589832 | tf_op jit(solution)/shard_map/ppermute | solution.py:381
  55.4 12.5 %collective-permute-start.4 = (bf16[4,12,16,128]{3,2,1,0:T(8,128)(2,1)S(1)}, bf16[4,12,16,128]{3,2,1,0:T(8,128)(2,1)S(1)}, u32[]{:S(2)}, u32[]{:S(2)}) collective-permute-start(bf16[4,12,16,128]{3,2,1,0:T(8,128)(2,1)S(1)} %pad_maximum_fusion.e_any), channel_id=1, source_target_pairs={{0,4},{4,8},{8,12},{12,16},{16,20},{20,24},{24,28},{28,32},{32,36}... | collective-permute-start | bytes 589832 | tf_op jit(solution)/shard_map/ppermute | solution.py:381
  59.8 8.1 %copy-start.4 = (bf16[4,12,16,128]{3,2,1,0:T(8,128)(2,1)}, bf16[4,12,16,128]{3,2,1,0:T(8,128)(2,1)S(1)}, u32[]{:S(2)}) copy-start(bf16[4,12,16,128]{3,2,1,0:T(8,128)(2,1)S(1)} %collective-permute-done.5.er_any) | copy-start | bytes 589828
  67.9 0.7 copy-start.5
  77.6 21.3 %all-to-all-start = ((bf16[256,4,128]{2,1,0:T(4,128)(2,1)}), bf16[256,4,128]{2,1,0:T(4,128)(2,1)S(1)}, u32[]{:S(2)}, u32[]{:S(2)}) async-start(bf16[256,4,128]{2,1,0:T(4,128)(2,1)} %bitcast.18), calls=%async_computation | async-start | bytes 524288 | tf_op jit(solution)/shard_map/all_to_all | solution.py:432
  99.0 0.7 copy-start

commit v4 on v2

--- a/solution.py
+++ b/solution.py
@@ -79,42 +79,81 @@
     small_ref[...] = jnp.concatenate([head_ref[...], bias_ref[...], jnp.zeros((3, 64), F32)], axis=0).T
 
 
-def loops_body(l_ref, xh_ref, zh_ref, o0_ref, o1_ref, xs_ref, zs_ref, pq_ref, tile_ref):
-    def stage(c, carry):
-        for tau in range(5):
-            xs_ref[c, pl.ds(4 * tau + 1, 2, stride=2), :] = xh_ref[c, tau]
-            zs_ref[c, 4 * tau + 2 : 4 * tau + 4, :] = zh_ref[c, tau]
-        return carry
-
-    lax.fori_loop(0, 54, stage, 0)
+def run(copies):
+    for copy in copies:
+        copy.start()
+    for copy in copies:
+        copy.wait()
+
+
+def fetch(links_ref, l_ref, sems, slices):
+    return [
+        pltpu.make_async_copy(
+            links_ref.at[:, :, :, :, tau, :, lb * 128 : lb * 128 + 128],
+            l_ref.at[0:4, :, :, :, tau * 4 + lb * 2 : tau * 4 + lb * 2 + 2, :],
+            sems.at[tau * 2 + lb],
+        )
+        for tau in range(slices)
+        for lb in range(2)
+    ]
+
+
+def send_body(links_ref, x_ref, z_ref, l_ref, sems):
+    run(fetch(links_ref, l_ref, sems, 5))
+    rows_ref = l_ref.reshape(90 * 24, 128)
+    for tau in range(5):
+        for half in range(2):
+            at = tau * 2 + half
+            x_ref[at] = rows_ref[pl.ds(18 * 24 + tau * 4 + half * 2, 54, stride=24), :].astype(BF16)
+            row = tau * 4 + half
+            first = rows_ref[pl.ds(row, 36, stride=24), :]
+            last = rows_ref[pl.ds(54 * 24 + row, 18, stride=24), :]
+            z_ref[at] = jnp.concatenate([first, last], axis=0).astype(BF16)
+
+
+def loops_body(
+    links_ref, xh_ref, zh_ref, o0_ref, o1_ref, l_ref, xs_ref, zs_ref, pq_ref, tile_ref, sems
+):
+    copies = fetch(links_ref, l_ref, sems, 6)
+    for copy in copies:
+        copy.start()
+    for tau in range(5):
+        for half in range(2):
+            at = tau * 2 + half
+            xs_ref[pl.ds(tau * 4 + half * 2 + 1, 54, stride=24), :] = xh_ref[at].astype(F32)
+            zs_ref[pl.ds(tau * 4 + 2 + half, 54, stride=24), :] = zh_ref[at].astype(F32)
+    for copy in copies:
+        copy.wait()
     row = lax.broadcasted_iota(jnp.int32, (8, 128), 0)
     odd_x = row % 2 == 1
     high_z = row % 4 >= 2
     upper = lanes((8, 128)) >= LY
 
-    def comp(d, ri, i, j):
-        return ((d * 2 + ri) * 3 + i) * 3 + j
-
     def at_site(d, k):
+        part = slice(8 * k, 8 * k + 8)
         return [
-            [[l_ref[comp(d, ri, i, j), 8 * k : 8 * k + 8, :] for j in range(3)] for i in range(3)]
-            for ri in range(2)
+            [[l_ref[d, ri, i, j, part, :] for j in range(3)] for i in range(3)] for ri in range(2)
         ]
 
+    def border(d, ri, i, j, k):
+        row = (((d * 2 + ri) * 3 + i) * 3 + j) * 24 + 8 * k
+        return slice(row, row + 8)
+
     def ahead(d, step, k):
+        part = slice(8 * k, 8 * k + 8)
+
         def one(ri, i, j):
-            c = comp(d, ri, i, j)
             if step == 3:
                 if k < 2:
-                    return l_ref[c, 8 * k + 4 : 8 * k + 12, :]
-                return pltpu.roll(l_ref[c, 16:24, :], 4, 0)
-            own = l_ref[c, 8 * k : 8 * k + 8, :]
+                    return l_ref[d, ri, i, j, 8 * k + 4 : 8 * k + 12, :]
+                return pltpu.roll(l_ref[d, ri, i, j, 16:24, :], 4, 0)
+            own = l_ref[d, ri, i, j, part, :]
             if step == 0:
-                return jnp.where(odd_x, xs_ref[c - 18, 8 * k : 8 * k + 8, :], pltpu.roll(own, 7, 0))
+                return jnp.where(odd_x, xs_ref[border(d - 1, ri, i, j, k), :], pltpu.roll(own, 7, 0))
             if step == 1:
                 return shift_y(own, 1)
-            h = c if d < 2 else c - 18
-            beyond = jnp.where(high_z, zs_ref[h, 8 * k : 8 * k + 8, :], pltpu.roll(own, 6, 0))
+            edge = zs_ref[border(min(d, 2), ri, i, j, k), :]
+            beyond = jnp.where(high_z, edge, pltpu.roll(own, 6, 0))
             return pltpu.roll(jnp.where(upper, own, beyond), LY, 1)
 
         return [[[one(ri, i, j) for j in range(3)] for i in range(3)] for ri in range(2)]
@@ -297,14 +336,16 @@
     b_ref[...] = small[4:5]
 
 
-def call(body, outs, scratch, *args, smem=0, name):
-    vmem = pl.BlockSpec(memory_space=pltpu.VMEM)
-    specs = [pl.BlockSpec(memory_space=pltpu.SMEM)] * smem + [vmem] * (len(args) - smem)
+def call(body, outs, scratch, *args, smem=0, away=(), name):
+    def spec(i, away):
+        return pl.BlockSpec(memory_space=pl.ANY if i in away else pltpu.VMEM)
+
+    specs = [pl.BlockSpec(memory_space=pltpu.SMEM)] * smem
     return pl.pallas_call(
         body,
         out_shape=outs,
-        in_specs=specs,
-        out_specs=jax.tree.map(lambda _: vmem, outs),
+        in_specs=specs + [spec(i, away) for i in range(smem, len(args))],
+        out_specs=(pl.BlockSpec(memory_space=pltpu.VMEM),) * len(outs),
         scratch_shapes=scratch,
         compiler_params=PARAMS,
         interpret=INTERPRET,
@@ -318,11 +359,15 @@
 
 
 def per_device(gauge_links, pattern, link_parity, conv_weight, conv_bias, head_weight, cotangent):
-    rows = gauge_links.reshape(72, 6, 2, 2, 128).transpose(0, 1, 3, 2, 4)
-    next_x = shifted(rows[18:, :5, :, 0, :], "xy", -1)
-    edge_z = jnp.concatenate([rows[:36, :5, 0], rows[54:, :5, 0]])
-    next_z = shifted(edge_z, "gz", -1)
     shape = jax.ShapeDtypeStruct
+    sems = pltpu.SemaphoreType.DMA
+    edge = shape((10, 54, 128), BF16)
+    links = pltpu.VMEM((5, 2, 3, 3, 24, 128), F32)
+    x_edge, z_edge = call(
+        send_body, (edge, edge), [links, sems((10,))], gauge_links, away=(0,), name="send"
+    )
+    next_x = shifted(x_edge, "xy", -1)
+    next_z = shifted(z_edge, "gz", -1)
     keep = jnp.asarray(np.concatenate(KEEP), BF16)
     spread = jnp.asarray(SPREAD, BF16)
     weights, small = call(
@@ -330,11 +375,11 @@
         conv_weight.transpose(1, 2, 0), spread, keep, head_weight.T, conv_bias[None], name="weights",
     )
     half = shape((12, 16, 128), BF16)
-    halo = pltpu.VMEM((54, 24, 128), F32)
+    border = pltpu.VMEM((57 * 24, 128), F32)
     low_z, high_z = call(
         loops_body, (half, half),
-        [halo, halo, pltpu.VMEM((12, 24, 128), F32), pltpu.VMEM((12, 2, 16, 128), F32)],
-        rows.reshape(72, 24, 128), next_x, next_z, name="loops",
+        [links, border, border, pltpu.VMEM((14, 24, 128), F32), pltpu.VMEM((12, 2, 16, 128), F32), sems((12,))],
+        gauge_links, next_x, next_z, away=(0,), name="loops",
     )
     before_z = shifted(high_z, "gz", 1)
     after_z = shifted(low_z, "gz", -1)
@@ -354,7 +399,7 @@
     chunks = grads.reshape(count, 1024 // count, 128)
     chunks = lax.all_to_all(chunks, both, 0, 0, tiled=True)
     me = lax.axis_index(both).reshape(1)
-    chunks = call(total_body, shape(chunks.shape, BF16), [], me, chunks, smem=1, name="total")
+    chunks = call(total_body, (shape(chunks.shape, BF16),), [], me, chunks, smem=1, name="total")[0]
     chunks = lax.all_to_all(chunks, both, 0, 0, tiled=True)
     grad_kernel, grad_bias, grad_head = call(
         expand_body, (shape((48, 64, 81), F32), shape((1, 64), F32), shape((4, 64), F32)),

time: 107 us -> 109 us (1.019)
  waiting for transfers between devices: 21.2 us -> 29.8 us
  starting transfers between devices: 32.2 us -> 27 us
  local copies, waits for them, and re-layouts: 6.41 us -> 2.06 us
  Pallas kernels: 22.5 us -> 25.5 us
    ppermute x6, waiting for transfers between devices: 5.96 us -> 14.1 us  [shifted(): return lax.ppermute(x, axis, [(i, (i + by) % count) for i in range(count)])]
    all_to_all x1, starting transfers between devices: 9.4 us -> 5.6 us  [per_device(): chunks = lax.all_to_all(chunks, both, 0, 0, tiled=True)]
    reshape x3 -> x0, local copies, waits for them, and re-layouts: 3.71 us -> none  [the longest x2 2.64 us: per_device(): rows = gauge_links.reshape(72, 6, 2, 2, 128).transpose(0, 1, 3, 2, 4)]
    pallas_call x5 -> x6, Pallas kernels: 22.5 us -> 25.5 us  [call(): pl.pallas_call(body, out_shape=outs, in_specs=specs + [spec(i, away) for...]
    ppermute x6, starting transfers between devices: 22.8 us -> 21.4 us  [shifted(): return lax.ppermute(x, axis, [(i, (i + by) % count) for i in range(count)])]
  transfers between devices with their start and end apart: 7 -> 7, of which waited for: 3 -> 6; matrix products, arithmetic and copies ran while one was open for 1% -> 0% of each run, Pallas kernels for 6% -> 5%
where the time goes in v4:
time: 109 us; the launch traced here: 108 us
  waiting for transfers between devices  29.8 us (27%)
  starting transfers between devices  27 us (25%)
  Pallas kernels  25.5 us (23%)
  blocking collectives  22.4 us (21%)
  local copies, waits for them, and re-layouts  2.06 us (2%)
    pallas_call x6, Pallas kernels, call(): pl.pallas_call(body, out_shape=outs, in_specs=specs + [spec(i, away) for...  25.5 us
    all_to_all x1, blocking collectives, per_device(): chunks = lax.all_to_all(chunks, both, 0, 0, tiled=True)  22.4 us
    ppermute x6, starting transfers between devices, shifted(): return lax.ppermute(x, axis, [(i, (i + by) % count) for i in range(count)])  21.4 us
    all_to_all x1, waiting for transfers between devices, per_device(): chunks = lax.all_to_all(chunks, both, 0, 0, tiled=True)  15.7 us
    ppermute x6, waiting for transfers between devices, shifted(): return lax.ppermute(x, axis, [(i, (i + by) % count) for i in range(count)])  14.1 us
    all_to_all x1, starting transfers between devices, per_device(): chunks = lax.all_to_all(chunks, both, 0, 0, tiled=True)  5.6 us
  transfers between devices with their start and end apart: 7, of which 6 were waited for; matrix products, arithmetic and copies ran while one was open for 0% of the time, Pallas kernels for 5%

profile of v4, /device:TPU:1, one launch (start us, length us, event | category | flops | bytes accessed | tf_op | source)
XLA Modules:
  0.0 108.2 jit_solution(11287674948098670514)
XLA Ops:
  0.6 2.1 %send.1 = (bf16[10,54,128]{2,1,0:T(8,128)(2,1)}, bf16[10,54,128]{2,1,0:T(8,128)(2,1)}) custom-call(f32[4,2,3,3,6,2,256]{6,5,4,3,2,1,0:T(2,128)} %links_ref.3), custom_call_target="tpu_custom_call" | custom-call | tf_op jit(solution)/shard_map/send/pallas_call | solution.py:344
  2.8 11.3 %collective-permute-start = (bf16[10,54,128]{2,1,0:T(8,128)(2,1)}, bf16[10,54,128]{2,1,0:T(8,128)(2,1)S(1)}, u32[]{:S(2)}, u32[]{:S(2)}) collective-permute-start(bf16[10,54,128]{2,1,0:T(8,128)(2,1)} %get-tuple-element.15), channel_id=1, source_target_pairs={{0,252},{4,0},{8,4},{12,8},{16,12},{20,16},{24,20},{28,24},{32,28}... | collective-permute-start | bytes 414728 | tf_op jit(solution)/shard_map/ppermute | solution.py:358
  14.1 1.0 collective-permute-start.1
  15.0 1.8 %collective-permute-done.xh_ref = bf16[10,54,128]{2,1,0:T(8,128)(2,1)S(1)} collective-permute-done((bf16[10,54,128]{2,1,0:T(8,128)(2,1)}, bf16[10,54,128]{2,1,0:T(8,128)(2,1)S(1)}, u32[]{:S(2)}, u32[]{:S(2)}) %collective-permute-start) | collective-permute-done | bytes 138272 | tf_op jit(solution)/shard_map/ppermute | solution.py:358
  16.8 0.0 copy-start.4
  16.8 2.0 %collective-permute-done.1.zh_ref = bf16[10,54,128]{2,1,0:T(8,128)(2,1)S(1)} collective-permute-done((bf16[10,54,128]{2,1,0:T(8,128)(2,1)}, bf16[10,54,128]{2,1,0:T(8,128)(2,1)S(1)}, u32[]{:S(2)}, u32[]{:S(2)}) %collective-permute-start.1) | collective-permute-done | bytes 138272 | tf_op jit(solution)/shard_map/ppermute | solution.py:358
  18.8 0.0 copy-done.4
  18.8 0.0 copy-start.5
  18.8 0.7 copy-done.5
  19.5 4.5 %loops.1 = (bf16[12,16,128]{2,1,0:T(8,128)(2,1)}, bf16[12,16,128]{2,1,0:T(8,128)(2,1)}) custom-call(f32[4,2,3,3,6,2,256]{6,5,4,3,2,1,0:T(2,128)} %links_ref.3, bf16[10,54,128]{2,1,0:T(8,128)(2,1)} %copy-done.4, bf16[10,54,128]{2,1,0:T(8,128)(2,1)} %copy-done.5), custom_call_target="tpu_custom_call" | custom-call | tf_op jit(solution)/shard_map/loops/pallas_call | solution.py:344
  24.0 0.6 collective-permute-start.2
  24.6 0.0 collective-permute-start.3
  24.6 1.5 %collective-permute-done.2 = bf16[12,16,128]{2,1,0:T(8,128)(2,1)S(1)} collective-permute-done((bf16[12,16,128]{2,1,0:T(8,128)(2,1)}, bf16[12,16,128]{2,1,0:T(8,128)(2,1)S(1)}, u32[]{:S(2)}, u32[]{:S(2)}) %collective-permute-start.2) | collective-permute-done | bytes 49184 | tf_op jit(solution)/shard_map/ppermute | solution.py:358
  26.0 2.2 %collective-permute-done.3 = bf16[12,16,128]{2,1,0:T(8,128)(2,1)S(1)} collective-permute-done((bf16[12,16,128]{2,1,0:T(8,128)(2,1)}, bf16[12,16,128]{2,1,0:T(8,128)(2,1)S(1)}, u32[]{:S(2)}, u32[]{:S(2)}) %collective-permute-start.3) | collective-permute-done | bytes 49184 | tf_op jit(solution)/shard_map/ppermute | solution.py:358
  28.3 0.8 pad_maximum_fusion.e_ref
  29.1 0.0 copy-start.1
  29.1 8.5 %collective-permute-start.5 = (bf16[4,12,16,128]{3,2,1,0:T(8,128)(2,1)S(1)}, bf16[4,12,16,128]{3,2,1,0:T(8,128)(2,1)S(1)}, u32[]{:S(2)}, u32[]{:S(2)}) collective-permute-start(bf16[4,12,16,128]{3,2,1,0:T(8,128)(2,1)S(1)} %pad_maximum_fusion.e_ref), channel_id=1, source_target_pairs={{0,252},{4,0},{8,4},{12,8},{16,12},{20,16},{24,20},{28,24},{32,28}... | collective-permute-start | bytes 589832 | tf_op jit(solution)/shard_map/ppermute | solution.py:358
  37.6 0.0 collective-permute-start.4
  37.6 5.9 %weights.1 = (bf16[12,128,256]{2,1,0:T(8,128)(2,1)}, f32[64,8]{1,0:T(8,128)}) custom-call(bf16[48,64,81]{2,1,0:T(8,128)(2,1)} %bitcast.16, bf16[6,144,512]{2,1,0:T(8,128)(2,1)} %constant.18.clone.spread_ref, bf16[1168,256]{1,0:T(8,128)(2,1)} %constant.17.clone.keep_ref, f32[4,64]{1,0:T(4,128)} %bitcast.22, f32[1,64]{1,0:T(1,128)} %bitcast.23), custom_call_target="tpu_custom_call" | custom-call | tf_op jit(solution)/shard_map/weights/pallas_call | solution.py:344
  43.6 0.0 collective-permute-done.5.er_ref
  43.6 0.0 copy-start.2
  43.6 6.6 %collective-permute-done.4.el_ref = bf16[4,12,16,128]{3,2,1,0:T(8,128)(2,1)S(1)} collective-permute-done((bf16[4,12,16,128]{3,2,1,0:T(8,128)(2,1)S(1)}, bf16[4,12,16,128]{3,2,1,0:T(8,128)(2,1)S(1)}, u32[]{:S(2)}, u32[]{:S(2)}) %collective-permute-start.4) | collective-permute-done | bytes 196640 | tf_op jit(solution)/shard_map/ppermute | solution.py:358
  50.2 0.0 copy-done.1
  50.2 0.0 copy-done.2
  50.2 0.7 copy-done.3
  50.8 8.0 %layer.1 = (f32[4,2,2,256]{3,2,1,0:T(2,128)}, bf16[64,16,128]{2,1,0:T(8,128)(2,1)}) custom-call(s32[1]{0:T(128)} %bitcast.x0_ref, s32[1]{0:T(128)} %bitcast.1.z0_ref, s32[4,4]{1,0:T(4,128)} %pat_ref.1, s32[4]{0:T(128)} %par_ref.1, bf16[4,12,16,128]{3,2,1,0:T(8,128)(2,1)} %copy-done.3, bf16[4,12,16,128]{3,2,1,0:T(8,128)(2,1)} %copy-done.1, ...), custom_call_target="tpu_custom_call" | custom-call | tf_op jit(solution)/shard_map/layer/pallas_call | solution.py:344
  58.8 5.6 %all-to-all-start = ((bf16[256,4,128]{2,1,0:T(4,128)(2,1)}), bf16[256,4,128]{2,1,0:T(4,128)(2,1)S(1)}, u32[]{:S(2)}, u32[]{:S(2)}) async-start(bf16[256,4,128]{2,1,0:T(4,128)(2,1)} %bitcast.17), calls=%async_computation | async-start | bytes 524288 | tf_op jit(solution)/shard_map/all_to_all | solution.py:400
  64.4 15.7 %all-to-all-done.in_ref = bf16[256,4,128]{2,1,0:T(4,128)(2,1)S(1)} async-done(((bf16[256,4,128]{2,1,0:T(4,128)(2,1)}), bf16[256,4,128]{2,1,0:T(4,128)(2,1)S(1)}, u32[]{:S(2)}, u32[]{:S(2)}) %all-to-all-start) | async-done | bytes 262176 | tf_op jit(solution)/shard_map/all_to_all | solution.py:400
  80.2 0.7 copy-done
  80.9 2.1 %total.1 = bf16[256,4,128]{2,1,0:T(4,128)(2,1)} custom-call(s32[1]{0:T(128)} %bitcast.9.me_ref, bf16[256,4,128]{2,1,0:T(4,128)(2,1)} %copy-done), custom_call_target="tpu_custom_call" | custom-call | tf_op jit(solution)/shard_map/total/pallas_call | solution.py:344
  83.0 22.4 %all_to_all.10 = bf16[256,4,128]{2,1,0:T(4,128)(2,1)} all-to-all(bf16[256,4,128]{2,1,0:T(4,128)(2,1)} %total.1), channel_id=1, replica_groups=mesh['xy'=64,'gz'=4] {'xy','gz'}, dimensions={0} | all-to-all | bytes 524288 | tf_op jit(solution)/shard_map/all_to_all | solution.py:403
  105.4 2.8 %expand.1 = (f32[48,64,81]{2,1,0:T(8,128)}, f32[1,64]{1,0:T(1,128)}, f32[4,64]{1,0:T(4,128)}) custom-call(bf16[64,16,128]{2,1,0:T(8,128)(2,1)} %bitcast.15, bf16[6,144,512]{2,1,0:T(8,128)(2,1)} %constant.18.clone.spread_ref), custom_call_target="tpu_custom_call" | custom-call | tf_op jit(solution)/shard_map/expand/pallas_call | solution.py:344
  (2 shorter events, 0.0 us)
Async XLA Ops:
  2.8 14.1 %collective-permute-start = (bf16[10,54,128]{2,1,0:T(8,128)(2,1)}, bf16[10,54,128]{2,1,0:T(8,128)(2,1)S(1)}, u32[]{:S(2)}, u32[]{:S(2)}) collective-permute-start(bf16[10,54,128]{2,1,0:T(8,128)(2,1)} %get-tuple-element.15), channel_id=1, source_target_pairs={{0,252},{4,0},{8,4},{12,8},{16,12},{20,16},{24,20},{28,24},{32,28}... | collective-permute-start | bytes 414728 | tf_op jit(solution)/shard_map/ppermute | solution.py:358
  14.1 4.7 %collective-permute-start.1 = (bf16[10,54,128]{2,1,0:T(8,128)(2,1)}, bf16[10,54,128]{2,1,0:T(8,128)(2,1)S(1)}, u32[]{:S(2)}, u32[]{:S(2)}) collective-permute-start(bf16[10,54,128]{2,1,0:T(8,128)(2,1)} %get-tuple-element.16), channel_id=1, source_target_pairs={{0,3},{1,0},{2,1},{3,2},{4,7},{5,4},{6,5},{7,6},{8,11},{9,8},{10,9... | collective-permute-start | bytes 414728 | tf_op jit(solution)/shard_map/ppermute | solution.py:358
  16.8 2.0 %copy-start.4 = (bf16[10,54,128]{2,1,0:T(8,128)(2,1)}, bf16[10,54,128]{2,1,0:T(8,128)(2,1)S(1)}, u32[]{:S(2)}) copy-start(bf16[10,54,128]{2,1,0:T(8,128)(2,1)S(1)} %collective-permute-done.xh_ref) | copy-start | bytes 414724
  18.8 0.7 copy-start.5
  24.0 2.1 %collective-permute-start.2 = (bf16[12,16,128]{2,1,0:T(8,128)(2,1)}, bf16[12,16,128]{2,1,0:T(8,128)(2,1)S(1)}, u32[]{:S(2)}, u32[]{:S(2)}) collective-permute-start(bf16[12,16,128]{2,1,0:T(8,128)(2,1)} %get-tuple-element.17), channel_id=1, source_target_pairs={{0,1},{1,2},{2,3},{3,0},{4,5},{5,6},{6,7},{7,4},{8,9},{9,10},{10,1... | collective-permute-start | bytes 147464 | tf_op jit(solution)/shard_map/ppermute | solution.py:358
  24.6 3.7 %collective-permute-start.3 = (bf16[12,16,128]{2,1,0:T(8,128)(2,1)}, bf16[12,16,128]{2,1,0:T(8,128)(2,1)S(1)}, u32[]{:S(2)}, u32[]{:S(2)}) collective-permute-start(bf16[12,16,128]{2,1,0:T(8,128)(2,1)} %get-tuple-element.18), channel_id=1, source_target_pairs={{0,3},{1,0},{2,1},{3,2},{4,7},{5,4},{6,5},{7,6},{8,11},{9,8},{10,9... | collective-permute-start | bytes 147464 | tf_op jit(solution)/shard_map/ppermute | solution.py:358
  29.1 21.0 %copy-start.1 = (bf16[4,12,16,128]{3,2,1,0:T(8,128)(2,1)}, bf16[4,12,16,128]{3,2,1,0:T(8,128)(2,1)S(1)}, u32[]{:S(2)}) copy-start(bf16[4,12,16,128]{3,2,1,0:T(8,128)(2,1)S(1)} %pad_maximum_fusion.e_ref) | copy-start | bytes 589828
  29.1 14.4 %collective-permute-start.5 = (bf16[4,12,16,128]{3,2,1,0:T(8,128)(2,1)S(1)}, bf16[4,12,16,128]{3,2,1,0:T(8,128)(2,1)S(1)}, u32[]{:S(2)}, u32[]{:S(2)}) collective-permute-start(bf16[4,12,16,128]{3,2,1,0:T(8,128)(2,1)S(1)} %pad_maximum_fusion.e_ref), channel_id=1, source_target_pairs={{0,252},{4,0},{8,4},{12,8},{16,12},{20,16},{24,20},{28,24},{32,28}... | collective-permute-start | bytes 589832 | tf_op jit(solution)/shard_map/ppermute | solution.py:358
  37.6 12.5 %collective-permute-start.4 = (bf16[4,12,16,128]{3,2,1,0:T(8,128)(2,1)S(1)}, bf16[4,12,16,128]{3,2,1,0:T(8,128)(2,1)S(1)}, u32[]{:S(2)}, u32[]{:S(2)}) collective-permute-start(bf16[4,12,16,128]{3,2,1,0:T(8,128)(2,1)S(1)} %pad_maximum_fusion.e_ref), channel_id=1, source_target_pairs={{0,4},{4,8},{8,12},{12,16},{16,20},{20,24},{24,28},{28,32},{32,36}... | collective-permute-start | bytes 589832 | tf_op jit(solution)/shard_map/ppermute | solution.py:358
  43.6 6.6 %copy-start.2 = (bf16[4,12,16,128]{3,2,1,0:T(8,128)(2,1)}, bf16[4,12,16,128]{3,2,1,0:T(8,128)(2,1)S(1)}, u32[]{:S(2)}) copy-start(bf16[4,12,16,128]{3,2,1,0:T(8,128)(2,1)S(1)} %collective-permute-done.5.er_ref) | copy-start | bytes 589828
  50.2 0.7 copy-start.3
  58.8 21.3 %all-to-all-start = ((bf16[256,4,128]{2,1,0:T(4,128)(2,1)}), bf16[256,4,128]{2,1,0:T(4,128)(2,1)S(1)}, u32[]{:S(2)}, u32[]{:S(2)}) async-start(bf16[256,4,128]{2,1,0:T(4,128)(2,1)} %bitcast.17), calls=%async_computation | async-start | bytes 524288 | tf_op jit(solution)/shard_map/all_to_all | solution.py:400
  80.2 0.7 copy-start

commit v5 on v4

--- a/solution.py
+++ b/solution.py
@@ -79,6 +79,10 @@
     small_ref[...] = jnp.concatenate([head_ref[...], bias_ref[...], jnp.zeros((3, 64), F32)], axis=0).T
 
 
+def place(c, x):
+    return 64 + 5 * c if x == 1 else (32 + 5 * c if c < 6 else 5 * (c - 6))
+
+
 def run(copies):
     for copy in copies:
         copy.start()
@@ -122,6 +126,7 @@
             at = tau * 2 + half
             xs_ref[pl.ds(tau * 4 + half * 2 + 1, 54, stride=24), :] = xh_ref[at].astype(F32)
             zs_ref[pl.ds(tau * 4 + 2 + half, 54, stride=24), :] = zh_ref[at].astype(F32)
+    tile_ref[...] = jnp.zeros_like(tile_ref)
     for copy in copies:
         copy.wait()
     row = lax.broadcasted_iota(jnp.int32, (8, 128), 0)
@@ -185,19 +190,33 @@
             pq_ref[2 * p + 1, 8 * k : 8 * k + 8, :] = im
     for c in range(12):
         for lb, o_ref in enumerate((o0_ref, o1_ref)):
-            for t in range(2):
-                for x in range(2):
-                    tile_ref[c, lb, t * 8 + x * 4 : t * 8 + x * 4 + 4, :] = pq_ref[
-                        c, pl.ds(4 * t + 2 * lb + x, 4, stride=4), :
-                    ]
-            o_ref[c] = tile_ref[c, lb].astype(BF16)
+            for x in range(2):
+                row = place(c, x)
+                tile_ref[lb, row : row + 5, :] = pq_ref[c, pl.ds(2 * lb + x, 5, stride=4), :]
+    o0_ref[...] = tile_ref[0].astype(BF16)
+    o1_ref[...] = tile_ref[1].astype(BF16)
 
 
 def layer_body(
-    x0_ref, z0_ref, pat_ref, par_ref, el_ref, e_ref, er_ref, w_ref, small_ref, keep_ref, cot_ref,
-    coef_ref, g_ref, a_ref, low_ref, rows_ref,
+    x0_ref, z0_ref, pat_ref, par_ref, before_ref, z0_own, z1_own, z2_own, z3_own, after_ref, w_ref, small_ref,
+    keep_ref, cot_ref, coef_ref, g_ref, a_ref, low_ref, rows_ref, left_ref, own_ref, right_ref,
 ):
-    first = lax.broadcasted_iota(jnp.int32, (8, 128), 0) < 4
+    left_ref[...] = before_ref[...].astype(F32)
+    right_ref[...] = after_ref[...].astype(F32)
+    for i, ref in enumerate((z0_own, z1_own, z2_own, z3_own)):
+        own_ref[i] = ref[...].astype(F32)
+
+    def piece(i, x, c, t):
+        if x == 0 and c >= 6:
+            return jnp.zeros((4, 128), F32)
+        if x < 2:
+            ref, row = left_ref, place(c, x) - 32
+        elif x < 4:
+            ref, row = own_ref, place(c, x - 2)
+        else:
+            ref, row = right_ref, place(c, 0)
+        return ref[i, row + t : row + t + 4, :]
+
     lane = lanes((8, 128))
     upper = lane >= LY
 
@@ -210,17 +229,13 @@
         for r in range(2):
             c = 2 * p + r
             for t in range(2):
-                part = slice(8 * t, 8 * t + 8)
                 cols = []
                 for i in range(4):
-                    left, own, right = (ref[i, c].astype(F32)[part] for ref in (el_ref, e_ref, er_ref))
-                    cols.append((
-                        (left, own),
-                        (
-                            pltpu.roll(jnp.where(first, own, left), 4, 0),
-                            pltpu.roll(jnp.where(first, right, own), 4, 0),
-                        ),
-                    ))
+                    pieces = [piece(i, x, c, t) for x in range(5)]
+                    cols.append([
+                        [jnp.concatenate(pieces[x + 2 * h : x + 2 * h + 2], axis=0) for h in range(2)]
+                        for x in range(2)
+                    ])
                 for x in range(2):
                     for y in offsets:
                         by = y - 2
@@ -374,25 +389,29 @@
         weights_body, (shape((12, 128, 256), BF16), shape((64, 8), F32)), [],
         conv_weight.transpose(1, 2, 0), spread, keep, head_weight.T, conv_bias[None], name="weights",
     )
-    half = shape((12, 16, 128), BF16)
+    next_x, next_z, weights, small = lax.optimization_barrier((next_x, next_z, weights, small))
+    half = shape((128, 128), BF16)
     border = pltpu.VMEM((57 * 24, 128), F32)
     low_z, high_z = call(
         loops_body, (half, half),
-        [links, border, border, pltpu.VMEM((14, 24, 128), F32), pltpu.VMEM((12, 2, 16, 128), F32), sems((12,))],
+        [links, border, border, pltpu.VMEM((14, 24, 128), F32), pltpu.VMEM((2, 128, 128), F32), sems((12,))],
         gauge_links, next_x, next_z, away=(0,), name="loops",
     )
     before_z = shifted(high_z, "gz", 1)
     after_z = shifted(low_z, "gz", -1)
-    block = jnp.stack([before_z, low_z, high_z, after_z])
-    before_x = shifted(block, "xy", 1)
-    after_x = shifted(block, "xy", -1)
+    layers = [before_z, low_z, high_z, after_z]
+    right_going = jnp.stack([v[32:] for v in layers])
+    before_x = shifted(right_going, "xy", 1)
+    held = lax.optimization_barrier((right_going, *layers))
+    after_x = shifted(jnp.stack([v[:64] for v in held[1:]]), "xy", -1)
     x_first = (lax.axis_index("xy") * 2).reshape(1)
     z_first = (lax.axis_index("gz") * 4).reshape(1)
     coefficients, grads = call(
         layer_body, (shape((4, 2, 2, 256), F32), shape((64, 16, 128), BF16)),
-        [pltpu.VMEM((12, 256, 1024), BF16), pltpu.VMEM((64, 1024), BF16), pltpu.VMEM((1024, 128), F32)],
-        x_first, z_first, pattern, link_parity, before_x, block, after_x, weights, small, keep,
-        cotangent, smem=4, name="layer",
+        [pltpu.VMEM((12, 256, 1024), BF16), pltpu.VMEM((64, 1024), BF16), pltpu.VMEM((1024, 128), F32)]
+        + [pltpu.VMEM((4, n, 128), F32) for n in (96, 128, 64)],
+        x_first, z_first, pattern, link_parity, before_x, *layers, after_x, weights, small, keep, cotangent,
+        smem=4, name="layer",
     )
     both = ("xy", "gz")
     count = lax.axis_size(both)

time: 109 us -> 106 us (0.972)
  waiting for transfers between devices: 29.8 us -> 21.2 us
  starting transfers between devices: 27 us -> 31.5 us
  local copies, waits for them, and re-layouts: 2.06 us -> 4.27 us
    ppermute x6, waiting for transfers between devices: 14.1 us -> 5.57 us  [shifted(): return lax.ppermute(x, axis, [(i, (i + by) % count) for i in range(count)])]
    all_to_all x1, starting transfers between devices: 5.6 us -> 11 us  [per_device(): chunks = lax.all_to_all(chunks, both, 0, 0, tiled=True)]
    another operation x0 -> x7, local copies, waits for them, and re-layouts: none -> 2.22 us  [the longest x4 1.44 us: per_device(): after_x = shifted(jnp.stack([v[:64] for v in held[1:]]), 'xy', -1)]
  transfers between devices with their start and end apart: 7 -> 7, of which waited for: 6 -> 4; matrix products, arithmetic and copies ran while one was open for 0% -> 2% of each run, Pallas kernels for 5% -> 6%
where the time goes in v5:
time: 106 us
  starting transfers between devices  31.5 us (30%)
  Pallas kernels  25.6 us (24%)
  blocking collectives  22.4 us (21%)
  waiting for transfers between devices  21.2 us (20%)
  local copies, waits for them, and re-layouts  4.27 us (4%)
    pallas_call x6, Pallas kernels, call(): pl.pallas_call(body, out_shape=outs, in_specs=specs + [spec(i, away) for...  25.6 us
    all_to_all x1, blocking collectives, per_device(): chunks = lax.all_to_all(chunks, both, 0, 0, tiled=True)  22.4 us
    ppermute x6, starting transfers between devices, shifted(): return lax.ppermute(x, axis, [(i, (i + by) % count) for i in range(count)])  20.5 us
    all_to_all x1, waiting for transfers between devices, per_device(): chunks = lax.all_to_all(chunks, both, 0, 0, tiled=True)  15.6 us
    all_to_all x1, starting transfers between devices, per_device(): chunks = lax.all_to_all(chunks, both, 0, 0, tiled=True)  11 us
    ppermute x6, waiting for transfers between devices, shifted(): return lax.ppermute(x, axis, [(i, (i + by) % count) for i in range(count)])  5.57 us
  transfers between devices with their start and end apart: 7, of which 4 were waited for; matrix products, arithmetic and copies ran while one was open for 2% of the time, Pallas kernels for 6%

profile of v5, /device:TPU:1, one launch (start us, length us, event | category | flops | bytes accessed | tf_op | source)
XLA Modules:
  0.0 105.6 jit_solution(10503728818319780551)
XLA Ops:
  0.6 2.1 %send.1 = (bf16[10,54,128]{2,1,0:T(8,128)(2,1)}, bf16[10,54,128]{2,1,0:T(8,128)(2,1)}) custom-call(f32[4,2,3,3,6,2,256]{6,5,4,3,2,1,0:T(2,128)} %links_ref.3), custom_call_target="tpu_custom_call" | custom-call | tf_op jit(solution)/shard_map/send/pallas_call | solution.py:359
  2.8 11.3 %collective-permute-start = (bf16[10,54,128]{2,1,0:T(8,128)(2,1)}, bf16[10,54,128]{2,1,0:T(8,128)(2,1)S(1)}, u32[]{:S(2)}, u32[]{:S(2)}) collective-permute-start(bf16[10,54,128]{2,1,0:T(8,128)(2,1)} %get-tuple-element.23), channel_id=1, source_target_pairs={{0,252},{4,0},{8,4},{12,8},{16,12},{20,16},{24,20},{28,24},{32,28}... | collective-permute-start | bytes 414728 | tf_op jit(solution)/shard_map/ppermute | solution.py:373
  14.1 1.0 collective-permute-start.1
  15.0 5.9 %weights.1 = (bf16[12,128,256]{2,1,0:T(8,128)(2,1)}, f32[64,8]{1,0:T(8,128)}) custom-call(bf16[48,64,81]{2,1,0:T(8,128)(2,1)} %bitcast.28, bf16[6,144,512]{2,1,0:T(8,128)(2,1)} %constant.18.clone.spread_ref, bf16[1168,256]{1,0:T(8,128)(2,1)} %constant.17.clone.keep_ref, f32[4,64]{1,0:T(4,128)} %bitcast.30, f32[1,64]{1,0:T(1,128)} %bitcast.31), custom_call_target="tpu_custom_call" | custom-call | tf_op jit(solution)/shard_map/weights/pallas_call | solution.py:359
  21.0 0.0 collective-permute-done.xh_ref
  21.0 0.0 collective-permute-done.1.zh_ref
  21.0 0.0 copy-start.4
  21.0 0.6 copy-done.3
  21.6 0.1 copy-done.4
  21.7 4.5 %loops.1 = (bf16[128,128]{1,0:T(8,128)(2,1)}, bf16[128,128]{1,0:T(8,128)(2,1)}) custom-call(f32[4,2,3,3,6,2,256]{6,5,4,3,2,1,0:T(2,128)} %links_ref.3, bf16[10,54,128]{2,1,0:T(8,128)(2,1)} %copy-done.3, bf16[10,54,128]{2,1,0:T(8,128)(2,1)} %copy-done.4), custom_call_target="tpu_custom_call" | custom-call | tf_op jit(solution)/shard_map/loops/pallas_call | solution.py:359
  26.1 0.9 collective-permute-start.2
  27.0 0.0 collective-permute-start.3
  27.0 0.8 slice_bitcast_fusion.2
  27.8 0.6 collective-permute-done.2.z0_own
  28.4 3.7 %collective-permute-done.3.z3_own = bf16[128,128]{1,0:T(8,128)(2,1)S(1)} collective-permute-done((bf16[128,128]{1,0:T(8,128)(2,1)}, bf16[128,128]{1,0:T(8,128)(2,1)S(1)}, u32[]{:S(2)}, u32[]{:S(2)}) %collective-permute-start.3) | collective-permute-done | bytes 32800 | tf_op jit(solution)/shard_map/ppermute | solution.py:373
  32.0 0.1 collective-permute-start.4
  32.1 0.7 slice_bitcast_fusion.6
  32.9 0.7 slice_bitcast_fusion.5
  33.6 7.2 %collective-permute-start.5 = (bf16[4,64,128]{2,1,0:T(8,128)(2,1)S(1)}, bf16[4,64,128]{2,1,0:T(8,128)(2,1)S(1)}, u32[]{:S(2)}, u32[]{:S(2)}) collective-permute-start(bf16[4,64,128]{2,1,0:T(8,128)(2,1)S(1)} %pad_maximum_fusion.1), channel_id=1, source_target_pairs={{0,252},{4,0},{8,4},{12,8},{16,12},{20,16},{24,20},{28,24},{32,28}... | collective-permute-start | bytes 196616 | tf_op jit(solution)/shard_map/ppermute | solution.py:373
  40.8 1.3 %collective-permute-done.5.after_ref = bf16[4,64,128]{2,1,0:T(8,128)(2,1)S(1)} collective-permute-done((bf16[4,64,128]{2,1,0:T(8,128)(2,1)S(1)}, bf16[4,64,128]{2,1,0:T(8,128)(2,1)S(1)}, u32[]{:S(2)}, u32[]{:S(2)}) %collective-permute-start.5) | collective-permute-done | bytes 65568 | tf_op jit(solution)/shard_map/ppermute | solution.py:373
  42.2 0.0 collective-permute-done.4.before_ref
  42.2 0.0 copy-done.1
  42.2 0.0 copy-done.2
  42.2 0.6 copy-done.6
  42.8 0.1 copy-done.5
  42.9 8.1 %layer.1 = (f32[4,2,2,256]{3,2,1,0:T(2,128)}, bf16[64,16,128]{2,1,0:T(8,128)(2,1)}) custom-call(s32[1]{0:T(128)} %bitcast.x0_ref, s32[1]{0:T(128)} %bitcast.1.z0_ref, s32[4,4]{1,0:T(4,128)} %pat_ref.1, s32[4]{0:T(128)} %par_ref.1, bf16[4,96,128]{2,1,0:T(8,128)(2,1)} %copy-done.5, bf16[128,128]{1,0:T(8,128)(2,1)} %copy-done.1, ...), custom_call_target="tpu_custom_call" | custom-call | tf_op jit(solution)/shard_map/layer/pallas_call | solution.py:359
  50.9 11.0 %all-to-all-start = ((bf16[256,4,128]{2,1,0:T(4,128)(2,1)}), bf16[256,4,128]{2,1,0:T(4,128)(2,1)S(1)}, u32[]{:S(2)}, u32[]{:S(2)}) async-start(bf16[256,4,128]{2,1,0:T(4,128)(2,1)} %bitcast.29), calls=%async_computation | async-start | bytes 524288 | tf_op jit(solution)/shard_map/all_to_all | solution.py:419
  61.9 15.6 %all-to-all-done.in_ref = bf16[256,4,128]{2,1,0:T(4,128)(2,1)S(1)} async-done(((bf16[256,4,128]{2,1,0:T(4,128)(2,1)}), bf16[256,4,128]{2,1,0:T(4,128)(2,1)S(1)}, u32[]{:S(2)}, u32[]{:S(2)}) %all-to-all-start) | async-done | bytes 262176 | tf_op jit(solution)/shard_map/all_to_all | solution.py:419
  77.5 0.7 copy-done
  78.2 2.1 %total.1 = bf16[256,4,128]{2,1,0:T(4,128)(2,1)} custom-call(s32[1]{0:T(128)} %bitcast.13.me_ref, bf16[256,4,128]{2,1,0:T(4,128)(2,1)} %copy-done), custom_call_target="tpu_custom_call" | custom-call | tf_op jit(solution)/shard_map/total/pallas_call | solution.py:359
  80.4 22.4 %all_to_all.10 = bf16[256,4,128]{2,1,0:T(4,128)(2,1)} all-to-all(bf16[256,4,128]{2,1,0:T(4,128)(2,1)} %total.1), channel_id=1, replica_groups=mesh['xy'=64,'gz'=4] {'xy','gz'}, dimensions={0} | all-to-all | bytes 524288 | tf_op jit(solution)/shard_map/all_to_all | solution.py:422
  102.7 2.8 %expand.1 = (f32[48,64,81]{2,1,0:T(8,128)}, f32[1,64]{1,0:T(1,128)}, f32[4,64]{1,0:T(4,128)}) custom-call(bf16[64,16,128]{2,1,0:T(8,128)(2,1)} %bitcast.27, bf16[6,144,512]{2,1,0:T(8,128)(2,1)} %constant.18.clone.spread_ref), custom_call_target="tpu_custom_call" | custom-call | tf_op jit(solution)/shard_map/expand/pallas_call | solution.py:359
  (12 shorter events, 0.0 us)
Async XLA Ops:
  2.8 18.2 %collective-permute-start = (bf16[10,54,128]{2,1,0:T(8,128)(2,1)}, bf16[10,54,128]{2,1,0:T(8,128)(2,1)S(1)}, u32[]{:S(2)}, u32[]{:S(2)}) collective-permute-start(bf16[10,54,128]{2,1,0:T(8,128)(2,1)} %get-tuple-element.23), channel_id=1, source_target_pairs={{0,252},{4,0},{8,4},{12,8},{16,12},{20,16},{24,20},{28,24},{32,28}... | collective-permute-start | bytes 414728 | tf_op jit(solution)/shard_map/ppermute | solution.py:373
  14.1 6.9 %collective-permute-start.1 = (bf16[10,54,128]{2,1,0:T(8,128)(2,1)}, bf16[10,54,128]{2,1,0:T(8,128)(2,1)S(1)}, u32[]{:S(2)}, u32[]{:S(2)}) collective-permute-start(bf16[10,54,128]{2,1,0:T(8,128)(2,1)} %get-tuple-element.24), channel_id=1, source_target_pairs={{0,3},{1,0},{2,1},{3,2},{4,7},{5,4},{6,5},{7,6},{8,11},{9,8},{10,9... | collective-permute-start | bytes 414728 | tf_op jit(solution)/shard_map/ppermute | solution.py:373
  21.0 0.6 copy-start.3
  21.0 0.7 copy-start.4
  26.1 2.2 %collective-permute-start.2 = (bf16[128,128]{1,0:T(8,128)(2,1)}, bf16[128,128]{1,0:T(8,128)(2,1)S(1)}, u32[]{:S(2)}, u32[]{:S(2)}) collective-permute-start(bf16[128,128]{1,0:T(8,128)(2,1)} %get-tuple-element.33.z2_own), channel_id=1, source_target_pairs={{0,1},{1,2},{2,3},{3,0},{4,5},{5,6},{6,7},{7,4},{8,9},{9,10},{10,1... | collective-permute-start | bytes 98312 | tf_op jit(solution)/shard_map/ppermute | solution.py:373
  27.0 5.0 %collective-permute-start.3 = (bf16[128,128]{1,0:T(8,128)(2,1)}, bf16[128,128]{1,0:T(8,128)(2,1)S(1)}, u32[]{:S(2)}, u32[]{:S(2)}) collective-permute-start(bf16[128,128]{1,0:T(8,128)(2,1)} %get-tuple-element.32.z1_own), channel_id=1, source_target_pairs={{0,3},{1,0},{2,1},{3,2},{4,7},{5,4},{6,5},{7,6},{8,11},{9,8},{10,9... | collective-permute-start | bytes 98312 | tf_op jit(solution)/shard_map/ppermute | solution.py:373
  28.4 13.8 %copy-start.1 = (bf16[128,128]{1,0:T(8,128)(2,1)}, bf16[128,128]{1,0:T(8,128)(2,1)S(1)}, u32[]{:S(2)}) copy-start(bf16[128,128]{1,0:T(8,128)(2,1)S(1)} %collective-permute-done.2.z0_own) | copy-start | bytes 98308
  32.0 10.2 %copy-start.2 = (bf16[128,128]{1,0:T(8,128)(2,1)}, bf16[128,128]{1,0:T(8,128)(2,1)S(1)}, u32[]{:S(2)}) copy-start(bf16[128,128]{1,0:T(8,128)(2,1)S(1)} %collective-permute-done.3.z3_own) | copy-start | bytes 98308
  32.0 10.1 %collective-permute-start.4 = (bf16[4,96,128]{2,1,0:T(8,128)(2,1)S(1)}, bf16[4,96,128]{2,1,0:T(8,128)(2,1)S(1)}, u32[]{:S(2)}, u32[]{:S(2)}) collective-permute-start(bf16[4,96,128]{2,1,0:T(8,128)(2,1)S(1)} %pad_maximum_fusion), channel_id=1, source_target_pairs={{0,4},{4,8},{8,12},{12,16},{16,20},{20,24},{24,28},{28,32},{32,36}... | collective-permute-start | bytes 294920 | tf_op jit(solution)/shard_map/ppermute | solution.py:373
  33.6 8.6 %collective-permute-start.5 = (bf16[4,64,128]{2,1,0:T(8,128)(2,1)S(1)}, bf16[4,64,128]{2,1,0:T(8,128)(2,1)S(1)}, u32[]{:S(2)}, u32[]{:S(2)}) collective-permute-start(bf16[4,64,128]{2,1,0:T(8,128)(2,1)S(1)} %pad_maximum_fusion.1), channel_id=1, source_target_pairs={{0,252},{4,0},{8,4},{12,8},{16,12},{20,16},{24,20},{28,24},{32,28}... | collective-permute-start | bytes 196616 | tf_op jit(solution)/shard_map/ppermute | solution.py:373
  42.2 0.6 copy-start.6
  42.2 0.7 copy-start.5
  50.9 26.6 %all-to-all-start = ((bf16[256,4,128]{2,1,0:T(4,128)(2,1)}), bf16[256,4,128]{2,1,0:T(4,128)(2,1)S(1)}, u32[]{:S(2)}, u32[]{:S(2)}) async-start(bf16[256,4,128]{2,1,0:T(4,128)(2,1)} %bitcast.29), calls=%async_computation | async-start | bytes 524288 | tf_op jit(solution)/shard_map/all_to_all | solution.py:419
  77.5 0.7 copy-start

commit v6 on v5

--- a/solution.py
+++ b/solution.py
@@ -1,3 +1,4 @@
+import functools
 import math
 
 import jax
@@ -79,10 +80,6 @@
     small_ref[...] = jnp.concatenate([head_ref[...], bias_ref[...], jnp.zeros((3, 64), F32)], axis=0).T
 
 
-def place(c, x):
-    return 64 + 5 * c if x == 1 else (32 + 5 * c if c < 6 else 5 * (c - 6))
-
-
 def run(copies):
     for copy in copies:
         copy.start()
@@ -115,17 +112,23 @@
             z_ref[at] = jnp.concatenate([first, last], axis=0).astype(BF16)
 
 
-def loops_body(
-    links_ref, xh_ref, zh_ref, o0_ref, o1_ref, l_ref, xs_ref, zs_ref, pq_ref, tile_ref, sems
-):
+def loops_body(planes, *refs):
+    if 0 in planes:
+        links_ref, z_edge, x_edge, low_in, high_in, o0_ref, o1_ref, l_ref = refs[:8]
+        zs_ref, xs_ref, pq_ref, tile_ref, sems = refs[8:]
+        o0_ref[64:128] = low_in[...]
+        o1_ref[64:128] = high_in[...]
+    else:
+        links_ref, z_edge, o0_ref, o1_ref, l_ref, zs_ref, pq_ref, tile_ref, sems = refs
     copies = fetch(links_ref, l_ref, sems, 6)
     for copy in copies:
         copy.start()
     for tau in range(5):
         for half in range(2):
             at = tau * 2 + half
-            xs_ref[pl.ds(tau * 4 + half * 2 + 1, 54, stride=24), :] = xh_ref[at].astype(F32)
-            zs_ref[pl.ds(tau * 4 + 2 + half, 54, stride=24), :] = zh_ref[at].astype(F32)
+            zs_ref[pl.ds(tau * 4 + 2 + half, 54, stride=24), :] = z_edge[at].astype(F32)
+            if 0 in planes:
+                xs_ref[pl.ds(tau * 4 + half * 2 + 1, 54, stride=24), :] = x_edge[at].astype(F32)
     tile_ref[...] = jnp.zeros_like(tile_ref)
     for copy in copies:
         copy.wait()
@@ -172,7 +175,9 @@
         return re, im
 
     for k in range(3):
-        for p, (mu, nu) in enumerate(plane_pairs):
+        for p in planes:
+            mu, nu = plane_pairs[p]
+            c = 2 * (p - planes[0])
             u_mu = at_site(mu, k)
             u_nu = at_site(nu, k)
             nu_ahead = ahead(nu, mu, k)
@@ -186,36 +191,47 @@
                     im_term = i1 * r2 - r1 * i2
                     re = re_term if re is None else re + re_term
                     im = im_term if im is None else im + im_term
-            pq_ref[2 * p, 8 * k : 8 * k + 8, :] = re
-            pq_ref[2 * p + 1, 8 * k : 8 * k + 8, :] = im
-    for c in range(12):
-        for lb, o_ref in enumerate((o0_ref, o1_ref)):
+            pq_ref[c, 8 * k : 8 * k + 8, :] = re
+            pq_ref[c + 1, 8 * k : 8 * k + 8, :] = im
+    for c in range(6):
+        for lb in range(2):
             for x in range(2):
-                row = place(c, x)
+                row = 32 * x + 5 * c
                 tile_ref[lb, row : row + 5, :] = pq_ref[c, pl.ds(2 * lb + x, 5, stride=4), :]
-    o0_ref[...] = tile_ref[0].astype(BF16)
-    o1_ref[...] = tile_ref[1].astype(BF16)
+    o0_ref[0:64] = tile_ref[0].astype(BF16)
+    o1_ref[0:64] = tile_ref[1].astype(BF16)
+
+
+def join_body(*refs):
+    right_ref, left_ref, own_ref = refs[4:]
+    for i in range(4):
+        right_ref[i, 0:64] = refs[i][0:64]
+        right_ref[i, 64:96] = refs[i][96:128]
+        left_ref[i, 0:32] = refs[i][64:96]
+        left_ref[i, 32:64] = refs[i][0:32]
+        own_ref[i] = refs[i][...]
 
 
 def layer_body(
-    x0_ref, z0_ref, pat_ref, par_ref, before_ref, z0_own, z1_own, z2_own, z3_own, after_ref, w_ref, small_ref,
-    keep_ref, cot_ref, coef_ref, g_ref, a_ref, low_ref, rows_ref, left_ref, own_ref, right_ref,
+    x0_ref, z0_ref, pat_ref, par_ref, before_in, own_in, after_in, w_ref, small_ref, keep_ref, cot_ref,
+    coef_ref, g_ref, a_ref, low_ref, rows_ref, before_ref, own_ref, after_ref,
 ):
-    left_ref[...] = before_ref[...].astype(F32)
-    right_ref[...] = after_ref[...].astype(F32)
-    for i, ref in enumerate((z0_own, z1_own, z2_own, z3_own)):
-        own_ref[i] = ref[...].astype(F32)
+    before_ref[...] = before_in[...].astype(F32)
+    own_ref[...] = own_in[...].astype(F32)
+    after_ref[...] = after_in[...].astype(F32)
 
     def piece(i, x, c, t):
-        if x == 0 and c >= 6:
+        with_x = c < 6
+        row = 5 * (c % 6) + t
+        if x == 0 and not with_x:
             return jnp.zeros((4, 128), F32)
         if x < 2:
-            ref, row = left_ref, place(c, x) - 32
+            ref, row = before_ref, row + (32 * x if with_x else 64)
         elif x < 4:
-            ref, row = own_ref, place(c, x - 2)
+            ref, row = own_ref, row + 32 * (x - 2) + (0 if with_x else 64)
         else:
-            ref, row = right_ref, place(c, 0)
-        return ref[i, row + t : row + t + 4, :]
+            ref, row = after_ref, row + (32 if with_x else 0)
+        return ref[i, row : row + 4, :]
 
     lane = lanes((8, 128))
     upper = lane >= LY
@@ -389,28 +405,33 @@
         weights_body, (shape((12, 128, 256), BF16), shape((64, 8), F32)), [],
         conv_weight.transpose(1, 2, 0), spread, keep, head_weight.T, conv_bias[None], name="weights",
     )
-    next_x, next_z, weights, small = lax.optimization_barrier((next_x, next_z, weights, small))
-    half = shape((128, 128), BF16)
     border = pltpu.VMEM((57 * 24, 128), F32)
-    low_z, high_z = call(
-        loops_body, (half, half),
-        [links, border, border, pltpu.VMEM((14, 24, 128), F32), pltpu.VMEM((2, 128, 128), F32), sems((12,))],
-        gauge_links, next_x, next_z, away=(0,), name="loops",
-    )
-    before_z = shifted(high_z, "gz", 1)
-    after_z = shifted(low_z, "gz", -1)
-    layers = [before_z, low_z, high_z, after_z]
-    right_going = jnp.stack([v[32:] for v in layers])
+
+    def loops(planes, *edges):
+        half = shape((128 if 0 in planes else 64, 128), BF16)
+        return call(
+            functools.partial(loops_body, planes), (half, half),
+            [links] + ([border, border] if 0 in planes else [border])
+            + [pltpu.VMEM((8, 24, 128), F32), pltpu.VMEM((2, 64, 128), F32), sems((12,))],
+            gauge_links, *edges, away=(0,), name="loops",
+        )
+
+    without_x = loops((3, 4, 5), next_z)
+    next_x, weights, small, *without_x = lax.optimization_barrier((next_x, weights, small, *without_x))
+    low_z, high_z = loops((0, 1, 2), next_z, next_x, *without_x)
+    right_going, left_going, block = call(
+        join_body, tuple(shape((4, n, 128), BF16) for n in (96, 64, 128)), [],
+        shifted(high_z, "gz", 1), low_z, high_z, shifted(low_z, "gz", -1), name="join",
+    )
     before_x = shifted(right_going, "xy", 1)
-    held = lax.optimization_barrier((right_going, *layers))
-    after_x = shifted(jnp.stack([v[:64] for v in held[1:]]), "xy", -1)
+    after_x = shifted(left_going, "xy", -1)
     x_first = (lax.axis_index("xy") * 2).reshape(1)
     z_first = (lax.axis_index("gz") * 4).reshape(1)
     coefficients, grads = call(
         layer_body, (shape((4, 2, 2, 256), F32), shape((64, 16, 128), BF16)),
         [pltpu.VMEM((12, 256, 1024), BF16), pltpu.VMEM((64, 1024), BF16), pltpu.VMEM((1024, 128), F32)]
         + [pltpu.VMEM((4, n, 128), F32) for n in (96, 128, 64)],
-        x_first, z_first, pattern, link_parity, before_x, *layers, after_x, weights, small, keep, cotangent,
+        x_first, z_first, pattern, link_parity, before_x, block, after_x, weights, small, keep, cotangent,
         smem=4, name="layer",
     )
     both = ("xy", "gz")

time: 106 us -> 110 us (1.038)
  Pallas kernels: 25.6 us -> 30 us
    pallas_call x6 -> x8, Pallas kernels: 25.6 us -> 30 us  [call(): pl.pallas_call(body, out_shape=outs, in_specs=specs + [spec(i, away) for...]
    another operation x7 -> x0, local copies, waits for them, and re-layouts: 2.22 us -> none  [the longest x4 1.44 us: per_device(): after_x = shifted(jnp.stack([v[:64] for v in held[1:]]), 'xy', -1)]
    unnamed x14, local copies, waits for them, and re-layouts: 2.05 us -> 3.25 us
  transfers between devices with their start and end apart: 7 -> 7, of which waited for: 4 -> 5; matrix products, arithmetic and copies ran while one was open for 2% -> 0% of each run, Pallas kernels for 6% -> 9%
where the time goes in v6:
time: 110 us; the launch traced here: 109 us
  starting transfers between devices  31.7 us (29%)
  Pallas kernels  30 us (27%)
  blocking collectives  22.3 us (20%)
  waiting for transfers between devices  21 us (19%)
  local copies, waits for them, and re-layouts  3.25 us (3%)
    pallas_call x8, Pallas kernels, call(): pl.pallas_call(body, out_shape=outs, in_specs=specs + [spec(i, away) for...  30 us
    all_to_all x1, blocking collectives, per_device(): chunks = lax.all_to_all(chunks, both, 0, 0, tiled=True)  22.3 us
    ppermute x6, starting transfers between devices, shifted(): return lax.ppermute(x, axis, [(i, (i + by) % count) for i in range(count)])  20.3 us
    all_to_all x1, waiting for transfers between devices, per_device(): chunks = lax.all_to_all(chunks, both, 0, 0, tiled=True)  15.6 us
    all_to_all x1, starting transfers between devices, per_device(): chunks = lax.all_to_all(chunks, both, 0, 0, tiled=True)  11.3 us
    ppermute x6, waiting for transfers between devices, shifted(): return lax.ppermute(x, axis, [(i, (i + by) % count) for i in range(count)])  5.41 us
    unnamed x14, local copies, waits for them, and re-layouts  3.25 us
  transfers between devices with their start and end apart: 7, of which 5 were waited for; matrix products, arithmetic and copies ran while one was open for 0% of the time, Pallas kernels for 9%

profile of v6, /device:TPU:1, one launch (start us, length us, event | category | flops | bytes accessed | tf_op | source)
XLA Modules:
  0.0 108.9 jit_solution(10928999895260706292)
XLA Ops:
  0.6 2.1 %send.1 = (bf16[10,54,128]{2,1,0:T(8,128)(2,1)}, bf16[10,54,128]{2,1,0:T(8,128)(2,1)}) custom-call(f32[4,2,3,3,6,2,256]{6,5,4,3,2,1,0:T(2,128)} %refs_0_.3), custom_call_target="tpu_custom_call" | custom-call | tf_op jit(solution)/shard_map/send/pallas_call | solution.py:375
  2.8 3.3 %collective-permute-start = (bf16[10,54,128]{2,1,0:T(8,128)(2,1)}, bf16[10,54,128]{2,1,0:T(8,128)(2,1)S(1)}, u32[]{:S(2)}, u32[]{:S(2)}) collective-permute-start(bf16[10,54,128]{2,1,0:T(8,128)(2,1)} %get-tuple-element.25), channel_id=1, source_target_pairs={{0,3},{1,0},{2,1},{3,2},{4,7},{5,4},{6,5},{7,6},{8,11},{9,8},{10,9... | collective-permute-start | bytes 414728 | tf_op jit(solution)/shard_map/ppermute | solution.py:389
  6.1 8.7 %collective-permute-start.1 = (bf16[10,54,128]{2,1,0:T(8,128)(2,1)}, bf16[10,54,128]{2,1,0:T(8,128)(2,1)S(1)}, u32[]{:S(2)}, u32[]{:S(2)}) collective-permute-start(bf16[10,54,128]{2,1,0:T(8,128)(2,1)} %get-tuple-element.26), channel_id=1, source_target_pairs={{0,252},{4,0},{8,4},{12,8},{16,12},{20,16},{24,20},{28,24},{32,28}... | collective-permute-start | bytes 414728 | tf_op jit(solution)/shard_map/ppermute | solution.py:389
  14.8 5.9 %weights.1 = (bf16[12,128,256]{2,1,0:T(8,128)(2,1)}, f32[64,8]{1,0:T(8,128)}) custom-call(bf16[48,64,81]{2,1,0:T(8,128)(2,1)} %bitcast.12, bf16[6,144,512]{2,1,0:T(8,128)(2,1)} %constant.18.clone.spread_ref, bf16[1168,256]{1,0:T(8,128)(2,1)} %constant.17.clone.keep_ref, f32[4,64]{1,0:T(4,128)} %bitcast.14, f32[1,64]{1,0:T(1,128)} %bitcast.15), custom_call_target="tpu_custom_call" | custom-call | tf_op jit(solution)/shard_map/weights/pallas_call | solution.py:375
  20.7 0.0 collective-permute-done.refs_1_
  20.7 0.0 copy-start.1
  20.7 0.7 copy-done.1
  21.4 3.7 %loops.2 = (bf16[64,128]{1,0:T(8,128)(2,1)}, bf16[64,128]{1,0:T(8,128)(2,1)}) custom-call(f32[4,2,3,3,6,2,256]{6,5,4,3,2,1,0:T(2,128)} %refs_0_.3, bf16[10,54,128]{2,1,0:T(8,128)(2,1)} %copy-done.1), custom_call_target="tpu_custom_call" | custom-call | tf_op jit(solution)/shard_map/loops/pallas_call | solution.py:375
  25.1 0.0 collective-permute-done.1.refs_2_
  25.1 0.0 copy-start.2
  25.1 0.6 copy-done.2
  25.7 3.7 %loops.3 = (bf16[128,128]{1,0:T(8,128)(2,1)}, bf16[128,128]{1,0:T(8,128)(2,1)}) custom-call(f32[4,2,3,3,6,2,256]{6,5,4,3,2,1,0:T(2,128)} %refs_0_.3, bf16[10,54,128]{2,1,0:T(8,128)(2,1)} %copy-done.1, bf16[10,54,128]{2,1,0:T(8,128)(2,1)} %copy-done.2, bf16[64,128]{1,0:T(8,128)(2,1)} %get-tuple-element.32.refs_3_, bf16[64,128]{1,0:T(8,128)(2,1)} %get-tuple-element.33.refs_4_), custom_call_target="tpu_custom_call" | custom-call | tf_op jit(solution)/shard_map/loops/pallas_call | solution.py:375
  29.5 0.8 collective-permute-start.2
  30.3 0.3 collective-permute-start.3
  30.6 1.0 collective-permute-done.2.refs_0_
  31.6 2.2 %collective-permute-done.3.refs_3_ = bf16[128,128]{1,0:T(8,128)(2,1)S(1)} collective-permute-done((bf16[128,128]{1,0:T(8,128)(2,1)}, bf16[128,128]{1,0:T(8,128)(2,1)S(1)}, u32[]{:S(2)}, u32[]{:S(2)}) %collective-permute-start.3) | collective-permute-done | bytes 32800 | tf_op jit(solution)/shard_map/ppermute | solution.py:389
  33.9 0.0 copy-done.5
  33.9 0.6 copy-done.6
  34.5 1.6 %join.1 = (bf16[4,96,128]{2,1,0:T(8,128)(2,1)}, bf16[4,64,128]{2,1,0:T(8,128)(2,1)}, bf16[4,128,128]{2,1,0:T(8,128)(2,1)}) custom-call(bf16[128,128]{1,0:T(8,128)(2,1)} %copy-done.5, bf16[128,128]{1,0:T(8,128)(2,1)} %get-tuple-element.35.refs_1_, bf16[128,128]{1,0:T(8,128)(2,1)} %get-tuple-element.34.refs_2_, bf16[128,128]{1,0:T(8,128)(2,1)} %copy-done.6), custom_call_target="tpu_custom_call" | custom-call | tf_op jit(solution)/shard_map/join/pallas_call | solution.py:375
  36.0 0.0 collective-permute-start.4
  36.0 7.2 %collective-permute-start.5 = (bf16[4,64,128]{2,1,0:T(8,128)(2,1)}, bf16[4,64,128]{2,1,0:T(8,128)(2,1)S(1)}, u32[]{:S(2)}, u32[]{:S(2)}) collective-permute-start(bf16[4,64,128]{2,1,0:T(8,128)(2,1)} %get-tuple-element.38), channel_id=1, source_target_pairs={{0,252},{4,0},{8,4},{12,8},{16,12},{20,16},{24,20},{28,24},{32,28}... | collective-permute-start | bytes 196616 | tf_op jit(solution)/shard_map/ppermute | solution.py:389
  43.2 1.6 %collective-permute-done.5.after_in = bf16[4,64,128]{2,1,0:T(8,128)(2,1)S(1)} collective-permute-done((bf16[4,64,128]{2,1,0:T(8,128)(2,1)}, bf16[4,64,128]{2,1,0:T(8,128)(2,1)S(1)}, u32[]{:S(2)}, u32[]{:S(2)}) %collective-permute-start.5) | collective-permute-done | bytes 65568 | tf_op jit(solution)/shard_map/ppermute | solution.py:389
  44.9 0.6 collective-permute-done.4.before_in
  45.4 0.1 copy-done.4
  45.5 0.6 copy-done.3
  46.0 7.9 %layer.1 = (f32[4,2,2,256]{3,2,1,0:T(2,128)}, bf16[64,16,128]{2,1,0:T(8,128)(2,1)}) custom-call(s32[1]{0:T(128)} %bitcast.x0_ref, s32[1]{0:T(128)} %bitcast.1.z0_ref, s32[4,4]{1,0:T(4,128)} %pat_ref.1, s32[4]{0:T(128)} %par_ref.1, bf16[4,96,128]{2,1,0:T(8,128)(2,1)} %copy-done.3, bf16[4,128,128]{2,1,0:T(8,128)(2,1)} %get-tuple-element.37.own_in, ...), custom_call_target="tpu_custom_call" | custom-call | tf_op jit(solution)/shard_map/layer/pallas_call | solution.py:375
  54.0 11.3 %all-to-all-start = ((bf16[256,4,128]{2,1,0:T(4,128)(2,1)}), bf16[256,4,128]{2,1,0:T(4,128)(2,1)S(1)}, u32[]{:S(2)}, u32[]{:S(2)}) async-start(bf16[256,4,128]{2,1,0:T(4,128)(2,1)} %bitcast.13), calls=%async_computation | async-start | bytes 524288 | tf_op jit(solution)/shard_map/all_to_all | solution.py:440
  65.3 15.6 %all-to-all-done.in_ref = bf16[256,4,128]{2,1,0:T(4,128)(2,1)S(1)} async-done(((bf16[256,4,128]{2,1,0:T(4,128)(2,1)}), bf16[256,4,128]{2,1,0:T(4,128)(2,1)S(1)}, u32[]{:S(2)}, u32[]{:S(2)}) %all-to-all-start) | async-done | bytes 262176 | tf_op jit(solution)/shard_map/all_to_all | solution.py:440
  80.9 0.7 copy-done
  81.6 2.1 %total.1 = bf16[256,4,128]{2,1,0:T(4,128)(2,1)} custom-call(s32[1]{0:T(128)} %bitcast.5.me_ref, bf16[256,4,128]{2,1,0:T(4,128)(2,1)} %copy-done), custom_call_target="tpu_custom_call" | custom-call | tf_op jit(solution)/shard_map/total/pallas_call | solution.py:375
  83.7 22.3 %all_to_all.10 = bf16[256,4,128]{2,1,0:T(4,128)(2,1)} all-to-all(bf16[256,4,128]{2,1,0:T(4,128)(2,1)} %total.1), channel_id=1, replica_groups=mesh['xy'=64,'gz'=4] {'xy','gz'}, dimensions={0} | all-to-all | bytes 524288 | tf_op jit(solution)/shard_map/all_to_all | solution.py:443
  106.1 2.8 %expand.1 = (f32[48,64,81]{2,1,0:T(8,128)}, f32[1,64]{1,0:T(1,128)}, f32[4,64]{1,0:T(4,128)}) custom-call(bf16[64,16,128]{2,1,0:T(8,128)(2,1)} %bitcast.11, bf16[6,144,512]{2,1,0:T(8,128)(2,1)} %constant.18.clone.spread_ref), custom_call_target="tpu_custom_call" | custom-call | tf_op jit(solution)/shard_map/expand/pallas_call | solution.py:375
  (5 shorter events, 0.0 us)
Async XLA Ops:
  2.8 17.9 %collective-permute-start = (bf16[10,54,128]{2,1,0:T(8,128)(2,1)}, bf16[10,54,128]{2,1,0:T(8,128)(2,1)S(1)}, u32[]{:S(2)}, u32[]{:S(2)}) collective-permute-start(bf16[10,54,128]{2,1,0:T(8,128)(2,1)} %get-tuple-element.25), channel_id=1, source_target_pairs={{0,3},{1,0},{2,1},{3,2},{4,7},{5,4},{6,5},{7,6},{8,11},{9,8},{10,9... | collective-permute-start | bytes 414728 | tf_op jit(solution)/shard_map/ppermute | solution.py:389
  6.1 19.0 %collective-permute-start.1 = (bf16[10,54,128]{2,1,0:T(8,128)(2,1)}, bf16[10,54,128]{2,1,0:T(8,128)(2,1)S(1)}, u32[]{:S(2)}, u32[]{:S(2)}) collective-permute-start(bf16[10,54,128]{2,1,0:T(8,128)(2,1)} %get-tuple-element.26), channel_id=1, source_target_pairs={{0,252},{4,0},{8,4},{12,8},{16,12},{20,16},{24,20},{28,24},{32,28}... | collective-permute-start | bytes 414728 | tf_op jit(solution)/shard_map/ppermute | solution.py:389
  20.7 0.7 copy-start.1
  25.1 0.7 copy-start.2
  29.5 2.2 %collective-permute-start.2 = (bf16[128,128]{1,0:T(8,128)(2,1)}, bf16[128,128]{1,0:T(8,128)(2,1)S(1)}, u32[]{:S(2)}, u32[]{:S(2)}) collective-permute-start(bf16[128,128]{1,0:T(8,128)(2,1)} %get-tuple-element.34.refs_2_), channel_id=1, source_target_pairs={{0,1},{1,2},{2,3},{3,0},{4,5},{5,6},{6,7},{7,4},{8,9},{9,10},{10,1... | collective-permute-start | bytes 98312 | tf_op jit(solution)/shard_map/ppermute | solution.py:389
  30.3 3.6 %collective-permute-start.3 = (bf16[128,128]{1,0:T(8,128)(2,1)}, bf16[128,128]{1,0:T(8,128)(2,1)S(1)}, u32[]{:S(2)}, u32[]{:S(2)}) collective-permute-start(bf16[128,128]{1,0:T(8,128)(2,1)} %get-tuple-element.35.refs_1_), channel_id=1, source_target_pairs={{0,3},{1,0},{2,1},{3,2},{4,7},{5,4},{6,5},{7,6},{8,11},{9,8},{10,9... | collective-permute-start | bytes 98312 | tf_op jit(solution)/shard_map/ppermute | solution.py:389
  31.6 2.2 %copy-start.5 = (bf16[128,128]{1,0:T(8,128)(2,1)}, bf16[128,128]{1,0:T(8,128)(2,1)S(1)}, u32[]{:S(2)}) copy-start(bf16[128,128]{1,0:T(8,128)(2,1)S(1)} %collective-permute-done.2.refs_0_) | copy-start | bytes 98308
  33.9 0.6 copy-start.6
  36.0 9.4 %collective-permute-start.4 = (bf16[4,96,128]{2,1,0:T(8,128)(2,1)}, bf16[4,96,128]{2,1,0:T(8,128)(2,1)S(1)}, u32[]{:S(2)}, u32[]{:S(2)}) collective-permute-start(bf16[4,96,128]{2,1,0:T(8,128)(2,1)} %get-tuple-element.36), channel_id=1, source_target_pairs={{0,4},{4,8},{8,12},{12,16},{16,20},{20,24},{24,28},{28,32},{32,36}... | collective-permute-start | bytes 294920 | tf_op jit(solution)/shard_map/ppermute | solution.py:389
  36.0 8.8 %collective-permute-start.5 = (bf16[4,64,128]{2,1,0:T(8,128)(2,1)}, bf16[4,64,128]{2,1,0:T(8,128)(2,1)S(1)}, u32[]{:S(2)}, u32[]{:S(2)}) collective-permute-start(bf16[4,64,128]{2,1,0:T(8,128)(2,1)} %get-tuple-element.38), channel_id=1, source_target_pairs={{0,252},{4,0},{8,4},{12,8},{16,12},{20,16},{24,20},{28,24},{32,28}... | collective-permute-start | bytes 196616 | tf_op jit(solution)/shard_map/ppermute | solution.py:389
  44.9 0.6 copy-start.4
  45.4 0.6 copy-start.3
  54.0 26.9 %all-to-all-start = ((bf16[256,4,128]{2,1,0:T(4,128)(2,1)}), bf16[256,4,128]{2,1,0:T(4,128)(2,1)S(1)}, u32[]{:S(2)}, u32[]{:S(2)}) async-start(bf16[256,4,128]{2,1,0:T(4,128)(2,1)} %bitcast.13), calls=%async_computation | async-start | bytes 524288 | tf_op jit(solution)/shard_map/all_to_all | solution.py:440
  80.9 0.7 copy-start

commit v7 on v5

--- a/solution.py
+++ b/solution.py
@@ -80,7 +80,11 @@
 
 
 def place(c, x):
-    return 64 + 5 * c if x == 1 else (32 + 5 * c if c < 6 else 5 * (c - 6))
+    return 64 + 32 * (c // 6) + 5 * (c % 6) if x == 1 else (32 + 5 * c if c < 6 else 5 * (c - 6))
+
+
+def group(g):
+    return slice(32 * g, 32 * g + 32)
 
 
 def run(copies):
@@ -198,13 +202,13 @@
 
 
 def layer_body(
-    x0_ref, z0_ref, pat_ref, par_ref, before_ref, z0_own, z1_own, z2_own, z3_own, after_ref, w_ref, small_ref,
-    keep_ref, cot_ref, coef_ref, g_ref, a_ref, low_ref, rows_ref, left_ref, own_ref, right_ref,
+    odd_ref, x0_ref, z0_ref, pat_ref, par_ref, second_in, own_in, first_in, w_ref, small_ref, keep_ref, cot_ref,
+    coef_ref, g_ref, a_ref, low_ref, rows_ref, left_ref, own_ref, right_ref,
 ):
-    left_ref[...] = before_ref[...].astype(F32)
-    right_ref[...] = after_ref[...].astype(F32)
-    for i, ref in enumerate((z0_own, z1_own, z2_own, z3_own)):
-        own_ref[i] = ref[...].astype(F32)
+    odd = odd_ref[0] == 1
+    own_ref[...] = own_in[...].astype(F32)
+    left_ref[...] = jnp.where(odd, second_in[:, 32:].astype(F32), first_in[:, 32:].astype(F32))
+    right_ref[...] = jnp.where(odd, first_in[:, :64].astype(F32), second_in[:, :64].astype(F32))
 
     def piece(i, x, c, t):
         if x == 0 and c >= 6:
@@ -373,6 +377,12 @@
     return lax.ppermute(x, axis, [(i, (i + by) % count) for i in range(count)])
 
 
+def swapped(x, axis, least):
+    count = lax.axis_size(axis)
+    pairs = [(i % count, (i + 1) % count) for i in range(least, least + count, 2)]
+    return lax.ppermute(x, axis, pairs + [(j, i) for i, j in pairs])
+
+
 def per_device(gauge_links, pattern, link_parity, conv_weight, conv_bias, head_weight, cotangent):
     shape = jax.ShapeDtypeStruct
     sems = pltpu.SemaphoreType.DMA
@@ -391,6 +401,7 @@
     )
     next_x, next_z, weights, small = lax.optimization_barrier((next_x, next_z, weights, small))
     half = shape((128, 128), BF16)
+    odd = (lax.axis_index("xy") % 2).reshape(1)
     border = pltpu.VMEM((57 * 24, 128), F32)
     low_z, high_z = call(
         loops_body, (half, half),
@@ -399,19 +410,17 @@
     )
     before_z = shifted(high_z, "gz", 1)
     after_z = shifted(low_z, "gz", -1)
-    layers = [before_z, low_z, high_z, after_z]
-    right_going = jnp.stack([v[32:] for v in layers])
-    before_x = shifted(right_going, "xy", 1)
-    held = lax.optimization_barrier((right_going, *layers))
-    after_x = shifted(jnp.stack([v[:64] for v in held[1:]]), "xy", -1)
+    block = jnp.stack([before_z, low_z, high_z, after_z])
+    first = swapped(block, "xy", 1)
+    second = swapped(block, "xy", 0)
     x_first = (lax.axis_index("xy") * 2).reshape(1)
     z_first = (lax.axis_index("gz") * 4).reshape(1)
     coefficients, grads = call(
         layer_body, (shape((4, 2, 2, 256), F32), shape((64, 16, 128), BF16)),
         [pltpu.VMEM((12, 256, 1024), BF16), pltpu.VMEM((64, 1024), BF16), pltpu.VMEM((1024, 128), F32)]
         + [pltpu.VMEM((4, n, 128), F32) for n in (96, 128, 64)],
-        x_first, z_first, pattern, link_parity, before_x, *layers, after_x, weights, small, keep, cotangent,
-        smem=4, name="layer",
+        odd, x_first, z_first, pattern, link_parity, second, block, first, weights, small, keep, cotangent,
+        smem=5, name="layer",
     )
     both = ("xy", "gz")
     count = lax.axis_size(both)

time: 106 us -> 103 us (0.972)
  starting transfers between devices: 31.5 us -> 21.8 us
  waiting for transfers between devices: 21.2 us -> 29 us
  local copies, waits for them, and re-layouts: 4.27 us -> 2.1 us
    ppermute x6 -> x4, starting transfers between devices: 20.5 us -> 13.1 us  [shifted(): return lax.ppermute(x, axis, [(i, (i + by) % count) for i in range(count)])]
    ppermute x0 -> x2, waiting for transfers between devices: none -> 7.03 us  [swapped(): return lax.ppermute(x, axis, pairs + [(j, i) for i, j in pairs])]
    all_to_all x1, starting transfers between devices: 11 us -> 6.11 us  [per_device(): chunks = lax.all_to_all(chunks, both, 0, 0, tiled=True)]
    ppermute x0 -> x2, starting transfers between devices: none -> 2.6 us  [swapped(): return lax.ppermute(x, axis, pairs + [(j, i) for i, j in pairs])]
    another operation x7 -> x0, local copies, waits for them, and re-layouts: 2.22 us -> none  [the longest x4 1.44 us: per_device(): after_x = shifted(jnp.stack([v[:64] for v in held[1:]]), 'xy', -1)]
    ppermute x6 -> x4, waiting for transfers between devices: 5.57 us -> 6.36 us  [shifted(): return lax.ppermute(x, axis, [(i, (i + by) % count) for i in range(count)])]
  transfers between devices with their start and end apart: 7 -> 7, of which waited for: 4 -> 4; matrix products, arithmetic and copies ran while one was open for 2% -> 0% of each run, Pallas kernels for 6% -> 6%
where the time goes in v7:
time: 103 us; the launch traced here: 102 us
  waiting for transfers between devices  29 us (28%)
  Pallas kernels  25.5 us (25%)
  blocking collectives  22.4 us (22%)
  starting transfers between devices  21.8 us (21%)
  local copies, waits for them, and re-layouts  2.1 us (2%)
    pallas_call x6, Pallas kernels, call(): pl.pallas_call(body, out_shape=outs, in_specs=specs + [spec(i, away) for...  25.5 us
    all_to_all x1, blocking collectives, per_device(): chunks = lax.all_to_all(chunks, both, 0, 0, tiled=True)  22.4 us
    all_to_all x1, waiting for transfers between devices, per_device(): chunks = lax.all_to_all(chunks, both, 0, 0, tiled=True)  15.6 us
    ppermute x4, starting transfers between devices, shifted(): return lax.ppermute(x, axis, [(i, (i + by) % count) for i in range(count)])  13.1 us
    ppermute x2, waiting for transfers between devices, swapped(): return lax.ppermute(x, axis, pairs + [(j, i) for i, j in pairs])  7.03 us
    ppermute x4, waiting for transfers between devices, shifted(): return lax.ppermute(x, axis, [(i, (i + by) % count) for i in range(count)])  6.36 us
    all_to_all x1, starting transfers between devices, per_device(): chunks = lax.all_to_all(chunks, both, 0, 0, tiled=True)  6.11 us
    ppermute x2, starting transfers between devices, swapped(): return lax.ppermute(x, axis, pairs + [(j, i) for i, j in pairs])  2.6 us
  transfers between devices with their start and end apart: 7, of which 4 were waited for; matrix products, arithmetic and copies ran while one was open for 0% of the time, Pallas kernels for 6%

profile of v7, /device:TPU:1, one launch (start us, length us, event | category | flops | bytes accessed | tf_op | source)
XLA Modules:
  0.0 102.3 jit_solution(14058678290461042998)
XLA Ops:
  0.6 2.1 %send.1 = (bf16[10,54,128]{2,1,0:T(8,128)(2,1)}, bf16[10,54,128]{2,1,0:T(8,128)(2,1)}) custom-call(f32[4,2,3,3,6,2,256]{6,5,4,3,2,1,0:T(2,128)} %links_ref.3), custom_call_target="tpu_custom_call" | custom-call | tf_op jit(solution)/shard_map/send/pallas_call | solution.py:363
  2.8 11.3 %collective-permute-start = (bf16[10,54,128]{2,1,0:T(8,128)(2,1)}, bf16[10,54,128]{2,1,0:T(8,128)(2,1)S(1)}, u32[]{:S(2)}, u32[]{:S(2)}) collective-permute-start(bf16[10,54,128]{2,1,0:T(8,128)(2,1)} %get-tuple-element.19), channel_id=1, source_target_pairs={{0,252},{4,0},{8,4},{12,8},{16,12},{20,16},{24,20},{28,24},{32,28}... | collective-permute-start | bytes 414728 | tf_op jit(solution)/shard_map/ppermute | solution.py:377
  14.1 1.0 collective-permute-start.1
  15.0 5.9 %weights.1 = (bf16[12,128,256]{2,1,0:T(8,128)(2,1)}, f32[64,8]{1,0:T(8,128)}) custom-call(bf16[48,64,81]{2,1,0:T(8,128)(2,1)} %bitcast.17, bf16[6,144,512]{2,1,0:T(8,128)(2,1)} %constant.29.clone.spread_ref, bf16[1168,256]{1,0:T(8,128)(2,1)} %constant.28.clone.keep_ref, f32[4,64]{1,0:T(4,128)} %bitcast.23, f32[1,64]{1,0:T(1,128)} %bitcast.24), custom_call_target="tpu_custom_call" | custom-call | tf_op jit(solution)/shard_map/weights/pallas_call | solution.py:363
  21.0 0.0 collective-permute-done.xh_ref
  21.0 0.0 copy-start.2
  21.0 0.0 collective-permute-done.1.zh_ref
  21.0 0.0 copy-start.3
  21.0 0.6 copy-done.2
  21.6 0.0 copy-done.3
  21.7 4.5 %loops.1 = (bf16[128,128]{1,0:T(8,128)(2,1)}, bf16[128,128]{1,0:T(8,128)(2,1)}) custom-call(f32[4,2,3,3,6,2,256]{6,5,4,3,2,1,0:T(2,128)} %links_ref.3, bf16[10,54,128]{2,1,0:T(8,128)(2,1)} %copy-done.2, bf16[10,54,128]{2,1,0:T(8,128)(2,1)} %copy-done.3), custom_call_target="tpu_custom_call" | custom-call | tf_op jit(solution)/shard_map/loops/pallas_call | solution.py:363
  26.2 0.9 collective-permute-start.2
  27.0 0.0 collective-permute-start.3
  27.0 1.3 %collective-permute-done.2 = bf16[128,128]{1,0:T(8,128)(2,1)S(1)} collective-permute-done((bf16[128,128]{1,0:T(8,128)(2,1)}, bf16[128,128]{1,0:T(8,128)(2,1)S(1)}, u32[]{:S(2)}, u32[]{:S(2)}) %collective-permute-start.2) | collective-permute-done | bytes 32800 | tf_op jit(solution)/shard_map/ppermute | solution.py:377
  28.4 5.0 %collective-permute-done.3 = bf16[128,128]{1,0:T(8,128)(2,1)S(1)} collective-permute-done((bf16[128,128]{1,0:T(8,128)(2,1)}, bf16[128,128]{1,0:T(8,128)(2,1)S(1)}, u32[]{:S(2)}, u32[]{:S(2)}) %collective-permute-start.3) | collective-permute-done | bytes 32800 | tf_op jit(solution)/shard_map/ppermute | solution.py:377
  33.4 0.8 pad_maximum_fusion.own_in
  34.2 0.0 copy-start.1
  34.2 2.6 %collective-permute-start.5 = (bf16[4,128,128]{2,1,0:T(8,128)(2,1)S(1)}, bf16[4,128,128]{2,1,0:T(8,128)(2,1)S(1)}, u32[]{:S(2)}, u32[]{:S(2)}) collective-permute-start(bf16[4,128,128]{2,1,0:T(8,128)(2,1)S(1)} %pad_maximum_fusion.own_in), channel_id=1, source_target_pairs={{4,8},{12,16},{20,24},{28,32},{36,40},{44,48},{52,56},{60,64},{68,... | collective-permute-start | bytes 393224 | tf_op jit(solution)/shard_map/ppermute | solution.py:383
  36.8 0.0 collective-permute-start.4
  36.8 7.0 %collective-permute-done.5.first_in = bf16[4,128,128]{2,1,0:T(8,128)(2,1)S(1)} collective-permute-done((bf16[4,128,128]{2,1,0:T(8,128)(2,1)S(1)}, bf16[4,128,128]{2,1,0:T(8,128)(2,1)S(1)}, u32[]{:S(2)}, u32[]{:S(2)}) %collective-permute-start.5) | collective-permute-done | bytes 131104 | tf_op jit(solution)/shard_map/ppermute | solution.py:383
  43.8 0.0 copy-start.4
  43.8 0.0 collective-permute-done.4.second_in
  43.8 0.0 copy-done.1
  43.8 0.6 copy-done.4
  44.5 0.1 copy-done.5
  44.5 8.0 %layer.1 = (f32[4,2,2,256]{3,2,1,0:T(2,128)}, bf16[64,16,128]{2,1,0:T(8,128)(2,1)}) custom-call(s32[1]{0:T(128)} %bitcast.odd_ref, s32[1]{0:T(128)} %bitcast.1.x0_ref, s32[1]{0:T(128)} %bitcast.2.z0_ref, s32[4,4]{1,0:T(4,128)} %pat_ref.1, s32[4]{0:T(128)} %par_ref.1, bf16[4,128,128]{2,1,0:T(8,128)(2,1)} %copy-done.5, bf16[4,128,128]{2,1,0:T(8,128)(2,1)} %copy-done.1, ...), custom_call_target="tpu_custom_call" | custom-call | tf_op jit(solution)/shard_map/layer/pallas_call | solution.py:363
  52.6 6.1 %all-to-all-start = ((bf16[256,4,128]{2,1,0:T(4,128)(2,1)}), bf16[256,4,128]{2,1,0:T(4,128)(2,1)S(1)}, u32[]{:S(2)}, u32[]{:S(2)}) async-start(bf16[256,4,128]{2,1,0:T(4,128)(2,1)} %bitcast.18), calls=%async_computation | async-start | bytes 524288 | tf_op jit(solution)/shard_map/all_to_all | solution.py:428
  58.7 15.6 %all-to-all-done.in_ref = bf16[256,4,128]{2,1,0:T(4,128)(2,1)S(1)} async-done(((bf16[256,4,128]{2,1,0:T(4,128)(2,1)}), bf16[256,4,128]{2,1,0:T(4,128)(2,1)S(1)}, u32[]{:S(2)}, u32[]{:S(2)}) %all-to-all-start) | async-done | bytes 262176 | tf_op jit(solution)/shard_map/all_to_all | solution.py:428
  74.3 0.7 copy-done
  75.0 2.1 %total.1 = bf16[256,4,128]{2,1,0:T(4,128)(2,1)} custom-call(s32[1]{0:T(128)} %bitcast.10.me_ref, bf16[256,4,128]{2,1,0:T(4,128)(2,1)} %copy-done), custom_call_target="tpu_custom_call" | custom-call | tf_op jit(solution)/shard_map/total/pallas_call | solution.py:363
  77.1 22.4 %all_to_all.10 = bf16[256,4,128]{2,1,0:T(4,128)(2,1)} all-to-all(bf16[256,4,128]{2,1,0:T(4,128)(2,1)} %total.1), channel_id=1, replica_groups=mesh['xy'=64,'gz'=4] {'xy','gz'}, dimensions={0} | all-to-all | bytes 524288 | tf_op jit(solution)/shard_map/all_to_all | solution.py:431
  99.5 2.8 %expand.1 = (f32[48,64,81]{2,1,0:T(8,128)}, f32[1,64]{1,0:T(1,128)}, f32[4,64]{1,0:T(4,128)}) custom-call(bf16[64,16,128]{2,1,0:T(8,128)(2,1)} %bitcast.16, bf16[6,144,512]{2,1,0:T(8,128)(2,1)} %constant.29.clone.spread_ref), custom_call_target="tpu_custom_call" | custom-call | tf_op jit(solution)/shard_map/expand/pallas_call | solution.py:363
  (2 shorter events, 0.0 us)
Async XLA Ops:
  2.8 18.2 %collective-permute-start = (bf16[10,54,128]{2,1,0:T(8,128)(2,1)}, bf16[10,54,128]{2,1,0:T(8,128)(2,1)S(1)}, u32[]{:S(2)}, u32[]{:S(2)}) collective-permute-start(bf16[10,54,128]{2,1,0:T(8,128)(2,1)} %get-tuple-element.19), channel_id=1, source_target_pairs={{0,252},{4,0},{8,4},{12,8},{16,12},{20,16},{24,20},{28,24},{32,28}... | collective-permute-start | bytes 414728 | tf_op jit(solution)/shard_map/ppermute | solution.py:377
  14.1 6.9 %collective-permute-start.1 = (bf16[10,54,128]{2,1,0:T(8,128)(2,1)}, bf16[10,54,128]{2,1,0:T(8,128)(2,1)S(1)}, u32[]{:S(2)}, u32[]{:S(2)}) collective-permute-start(bf16[10,54,128]{2,1,0:T(8,128)(2,1)} %get-tuple-element.20), channel_id=1, source_target_pairs={{0,3},{1,0},{2,1},{3,2},{4,7},{5,4},{6,5},{7,6},{8,11},{9,8},{10,9... | collective-permute-start | bytes 414728 | tf_op jit(solution)/shard_map/ppermute | solution.py:377
  21.0 0.7 copy-start.2
  21.0 0.7 copy-start.3
  26.2 2.2 %collective-permute-start.2 = (bf16[128,128]{1,0:T(8,128)(2,1)}, bf16[128,128]{1,0:T(8,128)(2,1)S(1)}, u32[]{:S(2)}, u32[]{:S(2)}) collective-permute-start(bf16[128,128]{1,0:T(8,128)(2,1)} %get-tuple-element.25), channel_id=1, source_target_pairs={{0,1},{1,2},{2,3},{3,0},{4,5},{5,6},{6,7},{7,4},{8,9},{9,10},{10,1... | collective-permute-start | bytes 98312 | tf_op jit(solution)/shard_map/ppermute | solution.py:377
  27.0 6.4 %collective-permute-start.3 = (bf16[128,128]{1,0:T(8,128)(2,1)}, bf16[128,128]{1,0:T(8,128)(2,1)S(1)}, u32[]{:S(2)}, u32[]{:S(2)}) collective-permute-start(bf16[128,128]{1,0:T(8,128)(2,1)} %get-tuple-element.26), channel_id=1, source_target_pairs={{0,3},{1,0},{2,1},{3,2},{4,7},{5,4},{6,5},{7,6},{8,11},{9,8},{10,9... | collective-permute-start | bytes 98312 | tf_op jit(solution)/shard_map/ppermute | solution.py:377
  34.2 9.6 %copy-start.1 = (bf16[4,128,128]{2,1,0:T(8,128)(2,1)}, bf16[4,128,128]{2,1,0:T(8,128)(2,1)S(1)}, u32[]{:S(2)}) copy-start(bf16[4,128,128]{2,1,0:T(8,128)(2,1)S(1)} %pad_maximum_fusion.own_in) | copy-start | bytes 393220
  34.2 9.6 %collective-permute-start.5 = (bf16[4,128,128]{2,1,0:T(8,128)(2,1)S(1)}, bf16[4,128,128]{2,1,0:T(8,128)(2,1)S(1)}, u32[]{:S(2)}, u32[]{:S(2)}) collective-permute-start(bf16[4,128,128]{2,1,0:T(8,128)(2,1)S(1)} %pad_maximum_fusion.own_in), channel_id=1, source_target_pairs={{4,8},{12,16},{20,24},{28,32},{36,40},{44,48},{52,56},{60,64},{68,... | collective-permute-start | bytes 393224 | tf_op jit(solution)/shard_map/ppermute | solution.py:383
  36.8 7.0 %collective-permute-start.4 = (bf16[4,128,128]{2,1,0:T(8,128)(2,1)S(1)}, bf16[4,128,128]{2,1,0:T(8,128)(2,1)S(1)}, u32[]{:S(2)}, u32[]{:S(2)}) collective-permute-start(bf16[4,128,128]{2,1,0:T(8,128)(2,1)S(1)} %pad_maximum_fusion.own_in), channel_id=1, source_target_pairs={{0,4},{8,12},{16,20},{24,28},{32,36},{40,44},{48,52},{56,60},{64,6... | collective-permute-start | bytes 393224 | tf_op jit(solution)/shard_map/ppermute | solution.py:383
  43.8 0.6 copy-start.4
  43.8 0.7 copy-start.5
  52.6 21.7 %all-to-all-start = ((bf16[256,4,128]{2,1,0:T(4,128)(2,1)}), bf16[256,4,128]{2,1,0:T(4,128)(2,1)S(1)}, u32[]{:S(2)}, u32[]{:S(2)}) async-start(bf16[256,4,128]{2,1,0:T(4,128)(2,1)} %bitcast.18), calls=%async_computation | async-start | bytes 524288 | tf_op jit(solution)/shard_map/all_to_all | solution.py:428
  74.3 0.7 copy-start

commit v8 on v7

--- a/solution.py
+++ b/solution.py
@@ -83,17 +83,6 @@
     return 64 + 32 * (c // 6) + 5 * (c % 6) if x == 1 else (32 + 5 * c if c < 6 else 5 * (c - 6))
 
 
-def group(g):
-    return slice(32 * g, 32 * g + 32)
-
-
-def run(copies):
-    for copy in copies:
-        copy.start()
-    for copy in copies:
-        copy.wait()
-
-
 def fetch(links_ref, l_ref, sems, slices):
     return [
         pltpu.make_async_copy(
@@ -107,9 +96,13 @@
 
 
 def send_body(links_ref, x_ref, z_ref, l_ref, sems):
-    run(fetch(links_ref, l_ref, sems, 5))
+    copies = fetch(links_ref, l_ref, sems, 5)
+    for copy in copies:
+        copy.start()
     rows_ref = l_ref.reshape(90 * 24, 128)
     for tau in range(5):
+        for copy in copies[2 * tau : 2 * tau + 2]:
+            copy.wait()
         for half in range(2):
             at = tau * 2 + half
             x_ref[at] = rows_ref[pl.ds(18 * 24 + tau * 4 + half * 2, 54, stride=24), :].astype(BF16)
@@ -120,7 +113,7 @@
 
 
 def loops_body(
-    links_ref, xh_ref, zh_ref, o0_ref, o1_ref, l_ref, xs_ref, zs_ref, pq_ref, tile_ref, sems
+    odd_ref, links_ref, xh_ref, zh_ref, o0_ref, o1_ref, l_ref, xs_ref, zs_ref, pq_ref, tile_ref, sems
 ):
     copies = fetch(links_ref, l_ref, sems, 6)
     for copy in copies:
@@ -131,8 +124,6 @@
             xs_ref[pl.ds(tau * 4 + half * 2 + 1, 54, stride=24), :] = xh_ref[at].astype(F32)
             zs_ref[pl.ds(tau * 4 + 2 + half, 54, stride=24), :] = zh_ref[at].astype(F32)
     tile_ref[...] = jnp.zeros_like(tile_ref)
-    for copy in copies:
-        copy.wait()
     row = lax.broadcasted_iota(jnp.int32, (8, 128), 0)
     odd_x = row % 2 == 1
     high_z = row % 4 >= 2
@@ -176,6 +167,8 @@
         return re, im
 
     for k in range(3):
+        for copy in (copies[:6], copies[6:10], copies[10:])[k]:
+            copy.wait()
         for p, (mu, nu) in enumerate(plane_pairs):
             u_mu = at_site(mu, k)
             u_nu = at_site(nu, k)
@@ -197,8 +190,9 @@
             for x in range(2):
                 row = place(c, x)
                 tile_ref[lb, row : row + 5, :] = pq_ref[c, pl.ds(2 * lb + x, 5, stride=4), :]
-    o0_ref[...] = tile_ref[0].astype(BF16)
-    o1_ref[...] = tile_ref[1].astype(BF16)
+    odd = odd_ref[0] == 1
+    o0_ref[...] = jnp.where(odd, tile_ref[1], tile_ref[0]).astype(BF16)
+    o1_ref[...] = jnp.where(odd, tile_ref[0], tile_ref[1]).astype(BF16)
 
 
 def layer_body(
@@ -206,9 +200,15 @@
     coef_ref, g_ref, a_ref, low_ref, rows_ref, left_ref, own_ref, right_ref,
 ):
     odd = odd_ref[0] == 1
-    own_ref[...] = own_in[...].astype(F32)
-    left_ref[...] = jnp.where(odd, second_in[:, 32:].astype(F32), first_in[:, 32:].astype(F32))
-    right_ref[...] = jnp.where(odd, first_in[:, :64].astype(F32), second_in[:, :64].astype(F32))
+    turned = lax.rem(lax.div(z0_ref[0], 4), 2) == 1
+    for i in range(4):
+
+        def pick(ref, part):
+            return jnp.where(turned, ref[3 - i, part].astype(F32), ref[i, part].astype(F32))
+
+        own_ref[i] = pick(own_in, slice(0, 128))
+        left_ref[i] = jnp.where(odd, pick(second_in, slice(32, 128)), pick(first_in, slice(32, 128)))
+        right_ref[i] = jnp.where(odd, pick(first_in, slice(0, 64)), pick(second_in, slice(0, 64)))
 
     def piece(i, x, c, t):
         if x == 0 and c >= 6:
@@ -402,15 +402,14 @@
     next_x, next_z, weights, small = lax.optimization_barrier((next_x, next_z, weights, small))
     half = shape((128, 128), BF16)
     odd = (lax.axis_index("xy") % 2).reshape(1)
+    z_odd = (lax.axis_index("gz") % 2).reshape(1)
     border = pltpu.VMEM((57 * 24, 128), F32)
-    low_z, high_z = call(
+    half_one, half_two = call(
         loops_body, (half, half),
         [links, border, border, pltpu.VMEM((14, 24, 128), F32), pltpu.VMEM((2, 128, 128), F32), sems((12,))],
-        gauge_links, next_x, next_z, away=(0,), name="loops",
-    )
-    before_z = shifted(high_z, "gz", 1)
-    after_z = shifted(low_z, "gz", -1)
-    block = jnp.stack([before_z, low_z, high_z, after_z])
+        z_odd, gauge_links, next_x, next_z, smem=1, away=(1,), name="loops",
+    )
+    block = jnp.stack([swapped(half_one, "gz", 1), half_one, half_two, swapped(half_two, "gz", 0)])
     first = swapped(block, "xy", 1)
     second = swapped(block, "xy", 0)
     x_first = (lax.axis_index("xy") * 2).reshape(1)

time: 103 us -> 102 us (level)
  waiting for transfers between devices: 29 us -> 23.7 us
  starting transfers between devices: 21.8 us -> 26.5 us
    ppermute x4 -> x2, waiting for transfers between devices: 6.36 us -> 0.01 us  [shifted(): return lax.ppermute(x, axis, [(i, (i + by) % count) for i in range(count)])]
    ppermute x2 -> x4, starting transfers between devices: 2.6 us -> 5.82 us  [swapped(): return lax.ppermute(x, axis, pairs + [(j, i) for i, j in pairs])]
    all_to_all x1, starting transfers between devices: 6.11 us -> 8.46 us  [per_device(): chunks = lax.all_to_all(chunks, both, 0, 0, tiled=True)]
    ppermute x2 -> x4, waiting for transfers between devices: 7.03 us -> 8.09 us  [swapped(): return lax.ppermute(x, axis, pairs + [(j, i) for i, j in pairs])]
    ppermute x4 -> x2, starting transfers between devices: 13.1 us -> 12.3 us  [shifted(): return lax.ppermute(x, axis, [(i, (i + by) % count) for i in range(count)])]
  transfers between devices with their start and end apart: 7 -> 7, of which waited for: 4 -> 3; matrix products, arithmetic and copies ran while one was open for 0% -> 0% of each run, Pallas kernels for 6% -> 6%
where the time goes in v8:
time: 102 us; the launch traced here: 101 us
  starting transfers between devices  26.5 us (26%)
  Pallas kernels  25.3 us (25%)
  waiting for transfers between devices  23.7 us (23%)
  blocking collectives  22.4 us (22%)
  local copies, waits for them, and re-layouts  2.1 us (2%)
    pallas_call x6, Pallas kernels, call(): pl.pallas_call(body, out_shape=outs, in_specs=specs + [spec(i, away) for...  25.3 us
    all_to_all x1, blocking collectives, per_device(): chunks = lax.all_to_all(chunks, both, 0, 0, tiled=True)  22.4 us
    all_to_all x1, waiting for transfers between devices, per_device(): chunks = lax.all_to_all(chunks, both, 0, 0, tiled=True)  15.6 us
    ppermute x2, starting transfers between devices, shifted(): return lax.ppermute(x, axis, [(i, (i + by) % count) for i in range(count)])  12.3 us
    all_to_all x1, starting transfers between devices, per_device(): chunks = lax.all_to_all(chunks, both, 0, 0, tiled=True)  8.46 us
    ppermute x4, waiting for transfers between devices, swapped(): return lax.ppermute(x, axis, pairs + [(j, i) for i, j in pairs])  8.09 us
    ppermute x4, starting transfers between devices, swapped(): return lax.ppermute(x, axis, pairs + [(j, i) for i, j in pairs])  5.82 us
    unnamed x12, local copies, waits for them, and re-layouts  2.1 us
  transfers between devices with their start and end apart: 7, of which 3 were waited for; matrix products, arithmetic and copies ran while one was open for 0% of the time, Pallas kernels for 6%

profile of v8, /device:TPU:1, one launch (start us, length us, event | category | flops | bytes accessed | tf_op | source)
XLA Modules:
  0.0 101.4 jit_solution(13548948973114089501)
XLA Ops:
  0.6 2.1 %send.1 = (bf16[10,54,128]{2,1,0:T(8,128)(2,1)}, bf16[10,54,128]{2,1,0:T(8,128)(2,1)}) custom-call(f32[4,2,3,3,6,2,256]{6,5,4,3,2,1,0:T(2,128)} %links_ref.3), custom_call_target="tpu_custom_call" | custom-call | tf_op jit(solution)/shard_map/send/pallas_call | solution.py:363
  2.7 11.3 %collective-permute-start = (bf16[10,54,128]{2,1,0:T(8,128)(2,1)}, bf16[10,54,128]{2,1,0:T(8,128)(2,1)S(1)}, u32[]{:S(2)}, u32[]{:S(2)}) collective-permute-start(bf16[10,54,128]{2,1,0:T(8,128)(2,1)} %get-tuple-element.19), channel_id=1, source_target_pairs={{0,252},{4,0},{8,4},{12,8},{16,12},{20,16},{24,20},{28,24},{32,28}... | collective-permute-start | bytes 414728 | tf_op jit(solution)/shard_map/ppermute | solution.py:377
  14.0 1.0 collective-permute-start.1
  15.0 5.9 %weights.1 = (bf16[12,128,256]{2,1,0:T(8,128)(2,1)}, f32[64,8]{1,0:T(8,128)}) custom-call(bf16[48,64,81]{2,1,0:T(8,128)(2,1)} %bitcast.18, bf16[6,144,512]{2,1,0:T(8,128)(2,1)} %constant.33.clone.spread_ref, bf16[1168,256]{1,0:T(8,128)(2,1)} %constant.32.clone.keep_ref, f32[4,64]{1,0:T(4,128)} %bitcast.24, f32[1,64]{1,0:T(1,128)} %bitcast.25), custom_call_target="tpu_custom_call" | custom-call | tf_op jit(solution)/shard_map/weights/pallas_call | solution.py:363
  20.9 0.0 collective-permute-done.xh_ref
  20.9 0.0 copy-start.2
  20.9 0.0 collective-permute-done.1.zh_ref
  20.9 0.0 copy-start.3
  20.9 0.6 copy-done.2
  21.6 0.0 copy-done.3
  21.6 4.3 %loops.1 = (bf16[128,128]{1,0:T(8,128)(2,1)}, bf16[128,128]{1,0:T(8,128)(2,1)}) custom-call(s32[1]{0:T(128)} %bitcast.3.odd_ref, f32[4,2,3,3,6,2,256]{6,5,4,3,2,1,0:T(2,128)} %links_ref.3, bf16[10,54,128]{2,1,0:T(8,128)(2,1)} %copy-done.2, bf16[10,54,128]{2,1,0:T(8,128)(2,1)} %copy-done.3), custom_call_target="tpu_custom_call" | custom-call | tf_op jit(solution)/shard_map/loops/pallas_call | solution.py:363
  25.9 0.9 collective-permute-start.2
  26.8 0.0 collective-permute-start.3
  26.8 2.8 %collective-permute-done.2 = bf16[128,128]{1,0:T(8,128)(2,1)S(1)} collective-permute-done((bf16[128,128]{1,0:T(8,128)(2,1)}, bf16[128,128]{1,0:T(8,128)(2,1)S(1)}, u32[]{:S(2)}, u32[]{:S(2)}) %collective-permute-start.2) | collective-permute-done | bytes 32800 | tf_op jit(solution)/shard_map/ppermute | solution.py:383
  29.5 0.0 collective-permute-done.3
  29.5 0.8 pad_maximum_fusion.own_in
  30.3 0.0 copy-start.1
  30.3 4.9 %collective-permute-start.5 = (bf16[4,128,128]{2,1,0:T(8,128)(2,1)S(1)}, bf16[4,128,128]{2,1,0:T(8,128)(2,1)S(1)}, u32[]{:S(2)}, u32[]{:S(2)}) collective-permute-start(bf16[4,128,128]{2,1,0:T(8,128)(2,1)S(1)} %pad_maximum_fusion.own_in), channel_id=1, source_target_pairs={{4,8},{12,16},{20,24},{28,32},{36,40},{44,48},{52,56},{60,64},{68,... | collective-permute-start | bytes 393224 | tf_op jit(solution)/shard_map/ppermute | solution.py:383
  35.3 0.0 collective-permute-start.4
  35.3 5.3 %collective-permute-done.5.first_in = bf16[4,128,128]{2,1,0:T(8,128)(2,1)S(1)} collective-permute-done((bf16[4,128,128]{2,1,0:T(8,128)(2,1)S(1)}, bf16[4,128,128]{2,1,0:T(8,128)(2,1)S(1)}, u32[]{:S(2)}, u32[]{:S(2)}) %collective-permute-start.5) | collective-permute-done | bytes 131104 | tf_op jit(solution)/shard_map/ppermute | solution.py:383
  40.6 0.0 copy-start.4
  40.6 0.0 collective-permute-done.4.second_in
  40.6 0.0 copy-done.1
  40.6 0.6 copy-done.4
  41.2 0.1 copy-done.5
  41.3 8.0 %layer.1 = (f32[4,2,2,256]{3,2,1,0:T(2,128)}, bf16[64,16,128]{2,1,0:T(8,128)(2,1)}) custom-call(s32[1]{0:T(128)} %bitcast.odd_ref, s32[1]{0:T(128)} %bitcast.1.x0_ref, s32[1]{0:T(128)} %bitcast.2.z0_ref, s32[4,4]{1,0:T(4,128)} %pat_ref.1, s32[4]{0:T(128)} %par_ref.1, bf16[4,128,128]{2,1,0:T(8,128)(2,1)} %copy-done.5, bf16[4,128,128]{2,1,0:T(8,128)(2,1)} %copy-done.1, ...), custom_call_target="tpu_custom_call" | custom-call | tf_op jit(solution)/shard_map/layer/pallas_call | solution.py:363
  49.4 8.5 %all-to-all-start = ((bf16[256,4,128]{2,1,0:T(4,128)(2,1)}), bf16[256,4,128]{2,1,0:T(4,128)(2,1)S(1)}, u32[]{:S(2)}, u32[]{:S(2)}) async-start(bf16[256,4,128]{2,1,0:T(4,128)(2,1)} %bitcast.19), calls=%async_computation | async-start | bytes 524288 | tf_op jit(solution)/shard_map/all_to_all | solution.py:427
  57.8 15.6 %all-to-all-done.in_ref = bf16[256,4,128]{2,1,0:T(4,128)(2,1)S(1)} async-done(((bf16[256,4,128]{2,1,0:T(4,128)(2,1)}), bf16[256,4,128]{2,1,0:T(4,128)(2,1)S(1)}, u32[]{:S(2)}, u32[]{:S(2)}) %all-to-all-start) | async-done | bytes 262176 | tf_op jit(solution)/shard_map/all_to_all | solution.py:427
  73.4 0.7 copy-done
  74.1 2.1 %total.1 = bf16[256,4,128]{2,1,0:T(4,128)(2,1)} custom-call(s32[1]{0:T(128)} %bitcast.11.me_ref, bf16[256,4,128]{2,1,0:T(4,128)(2,1)} %copy-done), custom_call_target="tpu_custom_call" | custom-call | tf_op jit(solution)/shard_map/total/pallas_call | solution.py:363
  76.3 22.4 %all_to_all.10 = bf16[256,4,128]{2,1,0:T(4,128)(2,1)} all-to-all(bf16[256,4,128]{2,1,0:T(4,128)(2,1)} %total.1), channel_id=1, replica_groups=mesh['xy'=64,'gz'=4] {'xy','gz'}, dimensions={0} | all-to-all | bytes 524288 | tf_op jit(solution)/shard_map/all_to_all | solution.py:430
  98.6 2.8 %expand.1 = (f32[48,64,81]{2,1,0:T(8,128)}, f32[1,64]{1,0:T(1,128)}, f32[4,64]{1,0:T(4,128)}) custom-call(bf16[64,16,128]{2,1,0:T(8,128)(2,1)} %bitcast.17, bf16[6,144,512]{2,1,0:T(8,128)(2,1)} %constant.33.clone.spread_ref), custom_call_target="tpu_custom_call" | custom-call | tf_op jit(solution)/shard_map/expand/pallas_call | solution.py:363
  (2 shorter events, 0.0 us)
Async XLA Ops:
  2.7 18.2 %collective-permute-start = (bf16[10,54,128]{2,1,0:T(8,128)(2,1)}, bf16[10,54,128]{2,1,0:T(8,128)(2,1)S(1)}, u32[]{:S(2)}, u32[]{:S(2)}) collective-permute-start(bf16[10,54,128]{2,1,0:T(8,128)(2,1)} %get-tuple-element.19), channel_id=1, source_target_pairs={{0,252},{4,0},{8,4},{12,8},{16,12},{20,16},{24,20},{28,24},{32,28}... | collective-permute-start | bytes 414728 | tf_op jit(solution)/shard_map/ppermute | solution.py:377
  14.0 6.9 %collective-permute-start.1 = (bf16[10,54,128]{2,1,0:T(8,128)(2,1)}, bf16[10,54,128]{2,1,0:T(8,128)(2,1)S(1)}, u32[]{:S(2)}, u32[]{:S(2)}) collective-permute-start(bf16[10,54,128]{2,1,0:T(8,128)(2,1)} %get-tuple-element.20), channel_id=1, source_target_pairs={{0,3},{1,0},{2,1},{3,2},{4,7},{5,4},{6,5},{7,6},{8,11},{9,8},{10,9... | collective-permute-start | bytes 414728 | tf_op jit(solution)/shard_map/ppermute | solution.py:377
  20.9 0.7 copy-start.2
  20.9 0.7 copy-start.3
  25.9 3.6 %collective-permute-start.2 = (bf16[128,128]{1,0:T(8,128)(2,1)}, bf16[128,128]{1,0:T(8,128)(2,1)S(1)}, u32[]{:S(2)}, u32[]{:S(2)}) collective-permute-start(bf16[128,128]{1,0:T(8,128)(2,1)} %get-tuple-element.25), channel_id=1, source_target_pairs={{1,2},{3,0},{2,1},{0,3},{5,6},{7,4},{6,5},{4,7},{9,10},{11,8},{10,... | collective-permute-start | bytes 98312 | tf_op jit(solution)/shard_map/ppermute | solution.py:383
  26.8 2.8 %collective-permute-start.3 = (bf16[128,128]{1,0:T(8,128)(2,1)}, bf16[128,128]{1,0:T(8,128)(2,1)S(1)}, u32[]{:S(2)}, u32[]{:S(2)}) collective-permute-start(bf16[128,128]{1,0:T(8,128)(2,1)} %get-tuple-element.26), channel_id=1, source_target_pairs={{0,1},{2,3},{1,0},{3,2},{4,5},{6,7},{5,4},{7,6},{8,9},{10,11},{9,8... | collective-permute-start | bytes 98312 | tf_op jit(solution)/shard_map/ppermute | solution.py:383
  30.3 10.3 %copy-start.1 = (bf16[4,128,128]{2,1,0:T(8,128)(2,1)}, bf16[4,128,128]{2,1,0:T(8,128)(2,1)S(1)}, u32[]{:S(2)}) copy-start(bf16[4,128,128]{2,1,0:T(8,128)(2,1)S(1)} %pad_maximum_fusion.own_in) | copy-start | bytes 393220
  30.3 10.3 %collective-permute-start.5 = (bf16[4,128,128]{2,1,0:T(8,128)(2,1)S(1)}, bf16[4,128,128]{2,1,0:T(8,128)(2,1)S(1)}, u32[]{:S(2)}, u32[]{:S(2)}) collective-permute-start(bf16[4,128,128]{2,1,0:T(8,128)(2,1)S(1)} %pad_maximum_fusion.own_in), channel_id=1, source_target_pairs={{4,8},{12,16},{20,24},{28,32},{36,40},{44,48},{52,56},{60,64},{68,... | collective-permute-start | bytes 393224 | tf_op jit(solution)/shard_map/ppermute | solution.py:383
  35.3 5.3 %collective-permute-start.4 = (bf16[4,128,128]{2,1,0:T(8,128)(2,1)S(1)}, bf16[4,128,128]{2,1,0:T(8,128)(2,1)S(1)}, u32[]{:S(2)}, u32[]{:S(2)}) collective-permute-start(bf16[4,128,128]{2,1,0:T(8,128)(2,1)S(1)} %pad_maximum_fusion.own_in), channel_id=1, source_target_pairs={{0,4},{8,12},{16,20},{24,28},{32,36},{40,44},{48,52},{56,60},{64,6... | collective-permute-start | bytes 393224 | tf_op jit(solution)/shard_map/ppermute | solution.py:383
  40.6 0.6 copy-start.4
  40.6 0.7 copy-start.5
  49.4 24.1 %all-to-all-start = ((bf16[256,4,128]{2,1,0:T(4,128)(2,1)}), bf16[256,4,128]{2,1,0:T(4,128)(2,1)S(1)}, u32[]{:S(2)}, u32[]{:S(2)}) async-start(bf16[256,4,128]{2,1,0:T(4,128)(2,1)} %bitcast.19), calls=%async_computation | async-start | bytes 524288 | tf_op jit(solution)/shard_map/all_to_all | solution.py:427
  73.4 0.7 copy-start

commit v9 on v8

--- a/solution.py
+++ b/solution.py
@@ -324,7 +324,7 @@
 
 
 def total_body(me_ref, in_ref, out_ref):
-    total = jnp.sum(in_ref[...].astype(F32), axis=0)
+    total = in_ref[...]
     row = me_ref[0] * total.shape[0] + lax.broadcasted_iota(jnp.int32, total.shape, 0)
     lane = lanes(total.shape)
     whole = jnp.where(lane < 8, total + pltpu.roll(total, 120, 1), 0.0)
@@ -426,7 +426,8 @@
     chunks = grads.reshape(count, 1024 // count, 128)
     chunks = lax.all_to_all(chunks, both, 0, 0, tiled=True)
     me = lax.axis_index(both).reshape(1)
-    chunks = call(total_body, (shape(chunks.shape, BF16),), [], me, chunks, smem=1, name="total")[0]
+    total = jnp.sum(chunks.astype(F32), axis=0)
+    chunks = call(total_body, (shape(chunks.shape, BF16),), [], me, total, smem=1, name="total")[0]
     chunks = lax.all_to_all(chunks, both, 0, 0, tiled=True)
     grad_kernel, grad_bias, grad_head = call(
         expand_body, (shape((48, 64, 81), F32), shape((1, 64), F32), shape((4, 64), F32)),

time: 102 us -> 102 us (level)
    unnamed x12 -> x10, local copies, waits for them, and re-layouts: 2.1 us -> 1.39 us
where the time goes in v9:
time: 102 us; the launch traced here: 101 us
  starting transfers between devices  26.5 us (26%)
  Pallas kernels  24.7 us (24%)
  waiting for transfers between devices  23.7 us (23%)
  blocking collectives  22.4 us (22%)
  other arithmetic  1.65 us (2%)
  local copies, waits for them, and re-layouts  1.39 us (1%)
    pallas_call x6, Pallas kernels, call(): pl.pallas_call(body, out_shape=outs, in_specs=specs + [spec(i, away) for...  24.7 us
    all_to_all x1, blocking collectives, per_device(): chunks = lax.all_to_all(chunks, both, 0, 0, tiled=True)  22.4 us
    all_to_all x1, waiting for transfers between devices, per_device(): chunks = lax.all_to_all(chunks, both, 0, 0, tiled=True)  15.6 us
    ppermute x2, starting transfers between devices, shifted(): return lax.ppermute(x, axis, [(i, (i + by) % count) for i in range(count)])  12.3 us
    all_to_all x1, starting transfers between devices, per_device(): chunks = lax.all_to_all(chunks, both, 0, 0, tiled=True)  8.45 us
    ppermute x4, waiting for transfers between devices, swapped(): return lax.ppermute(x, axis, pairs + [(j, i) for i, j in pairs])  8.08 us
    ppermute x4, starting transfers between devices, swapped(): return lax.ppermute(x, axis, pairs + [(j, i) for i, j in pairs])  5.82 us
  transfers between devices with their start and end apart: 7, of which 3 were waited for; matrix products, arithmetic and copies ran while one was open for 0% of the time, Pallas kernels for 6%

profile of v9, /device:TPU:1, one launch (start us, length us, event | category | flops | bytes accessed | tf_op | source)
XLA Modules:
  0.0 101.0 jit_solution(14933934432134060063)
XLA Ops:
  0.6 2.0 %send.1 = (bf16[10,54,128]{2,1,0:T(8,128)(2,1)}, bf16[10,54,128]{2,1,0:T(8,128)(2,1)}) custom-call(f32[4,2,3,3,6,2,256]{6,5,4,3,2,1,0:T(2,128)} %links_ref.3), custom_call_target="tpu_custom_call" | custom-call | tf_op jit(solution)/shard_map/send/pallas_call | solution.py:363
  2.7 11.3 %collective-permute-start = (bf16[10,54,128]{2,1,0:T(8,128)(2,1)}, bf16[10,54,128]{2,1,0:T(8,128)(2,1)S(1)}, u32[]{:S(2)}, u32[]{:S(2)}) collective-permute-start(bf16[10,54,128]{2,1,0:T(8,128)(2,1)} %get-tuple-element.19), channel_id=1, source_target_pairs={{0,252},{4,0},{8,4},{12,8},{16,12},{20,16},{24,20},{28,24},{32,28}... | collective-permute-start | bytes 414728 | tf_op jit(solution)/shard_map/ppermute | solution.py:377
  14.0 1.0 collective-permute-start.1
  14.9 5.9 %weights.1 = (bf16[12,128,256]{2,1,0:T(8,128)(2,1)}, f32[64,8]{1,0:T(8,128)}) custom-call(bf16[48,64,81]{2,1,0:T(8,128)(2,1)} %bitcast.18, bf16[6,144,512]{2,1,0:T(8,128)(2,1)} %constant.35.clone.spread_ref, bf16[1168,256]{1,0:T(8,128)(2,1)} %constant.34.clone.keep_ref, f32[4,64]{1,0:T(4,128)} %bitcast.24, f32[1,64]{1,0:T(1,128)} %bitcast.25), custom_call_target="tpu_custom_call" | custom-call | tf_op jit(solution)/shard_map/weights/pallas_call | solution.py:363
  20.9 0.0 collective-permute-done.xh_ref
  20.9 0.0 copy-start.1
  20.9 0.0 collective-permute-done.1.zh_ref
  20.9 0.0 copy-start.2
  20.9 0.6 copy-done.1
  21.5 0.0 copy-done.2
  21.6 4.3 %loops.1 = (bf16[128,128]{1,0:T(8,128)(2,1)}, bf16[128,128]{1,0:T(8,128)(2,1)}) custom-call(s32[1]{0:T(128)} %bitcast.3.odd_ref, f32[4,2,3,3,6,2,256]{6,5,4,3,2,1,0:T(2,128)} %links_ref.3, bf16[10,54,128]{2,1,0:T(8,128)(2,1)} %copy-done.1, bf16[10,54,128]{2,1,0:T(8,128)(2,1)} %copy-done.2), custom_call_target="tpu_custom_call" | custom-call | tf_op jit(solution)/shard_map/loops/pallas_call | solution.py:363
  25.9 0.9 collective-permute-start.2
  26.7 0.0 collective-permute-start.3
  26.7 2.8 %collective-permute-done.2 = bf16[128,128]{1,0:T(8,128)(2,1)S(1)} collective-permute-done((bf16[128,128]{1,0:T(8,128)(2,1)}, bf16[128,128]{1,0:T(8,128)(2,1)S(1)}, u32[]{:S(2)}, u32[]{:S(2)}) %collective-permute-start.2) | collective-permute-done | bytes 32800 | tf_op jit(solution)/shard_map/ppermute | solution.py:383
  29.5 0.0 collective-permute-done.3
  29.5 0.8 pad_maximum_fusion.own_in
  30.3 0.0 copy-start
  30.3 4.9 %collective-permute-start.5 = (bf16[4,128,128]{2,1,0:T(8,128)(2,1)S(1)}, bf16[4,128,128]{2,1,0:T(8,128)(2,1)S(1)}, u32[]{:S(2)}, u32[]{:S(2)}) collective-permute-start(bf16[4,128,128]{2,1,0:T(8,128)(2,1)S(1)} %pad_maximum_fusion.own_in), channel_id=1, source_target_pairs={{4,8},{12,16},{20,24},{28,32},{36,40},{44,48},{52,56},{60,64},{68,... | collective-permute-start | bytes 393224 | tf_op jit(solution)/shard_map/ppermute | solution.py:383
  35.2 0.0 collective-permute-start.4
  35.2 5.3 %collective-permute-done.5.first_in = bf16[4,128,128]{2,1,0:T(8,128)(2,1)S(1)} collective-permute-done((bf16[4,128,128]{2,1,0:T(8,128)(2,1)S(1)}, bf16[4,128,128]{2,1,0:T(8,128)(2,1)S(1)}, u32[]{:S(2)}, u32[]{:S(2)}) %collective-permute-start.5) | collective-permute-done | bytes 131104 | tf_op jit(solution)/shard_map/ppermute | solution.py:383
  40.6 0.0 copy-start.3
  40.6 0.0 collective-permute-done.4.second_in
  40.6 0.0 copy-done
  40.6 0.6 copy-done.3
  41.2 0.1 copy-done.4
  41.3 8.0 %layer.1 = (f32[4,2,2,256]{3,2,1,0:T(2,128)}, bf16[64,16,128]{2,1,0:T(8,128)(2,1)}) custom-call(s32[1]{0:T(128)} %bitcast.odd_ref, s32[1]{0:T(128)} %bitcast.1.x0_ref, s32[1]{0:T(128)} %bitcast.2.z0_ref, s32[4,4]{1,0:T(4,128)} %pat_ref.1, s32[4]{0:T(128)} %par_ref.1, bf16[4,128,128]{2,1,0:T(8,128)(2,1)} %copy-done.4, bf16[4,128,128]{2,1,0:T(8,128)(2,1)} %copy-done, ...), custom_call_target="tpu_custom_call" | custom-call | tf_op jit(solution)/shard_map/layer/pallas_call | solution.py:363
  49.3 8.4 %all-to-all-start = ((bf16[256,4,128]{2,1,0:T(4,128)(2,1)}), bf16[256,4,128]{2,1,0:T(4,128)(2,1)S(1)}, u32[]{:S(2)}, u32[]{:S(2)}) async-start(bf16[256,4,128]{2,1,0:T(4,128)(2,1)} %bitcast.19), calls=%async_computation | async-start | bytes 524288 | tf_op jit(solution)/shard_map/all_to_all | solution.py:427
  57.8 15.6 %all-to-all-done = bf16[256,4,128]{2,1,0:T(4,128)(2,1)S(1)} async-done(((bf16[256,4,128]{2,1,0:T(4,128)(2,1)}), bf16[256,4,128]{2,1,0:T(4,128)(2,1)S(1)}, u32[]{:S(2)}, u32[]{:S(2)}) %all-to-all-start) | async-done | bytes 262176 | tf_op jit(solution)/shard_map/all_to_all | solution.py:427
  73.4 0.9 convert_reduce_fusion.in_ref
  74.2 1.6 %total.1 = bf16[256,4,128]{2,1,0:T(4,128)(2,1)} custom-call(s32[1]{0:T(128)} %bitcast.11.me_ref, f32[4,128]{1,0:T(4,128)} %convert_reduce_fusion.in_ref), custom_call_target="tpu_custom_call" | custom-call | tf_op jit(solution)/shard_map/total/pallas_call | solution.py:363
  75.8 22.4 %all_to_all.10 = bf16[256,4,128]{2,1,0:T(4,128)(2,1)} all-to-all(bf16[256,4,128]{2,1,0:T(4,128)(2,1)} %total.1), channel_id=1, replica_groups=mesh['xy'=64,'gz'=4] {'xy','gz'}, dimensions={0} | all-to-all | bytes 524288 | tf_op jit(solution)/shard_map/all_to_all | solution.py:431
  98.2 2.8 %expand.1 = (f32[48,64,81]{2,1,0:T(8,128)}, f32[1,64]{1,0:T(1,128)}, f32[4,64]{1,0:T(4,128)}) custom-call(bf16[64,16,128]{2,1,0:T(8,128)(2,1)} %bitcast.17, bf16[6,144,512]{2,1,0:T(8,128)(2,1)} %constant.35.clone.spread_ref), custom_call_target="tpu_custom_call" | custom-call | tf_op jit(solution)/shard_map/expand/pallas_call | solution.py:363
  (1 shorter events, 0.0 us)
Async XLA Ops:
  2.7 18.2 %collective-permute-start = (bf16[10,54,128]{2,1,0:T(8,128)(2,1)}, bf16[10,54,128]{2,1,0:T(8,128)(2,1)S(1)}, u32[]{:S(2)}, u32[]{:S(2)}) collective-permute-start(bf16[10,54,128]{2,1,0:T(8,128)(2,1)} %get-tuple-element.19), channel_id=1, source_target_pairs={{0,252},{4,0},{8,4},{12,8},{16,12},{20,16},{24,20},{28,24},{32,28}... | collective-permute-start | bytes 414728 | tf_op jit(solution)/shard_map/ppermute | solution.py:377
  14.0 6.9 %collective-permute-start.1 = (bf16[10,54,128]{2,1,0:T(8,128)(2,1)}, bf16[10,54,128]{2,1,0:T(8,128)(2,1)S(1)}, u32[]{:S(2)}, u32[]{:S(2)}) collective-permute-start(bf16[10,54,128]{2,1,0:T(8,128)(2,1)} %get-tuple-element.20), channel_id=1, source_target_pairs={{0,3},{1,0},{2,1},{3,2},{4,7},{5,4},{6,5},{7,6},{8,11},{9,8},{10,9... | collective-permute-start | bytes 414728 | tf_op jit(solution)/shard_map/ppermute | solution.py:377
  20.9 0.7 copy-start.1
  20.9 0.7 copy-start.2
  25.9 3.6 %collective-permute-start.2 = (bf16[128,128]{1,0:T(8,128)(2,1)}, bf16[128,128]{1,0:T(8,128)(2,1)S(1)}, u32[]{:S(2)}, u32[]{:S(2)}) collective-permute-start(bf16[128,128]{1,0:T(8,128)(2,1)} %get-tuple-element.25), channel_id=1, source_target_pairs={{1,2},{3,0},{2,1},{0,3},{5,6},{7,4},{6,5},{4,7},{9,10},{11,8},{10,... | collective-permute-start | bytes 98312 | tf_op jit(solution)/shard_map/ppermute | solution.py:383
  26.7 2.8 %collective-permute-start.3 = (bf16[128,128]{1,0:T(8,128)(2,1)}, bf16[128,128]{1,0:T(8,128)(2,1)S(1)}, u32[]{:S(2)}, u32[]{:S(2)}) collective-permute-start(bf16[128,128]{1,0:T(8,128)(2,1)} %get-tuple-element.26), channel_id=1, source_target_pairs={{0,1},{2,3},{1,0},{3,2},{4,5},{6,7},{5,4},{7,6},{8,9},{10,11},{9,8... | collective-permute-start | bytes 98312 | tf_op jit(solution)/shard_map/ppermute | solution.py:383
  30.3 10.3 %copy-start = (bf16[4,128,128]{2,1,0:T(8,128)(2,1)}, bf16[4,128,128]{2,1,0:T(8,128)(2,1)S(1)}, u32[]{:S(2)}) copy-start(bf16[4,128,128]{2,1,0:T(8,128)(2,1)S(1)} %pad_maximum_fusion.own_in) | copy-start | bytes 393220
  30.3 10.3 %collective-permute-start.5 = (bf16[4,128,128]{2,1,0:T(8,128)(2,1)S(1)}, bf16[4,128,128]{2,1,0:T(8,128)(2,1)S(1)}, u32[]{:S(2)}, u32[]{:S(2)}) collective-permute-start(bf16[4,128,128]{2,1,0:T(8,128)(2,1)S(1)} %pad_maximum_fusion.own_in), channel_id=1, source_target_pairs={{4,8},{12,16},{20,24},{28,32},{36,40},{44,48},{52,56},{60,64},{68,... | collective-permute-start | bytes 393224 | tf_op jit(solution)/shard_map/ppermute | solution.py:383
  35.2 5.3 %collective-permute-start.4 = (bf16[4,128,128]{2,1,0:T(8,128)(2,1)S(1)}, bf16[4,128,128]{2,1,0:T(8,128)(2,1)S(1)}, u32[]{:S(2)}, u32[]{:S(2)}) collective-permute-start(bf16[4,128,128]{2,1,0:T(8,128)(2,1)S(1)} %pad_maximum_fusion.own_in), channel_id=1, source_target_pairs={{0,4},{8,12},{16,20},{24,28},{32,36},{40,44},{48,52},{56,60},{64,6... | collective-permute-start | bytes 393224 | tf_op jit(solution)/shard_map/ppermute | solution.py:383
  40.6 0.6 copy-start.3
  40.6 0.7 copy-start.4
  49.3 24.1 %all-to-all-start = ((bf16[256,4,128]{2,1,0:T(4,128)(2,1)}), bf16[256,4,128]{2,1,0:T(4,128)(2,1)S(1)}, u32[]{:S(2)}, u32[]{:S(2)}) async-start(bf16[256,4,128]{2,1,0:T(4,128)(2,1)} %bitcast.19), calls=%async_computation | async-start | bytes 524288 | tf_op jit(solution)/shard_map/all_to_all | solution.py:427

commit v10 on v9

--- a/solution.py
+++ b/solution.py
@@ -191,8 +191,8 @@
                 row = place(c, x)
                 tile_ref[lb, row : row + 5, :] = pq_ref[c, pl.ds(2 * lb + x, 5, stride=4), :]
     odd = odd_ref[0] == 1
-    o0_ref[...] = jnp.where(odd, tile_ref[1], tile_ref[0]).astype(BF16)
-    o1_ref[...] = jnp.where(odd, tile_ref[0], tile_ref[1]).astype(BF16)
+    o0_ref[...] = jnp.where(odd, tile_ref[1, 0:128, :], tile_ref[0, 0:128, :]).astype(BF16)
+    o1_ref[...] = jnp.where(odd, tile_ref[0, 0:128, :], tile_ref[1, 0:128, :]).astype(BF16)
 
 
 def layer_body(
@@ -206,9 +206,9 @@
         def pick(ref, part):
             return jnp.where(turned, ref[3 - i, part].astype(F32), ref[i, part].astype(F32))
 
-        own_ref[i] = pick(own_in, slice(0, 128))
-        left_ref[i] = jnp.where(odd, pick(second_in, slice(32, 128)), pick(first_in, slice(32, 128)))
-        right_ref[i] = jnp.where(odd, pick(first_in, slice(0, 64)), pick(second_in, slice(0, 64)))
+        own_ref[i, 0:128] = pick(own_in, slice(0, 128))
+        left_ref[i, 0:96] = jnp.where(odd, pick(second_in, slice(32, 128)), pick(first_in, slice(32, 128)))
+        right_ref[i, 0:64] = jnp.where(odd, pick(first_in, slice(0, 64)), pick(second_in, slice(0, 64)))
 
     def piece(i, x, c, t):
         if x == 0 and c >= 6:
@@ -406,7 +406,7 @@
     border = pltpu.VMEM((57 * 24, 128), F32)
     half_one, half_two = call(
         loops_body, (half, half),
-        [links, border, border, pltpu.VMEM((14, 24, 128), F32), pltpu.VMEM((2, 128, 128), F32), sems((12,))],
+        [links, border, border, pltpu.VMEM((14, 24, 128), F32), pltpu.VMEM((2, 136, 128), F32), sems((12,))],
         z_odd, gauge_links, next_x, next_z, smem=1, away=(1,), name="loops",
     )
     block = jnp.stack([swapped(half_one, "gz", 1), half_one, half_two, swapped(half_two, "gz", 0)])
@@ -417,7 +417,7 @@
     coefficients, grads = call(
         layer_body, (shape((4, 2, 2, 256), F32), shape((64, 16, 128), BF16)),
         [pltpu.VMEM((12, 256, 1024), BF16), pltpu.VMEM((64, 1024), BF16), pltpu.VMEM((1024, 128), F32)]
-        + [pltpu.VMEM((4, n, 128), F32) for n in (96, 128, 64)],
+        + [pltpu.VMEM((4, n, 128), F32) for n in (104, 136, 72)],
         odd, x_first, z_first, pattern, link_parity, second, block, first, weights, small, keep, cotangent,
         smem=5, name="layer",
     )

time: 102 us -> 102 us (level)
  no operation moved by 1% of the time
where the time goes in v10:
time: 102 us; the launch traced here: 101 us
  starting transfers between devices  26.5 us (26%)
  Pallas kernels  24.7 us (24%)
  waiting for transfers between devices  23.7 us (23%)
  blocking collectives  22.4 us (22%)
  other arithmetic  1.65 us (2%)
  local copies, waits for them, and re-layouts  1.39 us (1%)
    pallas_call x6, Pallas kernels, call(): pl.pallas_call(body, out_shape=outs, in_specs=specs + [spec(i, away) for...  24.7 us
    all_to_all x1, blocking collectives, per_device(): chunks = lax.all_to_all(chunks, both, 0, 0, tiled=True)  22.4 us
    all_to_all x1, waiting for transfers between devices, per_device(): chunks = lax.all_to_all(chunks, both, 0, 0, tiled=True)  15.6 us
    ppermute x2, starting transfers between devices, shifted(): return lax.ppermute(x, axis, [(i, (i + by) % count) for i in range(count)])  12.3 us
    all_to_all x1, starting transfers between devices, per_device(): chunks = lax.all_to_all(chunks, both, 0, 0, tiled=True)  8.46 us
    ppermute x4, waiting for transfers between devices, swapped(): return lax.ppermute(x, axis, pairs + [(j, i) for i, j in pairs])  8.08 us
    ppermute x4, starting transfers between devices, swapped(): return lax.ppermute(x, axis, pairs + [(j, i) for i, j in pairs])  5.82 us
  transfers between devices with their start and end apart: 7, of which 3 were waited for; matrix products, arithmetic and copies ran while one was open for 0% of the time, Pallas kernels for 6%

profile of v10, /device:TPU:1, one launch (start us, length us, event | category | flops | bytes accessed | tf_op | source)
XLA Modules:
  0.0 101.1 jit_solution(10663220110285885475)
XLA Ops:
  0.6 2.0 %send.1 = (bf16[10,54,128]{2,1,0:T(8,128)(2,1)}, bf16[10,54,128]{2,1,0:T(8,128)(2,1)}) custom-call(f32[4,2,3,3,6,2,256]{6,5,4,3,2,1,0:T(2,128)} %links_ref.3), custom_call_target="tpu_custom_call" | custom-call | tf_op jit(solution)/shard_map/send/pallas_call | solution.py:363
  2.7 11.3 %collective-permute-start = (bf16[10,54,128]{2,1,0:T(8,128)(2,1)}, bf16[10,54,128]{2,1,0:T(8,128)(2,1)S(1)}, u32[]{:S(2)}, u32[]{:S(2)}) collective-permute-start(bf16[10,54,128]{2,1,0:T(8,128)(2,1)} %get-tuple-element.19), channel_id=1, source_target_pairs={{0,252},{4,0},{8,4},{12,8},{16,12},{20,16},{24,20},{28,24},{32,28}... | collective-permute-start | bytes 414728 | tf_op jit(solution)/shard_map/ppermute | solution.py:377
  14.0 1.0 collective-permute-start.1
  14.9 5.9 %weights.1 = (bf16[12,128,256]{2,1,0:T(8,128)(2,1)}, f32[64,8]{1,0:T(8,128)}) custom-call(bf16[48,64,81]{2,1,0:T(8,128)(2,1)} %bitcast.18, bf16[6,144,512]{2,1,0:T(8,128)(2,1)} %constant.35.clone.spread_ref, bf16[1168,256]{1,0:T(8,128)(2,1)} %constant.34.clone.keep_ref, f32[4,64]{1,0:T(4,128)} %bitcast.24, f32[1,64]{1,0:T(1,128)} %bitcast.25), custom_call_target="tpu_custom_call" | custom-call | tf_op jit(solution)/shard_map/weights/pallas_call | solution.py:363
  20.9 0.0 collective-permute-done.xh_ref
  20.9 0.0 copy-start.1
  20.9 0.0 collective-permute-done.1.zh_ref
  20.9 0.0 copy-start.2
  20.9 0.6 copy-done.1
  21.5 0.0 copy-done.2
  21.6 4.3 %loops.1 = (bf16[128,128]{1,0:T(8,128)(2,1)}, bf16[128,128]{1,0:T(8,128)(2,1)}) custom-call(s32[1]{0:T(128)} %bitcast.3.odd_ref, f32[4,2,3,3,6,2,256]{6,5,4,3,2,1,0:T(2,128)} %links_ref.3, bf16[10,54,128]{2,1,0:T(8,128)(2,1)} %copy-done.1, bf16[10,54,128]{2,1,0:T(8,128)(2,1)} %copy-done.2), custom_call_target="tpu_custom_call" | custom-call | tf_op jit(solution)/shard_map/loops/pallas_call | solution.py:363
  25.8 0.9 collective-permute-start.2
  26.7 0.0 collective-permute-start.3
  26.7 2.8 %collective-permute-done.2 = bf16[128,128]{1,0:T(8,128)(2,1)S(1)} collective-permute-done((bf16[128,128]{1,0:T(8,128)(2,1)}, bf16[128,128]{1,0:T(8,128)(2,1)S(1)}, u32[]{:S(2)}, u32[]{:S(2)}) %collective-permute-start.2) | collective-permute-done | bytes 32800 | tf_op jit(solution)/shard_map/ppermute | solution.py:383
  29.5 0.0 collective-permute-done.3
  29.5 0.8 pad_maximum_fusion.own_in
  30.3 0.0 copy-start
  30.3 4.9 %collective-permute-start.5 = (bf16[4,128,128]{2,1,0:T(8,128)(2,1)S(1)}, bf16[4,128,128]{2,1,0:T(8,128)(2,1)S(1)}, u32[]{:S(2)}, u32[]{:S(2)}) collective-permute-start(bf16[4,128,128]{2,1,0:T(8,128)(2,1)S(1)} %pad_maximum_fusion.own_in), channel_id=1, source_target_pairs={{4,8},{12,16},{20,24},{28,32},{36,40},{44,48},{52,56},{60,64},{68,... | collective-permute-start | bytes 393224 | tf_op jit(solution)/shard_map/ppermute | solution.py:383
  35.2 0.0 collective-permute-start.4
  35.2 5.3 %collective-permute-done.5.first_in = bf16[4,128,128]{2,1,0:T(8,128)(2,1)S(1)} collective-permute-done((bf16[4,128,128]{2,1,0:T(8,128)(2,1)S(1)}, bf16[4,128,128]{2,1,0:T(8,128)(2,1)S(1)}, u32[]{:S(2)}, u32[]{:S(2)}) %collective-permute-start.5) | collective-permute-done | bytes 131104 | tf_op jit(solution)/shard_map/ppermute | solution.py:383
  40.6 0.0 copy-start.3
  40.6 0.0 collective-permute-done.4.second_in
  40.6 0.0 copy-done
  40.6 0.6 copy-done.3
  41.2 0.1 copy-done.4
  41.3 8.0 %layer.1 = (f32[4,2,2,256]{3,2,1,0:T(2,128)}, bf16[64,16,128]{2,1,0:T(8,128)(2,1)}) custom-call(s32[1]{0:T(128)} %bitcast.odd_ref, s32[1]{0:T(128)} %bitcast.1.x0_ref, s32[1]{0:T(128)} %bitcast.2.z0_ref, s32[4,4]{1,0:T(4,128)} %pat_ref.1, s32[4]{0:T(128)} %par_ref.1, bf16[4,128,128]{2,1,0:T(8,128)(2,1)} %copy-done.4, bf16[4,128,128]{2,1,0:T(8,128)(2,1)} %copy-done, ...), custom_call_target="tpu_custom_call" | custom-call | tf_op jit(solution)/shard_map/layer/pallas_call | solution.py:363
  49.3 8.5 %all-to-all-start = ((bf16[256,4,128]{2,1,0:T(4,128)(2,1)}), bf16[256,4,128]{2,1,0:T(4,128)(2,1)S(1)}, u32[]{:S(2)}, u32[]{:S(2)}) async-start(bf16[256,4,128]{2,1,0:T(4,128)(2,1)} %bitcast.19), calls=%async_computation | async-start | bytes 524288 | tf_op jit(solution)/shard_map/all_to_all | solution.py:427
  57.8 15.6 %all-to-all-done = bf16[256,4,128]{2,1,0:T(4,128)(2,1)S(1)} async-done(((bf16[256,4,128]{2,1,0:T(4,128)(2,1)}), bf16[256,4,128]{2,1,0:T(4,128)(2,1)S(1)}, u32[]{:S(2)}, u32[]{:S(2)}) %all-to-all-start) | async-done | bytes 262176 | tf_op jit(solution)/shard_map/all_to_all | solution.py:427
  73.4 0.9 convert_reduce_fusion.in_ref
  74.2 1.6 %total.1 = bf16[256,4,128]{2,1,0:T(4,128)(2,1)} custom-call(s32[1]{0:T(128)} %bitcast.11.me_ref, f32[4,128]{1,0:T(4,128)} %convert_reduce_fusion.in_ref), custom_call_target="tpu_custom_call" | custom-call | tf_op jit(solution)/shard_map/total/pallas_call | solution.py:363
  75.8 22.4 %all_to_all.10 = bf16[256,4,128]{2,1,0:T(4,128)(2,1)} all-to-all(bf16[256,4,128]{2,1,0:T(4,128)(2,1)} %total.1), channel_id=1, replica_groups=mesh['xy'=64,'gz'=4] {'xy','gz'}, dimensions={0} | all-to-all | bytes 524288 | tf_op jit(solution)/shard_map/all_to_all | solution.py:431
  98.2 2.8 %expand.1 = (f32[48,64,81]{2,1,0:T(8,128)}, f32[1,64]{1,0:T(1,128)}, f32[4,64]{1,0:T(4,128)}) custom-call(bf16[64,16,128]{2,1,0:T(8,128)(2,1)} %bitcast.17, bf16[6,144,512]{2,1,0:T(8,128)(2,1)} %constant.35.clone.spread_ref), custom_call_target="tpu_custom_call" | custom-call | tf_op jit(solution)/shard_map/expand/pallas_call | solution.py:363
  (1 shorter events, 0.0 us)
Async XLA Ops:
  2.7 18.2 %collective-permute-start = (bf16[10,54,128]{2,1,0:T(8,128)(2,1)}, bf16[10,54,128]{2,1,0:T(8,128)(2,1)S(1)}, u32[]{:S(2)}, u32[]{:S(2)}) collective-permute-start(bf16[10,54,128]{2,1,0:T(8,128)(2,1)} %get-tuple-element.19), channel_id=1, source_target_pairs={{0,252},{4,0},{8,4},{12,8},{16,12},{20,16},{24,20},{28,24},{32,28}... | collective-permute-start | bytes 414728 | tf_op jit(solution)/shard_map/ppermute | solution.py:377
  14.0 6.9 %collective-permute-start.1 = (bf16[10,54,128]{2,1,0:T(8,128)(2,1)}, bf16[10,54,128]{2,1,0:T(8,128)(2,1)S(1)}, u32[]{:S(2)}, u32[]{:S(2)}) collective-permute-start(bf16[10,54,128]{2,1,0:T(8,128)(2,1)} %get-tuple-element.20), channel_id=1, source_target_pairs={{0,3},{1,0},{2,1},{3,2},{4,7},{5,4},{6,5},{7,6},{8,11},{9,8},{10,9... | collective-permute-start | bytes 414728 | tf_op jit(solution)/shard_map/ppermute | solution.py:377
  20.9 0.7 copy-start.1
  20.9 0.7 copy-start.2
  25.8 3.6 %collective-permute-start.2 = (bf16[128,128]{1,0:T(8,128)(2,1)}, bf16[128,128]{1,0:T(8,128)(2,1)S(1)}, u32[]{:S(2)}, u32[]{:S(2)}) collective-permute-start(bf16[128,128]{1,0:T(8,128)(2,1)} %get-tuple-element.25), channel_id=1, source_target_pairs={{1,2},{3,0},{2,1},{0,3},{5,6},{7,4},{6,5},{4,7},{9,10},{11,8},{10,... | collective-permute-start | bytes 98312 | tf_op jit(solution)/shard_map/ppermute | solution.py:383
  26.7 2.8 %collective-permute-start.3 = (bf16[128,128]{1,0:T(8,128)(2,1)}, bf16[128,128]{1,0:T(8,128)(2,1)S(1)}, u32[]{:S(2)}, u32[]{:S(2)}) collective-permute-start(bf16[128,128]{1,0:T(8,128)(2,1)} %get-tuple-element.26), channel_id=1, source_target_pairs={{0,1},{2,3},{1,0},{3,2},{4,5},{6,7},{5,4},{7,6},{8,9},{10,11},{9,8... | collective-permute-start | bytes 98312 | tf_op jit(solution)/shard_map/ppermute | solution.py:383
  30.3 10.3 %copy-start = (bf16[4,128,128]{2,1,0:T(8,128)(2,1)}, bf16[4,128,128]{2,1,0:T(8,128)(2,1)S(1)}, u32[]{:S(2)}) copy-start(bf16[4,128,128]{2,1,0:T(8,128)(2,1)S(1)} %pad_maximum_fusion.own_in) | copy-start | bytes 393220
  30.3 10.3 %collective-permute-start.5 = (bf16[4,128,128]{2,1,0:T(8,128)(2,1)S(1)}, bf16[4,128,128]{2,1,0:T(8,128)(2,1)S(1)}, u32[]{:S(2)}, u32[]{:S(2)}) collective-permute-start(bf16[4,128,128]{2,1,0:T(8,128)(2,1)S(1)} %pad_maximum_fusion.own_in), channel_id=1, source_target_pairs={{4,8},{12,16},{20,24},{28,32},{36,40},{44,48},{52,56},{60,64},{68,... | collective-permute-start | bytes 393224 | tf_op jit(solution)/shard_map/ppermute | solution.py:383
  35.2 5.3 %collective-permute-start.4 = (bf16[4,128,128]{2,1,0:T(8,128)(2,1)S(1)}, bf16[4,128,128]{2,1,0:T(8,128)(2,1)S(1)}, u32[]{:S(2)}, u32[]{:S(2)}) collective-permute-start(bf16[4,128,128]{2,1,0:T(8,128)(2,1)S(1)} %pad_maximum_fusion.own_in), channel_id=1, source_target_pairs={{0,4},{8,12},{16,20},{24,28},{32,36},{40,44},{48,52},{56,60},{64,6... | collective-permute-start | bytes 393224 | tf_op jit(solution)/shard_map/ppermute | solution.py:383
  40.6 0.6 copy-start.3
  40.6 0.7 copy-start.4
  49.3 24.1 %all-to-all-start = ((bf16[256,4,128]{2,1,0:T(4,128)(2,1)}), bf16[256,4,128]{2,1,0:T(4,128)(2,1)S(1)}, u32[]{:S(2)}, u32[]{:S(2)}) async-start(bf16[256,4,128]{2,1,0:T(4,128)(2,1)} %bitcast.19), calls=%async_computation | async-start | bytes 524288 | tf_op jit(solution)/shard_map/all_to_all | solution.py:427
